TPU v7x, 32 devices: a whole 2x2x4 slice. The times are simulated.
32 devices in a mesh: dp: 16 (over z, x, core), mp: 2 (over y).
Axes of the slice: x: 2, y: 2, z: 4, core: 2. Of those that a mesh axis runs over, the one named last changes fastest.
Arguments:
- tokens: bfloat16 [16384, 1024], P(('dp', 'mp')), may hold values from -6 to 6
- lengths: int32 [16], P('dp'), may hold values from 512 to 1024, as said below
- first_gain: float32 [1024], replicated, may hold values from 0.5 to 1.5
- first_shift: float32 [1024], replicated, may hold values from -1 to 1
- heads_weight: bfloat16 [3, 1024, 1024], P(None, None, 'mp'), may hold values from -0.1875 to 0.1875
- relative_bias: float32 [16, 32], P('mp'), may hold values from -4 to 4
- mixer_weight: bfloat16 [1024, 1024], P('mp'), may hold values from -0.5 to 0.5
- second_gain: float32 [1024], replicated, may hold values from 0.5 to 1.5
- second_shift: float32 [1024], replicated, may hold values from -1 to 1
- expand_weight: bfloat16 [1024, 4096], P(None, 'mp'), may hold values from -0.1875 to 0.1875
- expand_bias: bfloat16 [4096], P('mp'), may hold values from -3 to 3
- reduce_weight: bfloat16 [4096, 1024], P('mp'), may hold values from -0.09375 to 0.09375
- reduce_bias: float32 [1024], replicated, may hold values from -1.5 to 1.5
- cotangent: bfloat16 [16384, 1024], P(('dp', 'mp')), may hold values from -6 to 6
Outputs:
- block_out: bfloat16 [16384, 1024], P(('dp', 'mp'))
- tokens_grad: bfloat16 [16384, 1024], P(('dp', 'mp'))
- first_gain_grad: float32 [1024], replicated
- first_shift_grad: float32 [1024], replicated
- heads_weight_grad: float32 [3, 1024, 1024], P(None, None, 'mp')
- relative_bias_grad: float32 [16, 32], P('mp')
- mixer_weight_grad: float32 [1024, 1024], P('mp')
- second_gain_grad: float32 [1024], replicated
- second_shift_grad: float32 [1024], replicated
- expand_weight_grad: float32 [1024, 4096], P(None, 'mp')
- expand_bias_grad: float32 [4096], P('mp')
- reduce_weight_grad: float32 [4096, 1024], P('mp')
- reduce_bias_grad: float32 [1024], replicated
Inputs may be any that keep to these rules, and one draw needn't show every extreme that they name: Each sequence holds lengths valid tokens followed by padding slots; some sequence fills all 1024 slots.
All inputs are finite; a program needn't handle non-finite values.
Results may differ from a plain program's by a relative error of at most 0.025.
Values may be sent and summed in bfloat16 or wider, within the bound.
No kernel may reach another device: no remote copies, remote signals or barrier semaphores. Data moves between devices by JAX's collectives and lax.ppermute only.
A program may use at most 320 MiB of HBM per device.

v0:
```python
import functools
import math

import jax
import jax.numpy as jnp
import numpy as np
from jax import lax
from jax.experimental import pallas as pl
from jax.experimental.pallas import tpu as pltpu
from jax.sharding import PartitionSpec as P

EPS = 1e-05
DH=64; MAXDIST=128; NEG=-1e30; BLK=256
F32=jnp.float32; BF16=jnp.bfloat16
HIGHEST=lax.Precision.HIGHEST

def bucket_table(count, buckets, reach):
    exact = buckets // 2
    entries = []
    for position in range(count):
        if position < exact:
            entries.append(position)
        else:
            level = exact + int(math.log(position / exact) / math.log(reach / exact) * (buckets - exact))
            entries.append(min(buckets - 1, level))
    return np.array(entries, dtype=np.int32)

def bucket_starts(buckets):
    table=bucket_table(4*MAXDIST+2*buckets,buckets,MAXDIST)
    return [int(np.argmax(table>=level)) for level in range(1,buckets)]

def bias_rows_kernel(r_ref,o_ref):
    heads,buckets=r_ref.shape
    W=2*BLK
    rel=r_ref[...]-r_ref[:,buckets-1:]
    place=lax.broadcasted_iota(jnp.int32,(heads,W),1)
    signed=jnp.where(place<BLK,place,place-W)
    for part,distance in enumerate((-signed,BLK-signed,signed,BLK+signed)):
        value=jnp.broadcast_to(rel[:,:1],(heads,W))
        for level,start in enumerate(bucket_starts(buckets)):
            value=jnp.where(distance>=start,rel[:,level+1:level+2],value)
        value=jnp.where(distance>=0,value,NEG)
        for pair in range(heads//2):
            o_ref[pair,:,part*W:(part+1)*W]=value[2*pair:2*pair+2]

def bias_rows(relative_bias):
    heads=relative_bias.shape[0]
    return pl.pallas_call(
        bias_rows_kernel,
        out_shape=jax.ShapeDtypeStruct((heads//2,2,8*BLK),F32),
        name="bias_rows",
    )(relative_bias)

def toeplitz(row):
    wide=jnp.broadcast_to(row,(BLK,2*BLK))
    return pltpu.roll(wide,0,1,stride=1,stride_axis=0)[:,:BLK]


def lane_masks():
    lane=lax.broadcasted_iota(jnp.int32,(1,128),1)
    head=[(lane//DH)==h for h in range(2)]
    mine=[jnp.where(m,1.0,0.0).astype(BF16) for m in head]
    spare=[jnp.where(lane==DH*(1-h),1.0,0.0) for h in range(2)]
    return head,mine,spare


def gone_rows(start,half,length,spare):
    pos=lax.broadcasted_iota(jnp.int32,(half,1),0)+start
    gone=jnp.where(pos<length,0.0,NEG)
    return [(gone*s).astype(BF16) for s in spare]


def fwd_kernel(sp, a_ref,c_ref,b_ref,o_ref,lse_ref,qs,ks,vs):
    half=a_ref.shape[1]; T=2*half; flip=sp[0]; length=sp[1]
    W=2*BLK
    head,mine,spare=lane_masks()
    for a,ref in enumerate((a_ref,c_ref)):
        start=pl.multiple_of((a^flip)*half,half)
        dst=pl.ds(start,half)
        gone=gone_rows(start,half,length,spare)
        for h in range(2):
            qs[h,dst,:]=ref[0]*(mine[h]*jnp.asarray(DH**-0.5,BF16))+spare[h].astype(BF16)
            ks[h,dst,:]=ref[1]*mine[h]+gone[h]
            vs[h,dst,:]=ref[2]*mine[h]+mine[1-h]
    tiles=[(toeplitz(b_ref[0,h:h+1,0:W]),toeplitz(b_ref[0,h:h+1,W:2*W])) for h in range(2)]
    outs={}

    def score(i,h):
        return dot(qs[h,i*BLK:(i+1)*BLK,:],ks[h,:(i+1)*BLK,:],1,1)

    def finish(i,h,s):
        kc=(i+1)*BLK; t0,t1=tiles[h]
        parts=[]
        if i>=2: parts.append(s[:,:kc-2*BLK])
        if i>=1: parts.append(s[:,kc-2*BLK:kc-BLK]+t1)
        parts.append(s[:,kc-BLK:]+t0)
        top=functools.reduce(jnp.maximum,[jnp.max(x,axis=1,keepdims=True) for x in parts])
        p=jnp.concatenate([jnp.exp(x-top).astype(BF16) for x in parts],axis=1)
        o=dot(p,vs[h,:kc,:],1,0)
        total=o[:,DH*(1-h):DH*(1-h)+1]
        outs[h]=(o*(1.0/total),top+jnp.log(total))
        if h==1:
            rows=pl.ds(pl.multiple_of((i*BLK+flip*half)%T,BLK),BLK)
            o_ref[rows,:]=jnp.where(head[0],outs[0][0],outs[1][0]).astype(BF16)
            lse_ref[0,i*BLK:kc,:]=jnp.where(head[0],outs[0][1],outs[1][1])

    run_ahead([(i,h) for i in range(T//BLK) for h in range(2)],score,finish,2)


def run_ahead(items,first,second,depth):
    waiting=[]
    for item in items:
        waiting.append((item,first(*item)))
        if len(waiting)>depth:
            done,value=waiting.pop(0)
            second(*done,value)
    for done,value in waiting:
        second(*done,value)


def attend_forward(sp,projected0,projected1,rows):
    _,half,HD=projected0.shape; pairs=HD//128; T=2*half
    part=pl.BlockSpec((3,half,128),lambda p,s:(0,0,p))
    return pl.pallas_call(
        fwd_kernel,
        grid_spec=pltpu.PrefetchScalarGridSpec(
            num_scalar_prefetch=1,grid=(pairs,),
            in_specs=[part,part,pl.BlockSpec((1,2,rows.shape[2]),lambda p,s:(p,0,0))],
            out_specs=[pl.BlockSpec((T,128),lambda p,s:(0,p)),pl.BlockSpec((1,T,128),lambda p,s:(p,0,0))],
            scratch_shapes=[pltpu.VMEM((2,T,128),BF16)]*3),
        out_shape=[jax.ShapeDtypeStruct((T,HD),BF16),jax.ShapeDtypeStruct((pairs,T,128),F32)],
        cost_estimate=cost(8*T*T*HD,8*T*HD+512*pairs*T),
        name="attend_forward",
    )(sp,projected0,projected1,rows)

def diagonal_sums(acc, offset):
    W=2*BLK
    wide=jnp.concatenate([acc,jnp.zeros_like(acc)],axis=1)
    n=BLK
    while n>1:
        n//=2
        top=wide[:n]; bottom=wide[n:2*n]
        wide=top+pltpu.roll(bottom,W-n,1)
    return pltpu.roll(wide,offset,1) if offset else wide

def bwd_kernel(sp, a_ref,c_ref,d0_ref,d1_ref,o_ref,lse_ref,b_ref,g_ref,d_ref,qs,ks,vs,dos,dq,acc0,acc1):
    half=a_ref.shape[1]; T=2*half; flip=sp[0]; length=sp[1]
    W=2*BLK
    n=T//BLK
    head,mine,spare=lane_masks()
    stats=[None,None]
    one=sum(spare).astype(BF16)
    for a,(ref,do_ref) in enumerate(((a_ref,d0_ref),(c_ref,d1_ref))):
        start=pl.multiple_of((a^flip)*half,half)
        dst=pl.ds(start,half)
        gone=gone_rows(start,half,length,spare)
        for h in range(2):
            qs[h,dst,:]=ref[0]*(mine[h]*jnp.asarray(DH**-0.5,BF16))+spare[h].astype(BF16)
            ks[h,dst,:]=ref[1]*mine[h]+gone[h]
            vs[h,dst,:]=ref[2]*mine[h]
        dos[dst,:]=do_ref[...]
        acc0[0,dst,:]=do_ref[...].astype(F32)*o_ref[a*half:(a+1)*half,:].astype(F32)
    turned=acc0[0].T
    deltas=[jnp.sum(turned[h*DH:(h+1)*DH],axis=0,keepdims=True) for h in range(2)]
    turned=lse_ref[0].T
    lses=[turned[h*DH:h*DH+1] for h in range(2)]
    near=acc1
    tiles=[(toeplitz(b_ref[0,h:h+1,2*W:3*W]),toeplitz(b_ref[0,h:h+1,3*W:])) for h in range(2)]

    def products(j,h):
        rj=slice(j*BLK,(j+1)*BLK)
        return dot(ks[h,rj,:],qs[h,j*BLK:,:],1,1),dot(vs[h,rj,:],dos[j*BLK:,:],1,1)

    keep={}

    def finish(j,h,value):
        s,dp=value
        rj=slice(j*BLK,(j+1)*BLK)
        ps=[];dss=[]
        for b in range(n-j):
            c=slice(b*BLK,(b+1)*BLK)
            cc=slice((j+b)*BLK,(j+b+1)*BLK)
            x=s[:,c]-lses[h][:,cc]
            if b<2: x=x+tiles[h][b]
            p=jnp.exp(x)
            ds=p*(dp[:,c]-deltas[h][:,cc])
            if b<2:
                if j==0: near[h,b]=ds
                else: near[h,b]+=ds
            ps.append(p.astype(BF16)); dss.append(ds.astype(BF16))
        p=jnp.concatenate(ps,axis=1); ds=jnp.concatenate(dss,axis=1)
        dv=dot(p,dos[j*BLK:,:],1,0)
        dk=dot(ds,qs[h,j*BLK:,:],1,0)
        kk=ks[h,rj,:]*mine[h]+mine[1-h]
        dqj=dot(ds,kk,0,0)
        if j==0: dq[h,:,:]=dqj
        else: dq[h,j*BLK:,:]+=dqj
        keep[h]=(dk,dv)
        if h==1:
            rows=pl.ds(pl.multiple_of((j*BLK+flip*half)%T,BLK),BLK)
            g_ref[1,rows,:]=jnp.where(head[0],keep[0][0],keep[1][0]).astype(BF16)
            g_ref[2,rows,:]=jnp.where(head[0],keep[0][1],keep[1][1]).astype(BF16)

    run_ahead([(j,h) for j in range(n) for h in range(2)],products,finish,1)
    for h in range(2):
        d_ref[0,h:h+1,:]=diagonal_sums(near[h,0],0)+diagonal_sums(near[h,1],BLK)
        total=jnp.sum(dq[h,:,:],axis=0,keepdims=True)[:,DH*(1-h):DH*(1-h)+1]
        d_ref[0,2+h:3+h,:]=jnp.broadcast_to(total,(1,W))
    for a in range(2):
        dst=pl.ds(pl.multiple_of((a^flip)*half,half),half)
        g_ref[0,a*half:(a+1)*half,:]=(jnp.where(head[0],dq[0,dst,:],dq[1,dst,:])*DH**-0.5).astype(BF16)

def attend_backward(sp,projected0,projected1,grad0,grad1,mixed,lse,rows,start=0,count=None,given=None):
    _,half,HD=projected0.shape; pairs=HD//128; T=2*half
    count=pairs if count is None else count
    part=pl.BlockSpec((3,half,128),lambda p,s:(0,0,p+start))
    grad=pl.BlockSpec((half,128),lambda p,s:(0,p+start))
    in_specs=[part,part,grad,grad,pl.BlockSpec((T,128),lambda p,s:(0,p+start)),
              pl.BlockSpec((1,T,128),lambda p,s:(p+start,0,0)),pl.BlockSpec((1,2,rows.shape[2]),lambda p,s:(p+start,0,0))]
    args=[sp,projected0,projected1,grad0,grad1,mixed,lse,rows]
    kernel=bwd_kernel
    if given is not None:
        in_specs.append(pl.BlockSpec(memory_space=pl.ANY)); args.append(given)
        kernel=lambda *refs: bwd_kernel(*refs[:8],*refs[9:])
    return pl.pallas_call(
        kernel,
        grid_spec=pltpu.PrefetchScalarGridSpec(
            num_scalar_prefetch=1,grid=(count,),
            in_specs=in_specs,
            out_specs=[pl.BlockSpec((3,T,128),lambda p,s:(0,0,p+start)),pl.BlockSpec((1,4,2*BLK),lambda p,s:(p,0,0))],
            scratch_shapes=[pltpu.VMEM((2,T,128),BF16)]*3+[pltpu.VMEM((T,128),BF16),pltpu.VMEM((2,T,128),F32),pltpu.VMEM((1,T,128),F32),pltpu.VMEM((2,2,BLK,BLK),F32)]),
        out_shape=[jax.ShapeDtypeStruct((3,T,HD),BF16),jax.ShapeDtypeStruct((count,4,2*BLK),F32)],
        input_output_aliases={} if given is None else {8:0},
        cost_estimate=cost(20*T*T*128*count,(16*T*128+512*T)*count),
        name="attend_backward",
    )(*args)

def bias_grad(sums, buckets):
    pairs=sums.shape[0]; W=2*BLK
    near=sums[:,0:2].reshape(pairs*2,W); total=sums[:,2:4,0].reshape(pairs*2,1)
    edges=[0]+bucket_starts(buckets)
    distance=jnp.arange(W)[None,None]
    low=jnp.asarray(np.array(edges[:-1],np.int32))[None,:,None]
    high=jnp.asarray(np.array(edges[1:],np.int32))[None,:,None]
    parts=jnp.sum(jnp.where((distance>=low)&(distance<high),near[:,None,:],0.0),axis=2)
    return jnp.concatenate([parts,total-jnp.sum(parts,axis=1,keepdims=True)],axis=1)


HALF_TANH = math.sqrt(2.0 / math.pi)


def dot(a, b, ca, cb):
    return lax.dot_general(a, b, (((ca,), (cb,)), ((), ())), preferred_element_type=F32)


def fixed(shape):
    return pl.BlockSpec(shape, lambda *_: (0,) * len(shape))


def cost(flops, moved):
    return pl.CostEstimate(flops=int(flops), transcendentals=0, bytes_accessed=int(moved))


def cost4(flops, moved):
    return cost(4 * flops, 4 * moved)


def cost16(flops, moved):
    return cost(16 * flops, 16 * moved)


def row_norm(values):
    center = jnp.mean(values, axis=-1, keepdims=True)
    centered = values - center
    inverse = lax.rsqrt(jnp.mean(centered * centered, axis=-1, keepdims=True) + EPS)
    return centered * inverse, inverse


def project_kernel(x_ref, gain_ref, shift_ref, w_ref, low_ref, out_ref):
    @pl.when(pl.program_id(0) == 0)
    def _():
        def some(i, _):
            rows = pl.ds(pl.multiple_of(i * 128, 128), 128)
            normed, _ = row_norm(x_ref[rows, :].astype(F32))
            low_ref[rows, :] = (normed * gain_ref[...] + shift_ref[...]).astype(BF16)
            return 0

        lax.fori_loop(0, x_ref.shape[0] // 128, some, 0)

    out_ref[0] = dot(low_ref[...], w_ref[0], 1, 0).astype(BF16)


def project(x, gain, shift, weight):
    rows, model = x.shape
    width = weight.shape[2]
    return pl.pallas_call(
        project_kernel,
        grid=(3,),
        in_specs=[fixed((rows, model)), fixed((1, model)), fixed((1, model)), pl.BlockSpec((1, model, width), lambda c: (c, 0, 0))],
        out_specs=[fixed((rows, model)), pl.BlockSpec((1, rows, width), lambda c: (c, 0, 0))],
        out_shape=[jax.ShapeDtypeStruct((rows, model), BF16), jax.ShapeDtypeStruct((3, rows, width), BF16)],
        cost_estimate=cost(6 * rows * model * width, 2 * (2 * rows * model + weight.size + 3 * rows * width)),
        name="project",
    )(x, gain, shift, weight)


def mix_kernel(own_blocks, x0_ref, x1_ref, m_ref, p_ref, w0_ref, w1_ref, gain_ref, shift_ref, mid_ref, low_ref):
    i = pl.program_id(0)
    attended = dot(m_ref[...], w0_ref[...], 1, 0) + dot(p_ref[...], w1_ref[...], 1, 0)

    def rows(x_ref):
        return x_ref[...].astype(F32) + attended

    def rest(middle):
        normed, _ = row_norm(middle)
        low_ref[...] = (normed * gain_ref[...] + shift_ref[...]).astype(BF16)

    @pl.when(i < own_blocks)
    def _():
        middle = rows(x0_ref)
        mid_ref[...] = middle
        rest(middle)

    @pl.when(i >= own_blocks)
    def _():
        rest(rows(x1_ref))


def mix(tokens, other, mixed, mixed_other, weight, weight_other, gain, shift):
    own, model = tokens.shape
    width = mixed.shape[1]
    step = 256
    n = own // step
    return pl.pallas_call(
        functools.partial(mix_kernel, n),
        grid=(2 * n,),
        in_specs=[
            pl.BlockSpec((step, model), lambda i: (jnp.minimum(i, n - 1), 0)),
            pl.BlockSpec((step, model), lambda i: (jnp.maximum(i - n, 0), 0)),
            pl.BlockSpec((step, width), lambda i: (i, 0)),
            pl.BlockSpec((step, width), lambda i: ((i + n) % (2 * n), 0)),
            fixed(weight.shape), fixed(weight.shape), fixed((1, model)), fixed((1, model)),
        ],
        out_specs=[
            pl.BlockSpec((step, model), lambda i: (jnp.minimum(i, n - 1), 0)),
            pl.BlockSpec((step, model), lambda i: (i, 0)),
        ],
        out_shape=[jax.ShapeDtypeStruct((own, model), F32), jax.ShapeDtypeStruct((2 * own, model), BF16)],
        cost_estimate=cost(8 * own * model * width, 2 * (4 * own * model + 4 * own * width + 2 * weight.size) + 4 * own * model),
        name="mix",
    )(tokens, other, mixed, mixed_other, weight, weight_other, gain, shift)


def expand_kernel(x_ref, g_ref, w_ref, b_ref, act_ref, ge_ref, gs_ref, bias_ref, acc_ref):
    i = pl.program_id(0)
    x = x_ref[...]
    width = w_ref.shape[1]
    sub = min(512, width)
    total = None
    for s in range(width // sub):
        cols = slice(s * sub, (s + 1) * sub)
        u = dot(x, w_ref[:, cols], 1, 0) + b_ref[:, cols].astype(F32)
        square = u * u
        t = jnp.tanh(HALF_TANH * u * (1.0 + 0.044715 * square))
        half = 0.5 + 0.5 * t
        act_ref[:, cols] = (u * half).astype(BF16)
        slope = half + 0.5 * u * (1.0 - t * t) * (HALF_TANH * (1.0 + 3 * 0.044715 * square))
        grad = g_ref[:, cols].astype(F32) * slope
        low = grad.astype(BF16)
        ge_ref[:, cols] = low
        bias_ref[:, cols] = jnp.sum(grad, axis=0, keepdims=True)
        part = dot(low, w_ref[:, cols], 1, 1)
        total = part if total is None else total + part

    @pl.when(i == 0)
    def _():
        acc_ref[...] = total

    @pl.when(i > 0)
    def _():
        acc_ref[...] += total

    @pl.when(i == pl.num_programs(0) - 1)
    def _():
        gs_ref[...] = acc_ref[...].astype(gs_ref.dtype)


def expand(x, block, rows, grad_active, weight, bias, dtype):
    model = x.shape[1]
    hidden = weight.shape[1]
    step = min(512, hidden)
    return pl.pallas_call(
        expand_kernel,
        grid=(hidden // step,),
        in_specs=[
            pl.BlockSpec((rows, model), lambda i: (block, 0)),
            pl.BlockSpec((rows, step), lambda i: (0, i)),
            pl.BlockSpec((model, step), lambda i: (0, i)),
            pl.BlockSpec((1, step), lambda i: (0, i)),
        ],
        out_specs=[
            pl.BlockSpec((rows, step), lambda i: (0, i)),
            pl.BlockSpec((rows, step), lambda i: (0, i)),
            fixed((rows, model)),
            pl.BlockSpec((1, step), lambda i: (0, i)),
        ],
        out_shape=[
            jax.ShapeDtypeStruct((rows, hidden), BF16),
            jax.ShapeDtypeStruct((rows, hidden), BF16),
            jax.ShapeDtypeStruct((rows, model), dtype),
            jax.ShapeDtypeStruct((1, hidden), F32),
        ],
        scratch_shapes=[pltpu.VMEM((rows, model), F32)],
        cost_estimate=cost(4 * rows * model * hidden, 2 * (2 * rows * model + 3 * rows * hidden + weight.size)),
        name="expand",
    )(x, grad_active, weight, bias)


STAGES = ((1, 2, 4, 8), (1, 4, 2, 8))


def place_of(index, stages):
    bit = [(index // s) % 2 for s in stages]
    return bit[0] * 4 + bit[1] * 2 + bit[2]


def trade(x, bit):
    size = lax.axis_size("dp")
    return lax.ppermute(x, "dp", [(i, i ^ bit) for i in range(size)])


def add_low(a, b):
    return (a.astype(F32) + b.astype(F32)).astype(BF16)


def pair_of(g, s, slot):
    return (3 - g) ^ (s[slot] // 2)


def put_pair(slot, s_ref, chunks, outs):
    flip = s_ref[slot] % 2
    sent = pl.program_id(0) < 2
    for j, value in enumerate(chunks):
        value = value.astype(BF16)[None]
        for out, here in zip(outs, (sent, jnp.logical_not(sent))):
            @pl.when(here)
            def _(out=out):
                out[pl.ds(j ^ flip, 1)] = value


def pair_call(kernel, slot, s, arrays, specs, tail, flops, name):
    zeros = (0,) * len(tail)
    moved = sum(2 * x.size for x in arrays) + 16 * math.prod(tail)
    return pl.pallas_call(
        functools.partial(kernel, slot),
        grid_spec=pltpu.PrefetchScalarGridSpec(
            num_scalar_prefetch=1, grid=(4,), in_specs=specs,
            out_specs=[
                pl.BlockSpec((2, *tail), lambda g, s: (jnp.maximum(1 - g, 0), *zeros)),
                pl.BlockSpec((2, *tail), lambda g, s: (jnp.minimum(3 - g, 1), *zeros)),
            ],
        ),
        out_shape=[jax.ShapeDtypeStruct((4, *tail), BF16)] * 2,
        cost_estimate=cost(flops, moved),
        name=name,
    )(s, *arrays)


def reduce_grad_kernel(slot, s_ref, *refs):
    (a0, a1, t0, t1), outs = refs[:4], refs[4:]
    value = dot(a0[...], t0[...], 0, 0) + dot(a1[...], t1[...], 0, 0)
    width = value.shape[0] // 2
    put_pair(slot, s_ref, [value[:width], value[width:]], outs)


def reduce_grad_part(s, slot, act0, act1, t0, t1):
    rows, hidden = act0.shape
    model = t0.shape[1]
    block = pl.BlockSpec((rows, hidden // 4), lambda g, s: (0, pair_of(g, s, slot)))
    return pair_call(
        reduce_grad_kernel, slot, s, (act0, act1, t0, t1), [block, block, fixed(t0.shape), fixed(t1.shape)],
        (hidden // 8, model), 4 * rows * model * hidden, "reduce_grad",
    )


def expand_grad_kernel(slot, s_ref, *refs):
    (x, g0, g1), outs = refs[:3], refs[3:]
    rows = g0.shape[0]
    value = dot(x[:rows], g0[...], 0, 0) + dot(x[rows:], g1[...], 0, 0)
    width = value.shape[1] // 2
    put_pair(slot, s_ref, [value[:, :width], value[:, width:]], outs)


def expand_grad_part(s, slot, x, g0, g1):
    rows, hidden = g0.shape
    model = x.shape[1]
    block = pl.BlockSpec((rows, hidden // 4), lambda g, s: (0, pair_of(g, s, slot)))
    return pair_call(
        expand_grad_kernel, slot, s, (x, g0, g1), [fixed(x.shape), block, block],
        (model, hidden // 8), 4 * rows * model * hidden, "expand_grad",
    )


def heads_grad_kernel(slot, s_ref, *refs):
    (l0, l1, g), outs = refs[:3], refs[3:]
    rows = l0.shape[0]
    both = [dot(l0[...], g[c, :rows], 0, 0) + dot(l1[...], g[c, rows:], 0, 0) for c in range(2)]
    width = both[0].shape[0] // 2
    chunks = [jnp.stack([v[j * width:(j + 1) * width] for v in both]) for j in range(2)]
    put_pair(slot, s_ref, chunks, outs)


def heads_grad_part(s, slot, low0, low1, grad):
    rows, model = low0.shape
    width = grad.shape[2]
    block = pl.BlockSpec((rows, model // 4), lambda g, s: (0, pair_of(g, s, slot)))
    return pair_call(
        heads_grad_kernel, slot, s, (low0, low1, grad),
        [block, block, pl.BlockSpec((2, 2 * rows, width), lambda g, s: (0, 0, 0))],
        (2, model // 8, width), 8 * rows * model * width, "heads_grad",
    )


def values_grad_kernel(slot, s_ref, *refs):
    (l0, l1, g, a0, a1, m), outs = refs[:6], refs[6:]
    rows = l0.shape[0]
    both = [
        dot(l0[...], g[0, :rows], 0, 0) + dot(l1[...], g[0, rows:], 0, 0),
        dot(a0[...], m[:rows], 0, 0) + dot(a1[...], m[rows:], 0, 0),
    ]
    width = both[0].shape[0] // 2
    chunks = [jnp.stack([v[j * width:(j + 1) * width] for v in both]) for j in range(2)]
    put_pair(slot, s_ref, chunks, outs)


def values_grad_part(s, slot, low0, low1, grad, att0, att1, mixed):
    rows, model = low0.shape
    width = grad.shape[2]
    block = pl.BlockSpec((rows, model // 4), lambda g, s: (0, pair_of(g, s, slot)))
    return pair_call(
        values_grad_kernel, slot, s, (low0, low1, grad, att0, att1, mixed),
        [block, block, pl.BlockSpec((1, 2 * rows, width), lambda g, s: (2, 0, 0)), block, block, fixed(mixed.shape)],
        (2, model // 8, width), 8 * rows * model * width, "values_grad",
    )


def columns_kernel(turn, a_ref, b_ref, out_ref):
    out_ref[...] = dot(a_ref[...], b_ref[...], 1, turn).astype(out_ref.dtype)


def columns_dot(a, b, turn, name):
    rows, depth = a.shape
    columns = b.shape[1 - turn]
    step = min(512, columns)
    block = ((step, depth), lambda i: (i, 0)) if turn else ((depth, step), lambda i: (0, i))
    return pl.pallas_call(
        functools.partial(columns_kernel, turn),
        grid=(columns // step,),
        in_specs=[fixed(a.shape), pl.BlockSpec(*block)],
        out_specs=pl.BlockSpec((rows, step), lambda i: (0, i)),
        out_shape=jax.ShapeDtypeStruct((rows, columns), BF16),
        cost_estimate=cost(2 * rows * depth * columns, 2 * (a.size + b.size + rows * columns)),
        name=name,
    )(a, b)


def output_kernel(m_ref, a_ref, w_ref, r_ref, bias_ref, out_ref):
    out_ref[...] = (
        m_ref[...] + dot(a_ref[...], w_ref[...], 1, 0) + r_ref[...].astype(F32) + bias_ref[...]
    ).astype(BF16)


def output_rows(middle, act, weight, reduced, bias):
    rows, hidden = act.shape
    model = weight.shape[1]
    step = 256
    block = pl.BlockSpec((rows, step), lambda i: (0, i))
    return pl.pallas_call(
        output_kernel,
        grid=(model // step,),
        in_specs=[
            block, fixed(act.shape), pl.BlockSpec((hidden, step), lambda i: (0, i)), block,
            pl.BlockSpec((1, step), lambda i: (0, i)),
        ],
        out_specs=block,
        out_shape=jax.ShapeDtypeStruct((rows, model), BF16),
        cost_estimate=cost16(2 * rows * hidden * model, 2 * (act.size + weight.size) + 8 * rows * model),
        name="output",
    )(middle, act, weight, reduced, bias)


def first_kernel(g_ref, w_ref, out_ref, acc_ref):
    c = pl.program_id(0)
    value = dot(g_ref[0], w_ref[0], 1, 1)

    @pl.when(c == 0)
    def _():
        acc_ref[...] = value

    @pl.when(c > 0)
    def _():
        acc_ref[...] += value

    @pl.when(c == pl.num_programs(0) - 1)
    def _():
        out_ref[...] = acc_ref[...].astype(out_ref.dtype)


def first_rows(grad, weight, part, rows, dtype):
    kinds, model, width = weight.shape
    return pl.pallas_call(
        first_kernel,
        grid=(kinds,),
        in_specs=[
            pl.BlockSpec((1, rows, width), lambda c: (c, part, 0)),
            pl.BlockSpec((1, model, width), lambda c: (c, 0, 0)),
        ],
        out_specs=fixed((rows, model)),
        out_shape=jax.ShapeDtypeStruct((rows, model), dtype),
        scratch_shapes=[pltpu.VMEM((rows, model), F32)],
        cost_estimate=cost(2 * kinds * rows * width * model, 2 * (grad.size + weight.size) + 4 * rows * model),
        name="first_rows",
    )(grad, weight)


def back_kernel(keep, a_ref, b_ref, source_ref, add_ref, gain_ref, *outs):
    @pl.when(pl.program_id(0) == 0)
    def _():
        outs[-1][...] = jnp.zeros_like(outs[-1])

    def some(i, _):
        rows = pl.ds(pl.multiple_of(i * 64, 64), 64)
        normed, inverse = row_norm(source_ref[rows, :].astype(F32))
        grad = a_ref[rows, :] + b_ref[rows, :].astype(F32)
        add = add_ref[rows, :].astype(F32)
        scaled = grad * gain_ref[...]
        weighted = grad * normed
        mean = jnp.mean(scaled, axis=-1, keepdims=True)
        along = jnp.mean(scaled * normed, axis=-1, keepdims=True)
        out = add + inverse * (scaled - mean - normed * along)
        if keep:
            outs[0][rows, :] = out
        outs[-2][rows, :] = out.astype(BF16)
        for k, value in enumerate((weighted, grad, add)):
            outs[-1][k:k + 1] += jnp.sum(value, axis=0, keepdims=True)
        return 0

    lax.fori_loop(0, source_ref.shape[0] // 64, some, 0)


def back_rows(a, b, source, add, gain, keep):
    rows, model = a.shape
    step = 256
    block = pl.BlockSpec((step, model), lambda i: (i, 0))
    kinds = ([F32] if keep else []) + [BF16]
    return pl.pallas_call(
        functools.partial(back_kernel, keep),
        grid=(rows // step,),
        in_specs=[block] * 4 + [fixed((1, model))],
        out_specs=[block] * len(kinds) + [fixed((8, model))],
        out_shape=[jax.ShapeDtypeStruct((rows, model), kind) for kind in kinds] + [jax.ShapeDtypeStruct((8, model), F32)],
        cost_estimate=cost(30 * rows * model, 16 * rows * model),
        name="back_rows",
    )(a, b, source, add, gain)


def order_kernel(s_ref, a_ref, b_ref, out_ref):
    @pl.when(pl.program_id(0) == 0)
    def _():
        out_ref[...] = a_ref[...]

    @pl.when(pl.program_id(0) == 1)
    def _():
        out_ref[...] = b_ref[...]


def order_rows(core, a, b):
    rows, model = a.shape
    return pl.pallas_call(
        order_kernel,
        grid_spec=pltpu.PrefetchScalarGridSpec(
            num_scalar_prefetch=1, grid=(2,),
            in_specs=[pl.BlockSpec((rows, model), lambda g, s: (0, 0))] * 2,
            out_specs=pl.BlockSpec((rows, model), lambda g, s: (g ^ s[0], 0)),
        ),
        out_shape=jax.ShapeDtypeStruct((2 * rows, model), a.dtype),
        cost_estimate=cost(0, 8 * rows * model),
        name="order_rows",
    )(core, a, b)


def spread_kernel(put, s_ref, *refs):
    g = pl.program_id(0)
    pieces, outs = refs[-4 - put.outs:-put.outs], refs[-put.outs:]
    for a in range(4):
        @pl.when(g // 2 == a)
        def _(a=a):
            put(pieces[a], outs)


def spread(places, slot, pieces, put, tail, out_specs, out_shape, given=None, name=None):
    zeros = (0,) * len(tail)
    at = lambda g, s: g ^ s[slot]
    in_specs = [
        pl.BlockSpec((1, *tail), lambda g, s, a=a: (jnp.clip(g - 2 * a, 0, 1), *zeros)) for a in range(4)
    ]
    args = list(pieces)
    aliases = {}
    if given is not None:
        in_specs.insert(0, pl.BlockSpec(memory_space=pl.ANY))
        args.insert(0, given)
        aliases = {1: 0}
    return pl.pallas_call(
        functools.partial(spread_kernel, put),
        grid_spec=pltpu.PrefetchScalarGridSpec(
            num_scalar_prefetch=1, grid=(8,), in_specs=in_specs, out_specs=[spec(at) for spec in out_specs],
        ),
        out_shape=out_shape,
        input_output_aliases=aliases,
        cost_estimate=cost(0, 6 * 8 * math.prod(tail)),
        name=name,
    )(places, *args)


def put_rows(piece, outs):
    outs[0][...] = piece[0].astype(F32)


put_rows.outs = 1


def spread_heads_kernel(value_slot, s_ref, *refs):
    k = pl.program_id(0)
    heads_ref, mixer_ref = refs[8:]
    for slot in range(2):
        r = k ^ s_ref[slot * value_slot]
        for a in range(4):
            piece = refs[4 * slot + a]

            @pl.when(r // 2 == a)
            def _(slot=slot, piece=piece):
                if slot == 0:
                    heads_ref[:2] = piece[0].astype(F32)
                else:
                    heads_ref[2] = piece[0, 0].astype(F32)
                    mixer_ref[...] = piece[0, 1].astype(F32).T


def spread_heads(places, value_slot, queries, values, model, width):
    tail = (2, model // 8, width)

    def spec(slot, a):
        def at(k, s):
            r = k ^ s[slot]
            return (jnp.where(r // 2 == a, r % 2, 0), 0, 0, 0)

        return pl.BlockSpec((1, *tail), at)

    return pl.pallas_call(
        functools.partial(spread_heads_kernel, value_slot),
        grid_spec=pltpu.PrefetchScalarGridSpec(
            num_scalar_prefetch=1, grid=(8,),
            in_specs=[spec(slot * value_slot, a) for slot in range(2) for a in range(4)],
            out_specs=[
                pl.BlockSpec((3, model // 8, width), lambda k, s: (0, k, 0)),
                pl.BlockSpec((width, model // 8), lambda k, s: (0, k)),
            ],
        ),
        out_shape=[jax.ShapeDtypeStruct((3, model, width), F32), jax.ShapeDtypeStruct((width, model), F32)],
        cost_estimate=cost(0, 12 * 8 * math.prod(tail)),
        name="spread_heads",
    )(places, *queries, *values)


def normalize(values):
    return row_norm(values)


def norm_back(grad_norm, normed, inverse):
    return inverse * (
        grad_norm
        - jnp.mean(grad_norm, axis=-1, keepdims=True)
        - normed * jnp.mean(grad_norm * normed, axis=-1, keepdims=True)
    )


def gelu_back(expanded, grad_active):
    pull = jax.vjp(lambda value: jax.nn.gelu(value, approximate=True), expanded)[1]
    return pull(grad_active)[0]


def swap(x):
    return lax.ppermute(x, "mp", [(0, 1), (1, 0)])


def keep_valid(x, places, length):
    return jnp.where((places < length)[:, None], x, jnp.zeros_like(x))


def tie(x, *others):
    return lax.optimization_barrier((x, *others))[0]


class Line:
    def __init__(self):
        self.last = None

    def __call__(self, step, *args):
        if self.last is not None:
            args, _ = lax.optimization_barrier((args, self.last))
        out = step(*args)
        self.last = jax.tree.leaves(out)
        return out


def halve(stay, got):
    n = stay.shape[0] // 2
    return add_low(stay[n:], got[n:]), add_low(stay[:n], got[:n])


def join(a, b):
    return jnp.concatenate([a, b], axis=0)


class Sum:
    def __init__(self, line, stages):
        self.line, self.stages = line, stages

    def begin(self, send, stay):
        self.stay, self.got = stay, trade(send, self.stages[0])

    def first(self, *after):
        out, self.stay = self.line(halve, self.stay, self.got)
        self.got = trade(tie(out, *after) if after else out, self.stages[1])

    def second(self):
        out, self.stay = self.line(halve, self.stay, self.got)
        self.got = trade(out, self.stages[2])

    def third(self):
        self.stay = self.line(add_low, self.stay, self.got)
        self.got = trade(self.stay, self.stages[3])

    def fourth(self):
        self.done = self.line(add_low, self.stay, self.got)
        self.got = trade(self.done, self.stages[2])

    def fifth(self):
        self.near = self.line(join, self.done, self.got)
        self.far = trade(self.near, self.stages[1])
        self.near_other = trade(self.near, self.stages[0])

    def sixth(self):
        self.far_other = trade(tie(self.far, self.line.last), self.stages[0])

    def pieces(self):
        return self.near, self.far, self.near_other, self.far_other


class Held:
    pass


def paired(
    tokens, lengths, first_gain, first_shift, heads_weight, relative_bias, mixer_weight, second_gain,
    second_shift, expand_weight, expand_bias, reduce_weight, reduce_bias, cotangent,
):
    member = lax.axis_index("mp")
    index = lax.axis_index("dp")
    core = index % 2
    length = lengths[0]
    own, model = tokens.shape
    buckets = relative_bias.shape[1]
    width = heads_weight.shape[2]
    hidden = expand_bias.shape[0]
    sp = jnp.stack([member.astype(jnp.int32), length.astype(jnp.int32)])
    at = jnp.stack([place_of(index, s).astype(jnp.int32) for s in STAGES])
    places = member * own + jnp.arange(own)
    places_other = (1 - member) * own + jnp.arange(own)
    row = lambda v: v.reshape(1, -1)
    line = Line()
    v = Held()
    reduce_sum, expand_sum = Sum(line, STAGES[0]), Sum(line, STAGES[0])
    query_sum, value_sum = Sum(line, STAGES[0]), Sum(line, STAGES[0])

    rows = bias_rows(relative_bias)
    target0 = keep_valid(cotangent, places, length)
    other = swap(tokens)

    def project_own():
        v.low0, v.projected0 = line(project, tokens, row(first_gain), row(first_shift), heads_weight)

    def project_other():
        v.low1, v.projected1 = line(project, other, row(first_gain), row(first_shift), heads_weight)

    active_grad = lambda t, w: columns_dot(t, w, 1, name="active_grad")

    def active_own():
        v.active_grad0 = line(active_grad, target0, reduce_weight)

    def send_more():
        n = width // 2
        half = lax.dynamic_slice_in_dim(mixer_weight, core * n, n, 0)
        ready = line.last
        v.cotangent_other = swap(tie(cotangent, other, *ready))
        v.mixer_half = swap(tie(half, other, *ready))

    def attend():
        v.mixed, v.logsum = line(attend_forward, sp, v.projected0, v.projected1, rows)
        v.mixed_other = swap(v.mixed)

    def active_other():
        v.target1 = line(lambda x: keep_valid(x, places_other, length), v.cotangent_other)
        v.active_grad1 = line(active_grad, v.target1, reduce_weight)

    def mixer_rest():
        v.mixer_rest = trade(tie(v.mixer_half, *line.last), 1)

    def mixer_both():
        a, b = v.mixer_half, v.mixer_rest
        v.mixer_other = line(order_rows, core.astype(jnp.int32).reshape(1), a, b)

    def mix_rows():
        v.middle, v.second = line(
            mix, tokens, other, v.mixed, v.mixed_other, mixer_weight, v.mixer_other,
            row(second_gain), row(second_shift),
        )

    def expand_other():
        v.act1, v.ge1, gs1, v.eb1 = line(
            lambda x, g, w, b: expand(x, 1, own, g, w, b, BF16),
            v.second, v.active_grad1, expand_weight, row(expand_bias),
        )
        v.gs_got = swap(gs1)

    def expand_own():
        v.act0, v.ge0, v.gs0, v.eb0 = line(
            lambda x, g, w, b: expand(x, 0, own, g, w, b, F32),
            v.second, v.active_grad0, expand_weight, row(expand_bias),
        )

    def reduce_chunks():
        reduce_sum.begin(*line(
            lambda *xs: reduce_grad_part(at, 0, *xs), v.act0, v.act1, target0, v.target1
        ))

    def expand_chunks():
        expand_sum.begin(*line(lambda *xs: expand_grad_part(at, 0, *xs), v.second, v.ge0, v.ge1))

    def middle_back():
        v.grad_middle, v.attended0, v.second_sums = line(
            lambda *xs: back_rows(*xs, True), v.gs0, v.gs_got, v.middle, target0, row(second_gain)
        )

    grad_mix = lambda a, w: dot(a, w, 1, 1).astype(BF16)

    def mixed_send():
        out = line(grad_mix, v.attended0, v.mixer_other)
        v.grad_mixed1 = swap(out)

    def mixed_own():
        v.grad_mixed0 = line(grad_mix, v.attended0, mixer_weight)

    def attended_send():
        v.attended1 = swap(tie(v.attended0, *line.last))

    def reduced_other():
        out = line(lambda a, w: columns_dot(a, w, 0, name="reduced"), v.act1, reduce_weight)
        v.reduced_got = swap(out)

    def attend_back():
        v.grad_projected, v.sums = line(
            attend_backward, sp, v.projected0, v.projected1, v.grad_mixed0, v.grad_mixed1,
            v.mixed, v.logsum, rows,
        )

    def query_chunks():
        query_sum.begin(*line(lambda *xs: heads_grad_part(at, 0, *xs), v.low0, v.low1, v.grad_projected))

    def value_chunks():
        value_sum.begin(*line(
            lambda *xs: values_grad_part(at, 0, *xs), v.low0, v.low1, v.grad_projected,
            v.attended0, v.attended1, v.mixed,
        ))

    def first_other():
        out = line(lambda g, w: first_rows(g, w, 1, own, BF16), v.grad_projected, heads_weight)
        v.first_got = swap(out)

    def first_own():
        v.first_part = line(lambda g, w: first_rows(g, w, 0, own, F32), v.grad_projected, heads_weight)

    def first_back():
        v.tokens_grad, first_sums = line(
            lambda *xs: back_rows(*xs, False), v.first_part, v.first_got, tokens, v.grad_middle, row(first_gain)
        )
        v.both = join(first_sums[:2], v.second_sums[:3])
        v.both_got = swap(v.both)

    def output():
        v.block_out = line(
            output_rows, v.middle, v.act0, reduce_weight, v.reduced_got, row(reduce_bias)
        )

    def pack_first():
        v.pack = line(
            lambda both, got, eb0, eb1, bias: jnp.concatenate(
                [(both + got).reshape(-1), (eb0 + eb1).reshape(-1), bias.reshape(-1)]
            ).reshape(-1, 128),
            v.both, v.both_got, v.eb0, v.eb1, bias_grad(v.sums, buckets),
        )
        v.pack_got = trade(v.pack, 1)

    def pack_next(bit):
        def step():
            v.pack = line(jnp.add, v.pack, v.pack_got)
            if bit:
                v.pack_got = trade(v.pack, bit)

        return step

    chunk = (hidden // 8, model)
    turned = (model, hidden // 8)

    def reduce_spread():
        (v.reduce_grad,) = line(
            lambda *xs: spread(
                at, 0, xs, put_rows, chunk, [lambda to: pl.BlockSpec(chunk, lambda g, s: (to(g, s), 0))],
                [jax.ShapeDtypeStruct(reduce_weight.shape, F32)], name="spread_reduce",
            ),
            *reduce_sum.pieces(),
        )

    def expand_spread():
        (v.expand_grad,) = line(
            lambda *xs: spread(
                at, 0, xs, put_rows, turned, [lambda to: pl.BlockSpec(turned, lambda g, s: (0, to(g, s)))],
                [jax.ShapeDtypeStruct(expand_weight.shape, F32)], name="spread_expand",
            ),
            *expand_sum.pieces(),
        )

    def heads_spread():
        v.heads_grad, v.mixer_grad = line(
            lambda *xs: spread_heads(at, 0, xs[:4], xs[4:], model, width), *query_sum.pieces(), *value_sum.pieces()
        )

    order = (
        project_own, active_own, send_more, project_other, attend, mixer_rest, mixer_both, active_other,
        mix_rows, expand_other, expand_own, reduce_chunks, middle_back, mixed_send, expand_chunks,
        attended_send, mixed_own, reduce_sum.first, expand_sum.first, attend_back, reduce_sum.second,
        query_chunks, reduce_sum.third, value_chunks, first_other, expand_sum.second, reduce_sum.fourth,
        query_sum.first, value_sum.first, expand_sum.third, reduce_sum.fifth, query_sum.second,
        value_sum.second, first_own, first_back, expand_sum.fourth, pack_first, reduce_sum.sixth, pack_next(2),
        value_sum.third, expand_sum.fifth, query_sum.third, reduced_other, value_sum.fourth, reduce_spread,
        query_sum.fourth, expand_sum.sixth, pack_next(4), value_sum.fifth, query_sum.fifth, output,
        value_sum.sixth, expand_spread, pack_next(8), query_sum.sixth, pack_next(0), heads_spread,
    )
    for step in order:
        step()
    pack = v.pack.reshape(-1)
    both = pack[: 5 * model].reshape(5, model)
    expand_bias_grad = pack[5 * model : 5 * model + hidden]
    bias_part = pack[5 * model + hidden :].reshape(relative_bias.shape)
    return (
        v.block_out, v.tokens_grad, both[0], both[1], v.heads_grad, bias_part, v.mixer_grad, both[2], both[3],
        v.expand_grad, expand_bias_grad, v.reduce_grad, both[4],
    )


def gathered(
    tokens, lengths, first_gain, first_shift, heads_weight, relative_bias, mixer_weight, second_gain,
    second_shift, expand_weight, expand_bias, reduce_weight, reduce_bias, cotangent,
):
    def gather(x):
        return lax.all_gather(x, "mp", axis=0, tiled=True)

    def scatter(x):
        return lax.psum_scatter(x.astype(BF16), "mp", scatter_dimension=0, tiled=True).astype(F32)

    members = lax.axis_size("mp")
    length = lengths[0]
    own = tokens.shape[0]
    whole = own * members
    half = whole // 2
    buckets = relative_bias.shape[1]
    sp = jnp.stack([jnp.zeros((), jnp.int32), length.astype(jnp.int32)])
    places = lax.axis_index("mp") * own + jnp.arange(own)
    rows = bias_rows(relative_bias)
    source_all = gather(tokens)
    first_all, projected = project(source_all, first_gain.reshape(1, -1), first_shift.reshape(1, -1), heads_weight)
    projected0, projected1 = projected[:, :half], projected[:, half:]
    mixed, logsum = attend_forward(sp, projected0, projected1, rows)
    source = tokens.astype(F32)
    middle = source + scatter(dot(mixed, mixer_weight, 1, 0))
    second_norm, second_inverse = normalize(middle)
    second_all = gather((second_norm * second_gain + second_shift).astype(BF16))
    target = keep_valid(cotangent, places, length)
    target_wide = target.astype(F32)
    target_all = gather(target)
    expanded = dot(second_all, expand_weight, 1, 0) + expand_bias
    active_low = jax.nn.gelu(expanded, approximate=True).astype(BF16)
    grad_expanded = gelu_back(expanded, dot(target_all, reduce_weight, 1, 1)).astype(BF16)
    grad_second = scatter(dot(grad_expanded, expand_weight, 1, 1))
    reduced = scatter(dot(active_low, reduce_weight, 1, 0))
    reduce_grad = dot(active_low, target_all, 0, 0)
    expand_grad = dot(second_all, grad_expanded, 0, 0)
    expand_bias_grad = jnp.sum(grad_expanded.astype(F32), axis=0)
    block_out = (middle + reduced + reduce_bias).astype(BF16)
    grad_middle = target_wide + norm_back(grad_second * second_gain, second_norm, second_inverse)
    attended_all = gather(grad_middle.astype(BF16))
    mixer_grad = dot(mixed, attended_all, 0, 0)
    grad_mixed = dot(attended_all, mixer_weight, 1, 1).astype(BF16)
    grad_projected, sums = attend_backward(
        sp, projected0, projected1, grad_mixed[:half], grad_mixed[half:], mixed, logsum, rows
    )
    bias_part = bias_grad(sums, buckets)
    heads_grad = jnp.einsum("td,cte->cde", first_all, grad_projected, preferred_element_type=F32)
    grad_first = scatter(jnp.einsum("cte,cde->td", grad_projected, heads_weight, preferred_element_type=F32))
    first_norm, first_inverse = normalize(source)
    tokens_grad = (
        grad_middle + norm_back(grad_first * first_gain, first_norm, first_inverse)
    ).astype(BF16)
    first_gain_grad, first_shift_grad, second_gain_grad, second_shift_grad, reduce_bias_grad = (
        lax.psum(
            (
                jnp.sum(grad_first * first_norm, axis=0),
                jnp.sum(grad_first, axis=0),
                jnp.sum(grad_second * second_norm, axis=0),
                jnp.sum(grad_second, axis=0),
                jnp.sum(target_wide, axis=0),
            ),
            ("dp", "mp"),
        )
    )
    heads_grad, bias_part, mixer_grad, expand_grad, expand_bias_grad, reduce_grad = (
        lax.psum(x.astype(BF16), "dp").astype(F32)
        for x in (heads_grad, bias_part, mixer_grad, expand_grad, expand_bias_grad, reduce_grad)
    )
    return (
        block_out, tokens_grad, first_gain_grad, first_shift_grad, heads_grad, bias_part, mixer_grad,
        second_gain_grad, second_shift_grad, expand_grad, expand_bias_grad, reduce_grad, reduce_bias_grad,
    )


def per_device(*args):
    if lax.axis_size("mp") == 2 and lax.axis_size("dp") == 16:
        return paired(*args)
    return gathered(*args)


def solution(mesh):
    return jax.shard_map(
        per_device,
        mesh=mesh,
        in_specs=(
            P(("dp", "mp"), None),
            P("dp"),
            P(),
            P(),
            P(None, None, "mp"),
            P("mp", None),
            P("mp", None),
            P(),
            P(),
            P(None, "mp"),
            P("mp"),
            P("mp", None),
            P(),
            P(("dp", "mp"), None),
        ),
        out_specs=(
            P(("dp", "mp"), None),
            P(("dp", "mp"), None),
            P(),
            P(),
            P(None, None, "mp"),
            P("mp", None),
            P("mp", None),
            P(),
            P(),
            P(None, "mp"),
            P("mp"),
            P("mp", None),
            P(),
        ),
        check_vma=False,
    )
```

profile of v0, /device:TPU:25, one launch (start us, length us, event | category | flops | bytes accessed | tf_op | source)
XLA Modules:
  0.0 362.0 jit_solution(8854544502938347586)
XLA Ops:
  0.6 1.3 collective-permute-start
  2.6 6.4 %project.2 = (bf16[512,1024]{1,0:T(8,128)(2,1)}, bf16[3,512,512]{2,1,0:T(8,128)(2,1)}) custom-call(bf16[512,1024]{1,0:T(8,128)(2,1)} %source_ref, f32[1,1024]{1,0:T(1,128)} %bitcast.35, f32[1,1024]{1,0:T(1,128)} %bitcast.38, bf16[3,1024,512]{2,1,0:T(8,128)(2,1)} %w_ref.6), custom_call_target="tpu_custom_call" | custom-call | flops 1610612736 | bytes 6815744 | tf_op jit(solution)/shard_map/project/pallas_call | solution.py:296
  10.1 1.5 bias_rows.1.b_ref
  12.2 6.1 %active_grad.2.g_ref = bf16[512,2048]{1,0:T(8,128)(2,1)} custom-call(bf16[512,1024]{1,0:T(8,128)(2,1)} %broadcast_select_fusion.1.a_ref.refs_2_.add_ref, bf16[2048,1024]{1,0:T(8,128)(2,1)} %w_ref.7), custom_call_target="tpu_custom_call" | custom-call | flops 2147483648 | bytes 7340032 | tf_op jit(solution)/shard_map/active_grad/pallas_call | solution.py:556
  18.3 6.7 %collective-permute-done.x_ref.x1_ref = bf16[512,1024]{1,0:T(8,128)(2,1)} collective-permute-done((bf16[512,1024]{1,0:T(8,128)(2,1)}, bf16[512,1024]{1,0:T(8,128)(2,1)}, u32[]{:S(2)}, u32[]{:S(2)}) %collective-permute-start) | collective-permute-done | bytes 1048608 | tf_op jit(solution)/shard_map/ppermute | solution.py:793
  25.1 1.2 collective-permute-start.2
  26.5 6.3 %project.3 = (bf16[512,1024]{1,0:T(8,128)(2,1)}, bf16[3,512,512]{2,1,0:T(8,128)(2,1)}) custom-call(bf16[512,1024]{1,0:T(8,128)(2,1)} %collective-permute-done.x_ref.x1_ref, f32[1,1024]{1,0:T(1,128)} %bitcast.36, f32[1,1024]{1,0:T(1,128)} %bitcast.39, bf16[3,1024,512]{2,1,0:T(8,128)(2,1)} %w_ref.6), custom_call_target="tpu_custom_call" | custom-call | flops 1610612736 | bytes 6815744 | tf_op jit(solution)/shard_map/project/pallas_call | solution.py:296
  32.8 14.4 %attend_forward.1 = (bf16[1024,512]{1,0:T(8,128)(2,1)}, f32[4,1024,128]{2,1,0:T(8,128)}) custom-call(s32[2]{0:T(128)} %pad_add_fusion.sp, bf16[3,512,512]{2,1,0:T(8,128)(2,1)} %get-tuple-element.283.a_ref, bf16[3,512,512]{2,1,0:T(8,128)(2,1)} %get-tuple-element.284.c_ref, f32[4,2,2048]{2,1,0:T(2,128)} %bias_rows.1.b_ref), custom_call_target="tpu_custom_call" | custom-call | flops 4294967296 | bytes 6291456 | tf_op jit(solution)/shard_map/attend_forward/pallas_call | solution.py:124
  47.2 1.2 collective-permute-start.1
  48.4 2.4 collective-permute-start.3
  53.1 2.2 order_rows.1.w1_ref
  55.3 4.1 %collective-permute-done.4 = bf16[512,1024]{1,0:T(8,128)(2,1)S(1)} collective-permute-done((bf16[512,1024]{1,0:T(8,128)(2,1)S(1)}, bf16[512,1024]{1,0:T(8,128)(2,1)S(1)}, u32[]{:S(2)}, u32[]{:S(2)}) %collective-permute-start.4) | collective-permute-done | bytes 1048608 | tf_op jit(solution)/shard_map/ppermute | solution.py:793
  60.5 6.1 %active_grad.3.g_ref = bf16[512,2048]{1,0:T(8,128)(2,1)} custom-call(bf16[512,1024]{1,0:T(8,128)(2,1)} %broadcast_select_fusion.a_ref.refs_3_, bf16[2048,1024]{1,0:T(8,128)(2,1)} %w_ref.7), custom_call_target="tpu_custom_call" | custom-call | flops 2147483648 | bytes 7340032 | tf_op jit(solution)/shard_map/active_grad/pallas_call | solution.py:556
  66.7 15.3 %collective-permute-done.1.p_ref = bf16[1024,512]{1,0:T(8,128)(2,1)} collective-permute-done((bf16[1024,512]{1,0:T(8,128)(2,1)}, bf16[1024,512]{1,0:T(8,128)(2,1)}, u32[]{:S(2)}, u32[]{:S(2)}) %collective-permute-start.1) | collective-permute-done | bytes 1048608 | tf_op jit(solution)/shard_map/ppermute | solution.py:793
  82.0 8.0 %mix.1 = (f32[512,1024]{1,0:T(8,128)}, bf16[1024,1024]{1,0:T(8,128)(2,1)}) custom-call(bf16[512,1024]{1,0:T(8,128)(2,1)} %source_ref, bf16[512,1024]{1,0:T(8,128)(2,1)} %collective-permute-done.x_ref.x1_ref, bf16[1024,512]{1,0:T(8,128)(2,1)} %get-tuple-element.307.m_ref.o_ref.refs_5_, bf16[1024,512]{1,0:T(8,128)(2,1)} %collective-permute-done.1.p_ref, ...), custom_call_target="tpu_custom_call" | custom-call | flops 2147483648 | bytes 10485760 | tf_op jit(solution)/shard_map/mix/pallas_call | solution.py:334
  90.0 11.8 %expand.2 = (bf16[512,2048]{1,0:T(8,128)(2,1)}, bf16[512,2048]{1,0:T(8,128)(2,1)}, bf16[512,1024]{1,0:T(8,128)(2,1)}, f32[1,2048]{1,0:T(1,128)}) custom-call(bf16[1024,1024]{1,0:T(8,128)(2,1)} %get-tuple-element.271.x_ref.refs_0_, bf16[512,2048]{1,0:T(8,128)(2,1)} %active_grad.3.g_ref, bf16[1024,2048]{1,0:T(8,128)(2,1)} %w_ref.4, bf16[1,2048]{1,0:T(2,128)(2,1)} %reshape.162.b_ref), custom_call_target="tpu_custom_call" | custom-call | flops 4294967296 | bytes 12582912 | tf_op jit(solution)/shard_map/expand/pallas_call | solution.py:392
  101.7 1.3 collective-permute-start.5
  103.7 12.0 %expand.3 = (bf16[512,2048]{1,0:T(8,128)(2,1)}, bf16[512,2048]{1,0:T(8,128)(2,1)}, f32[512,1024]{1,0:T(8,128)}, f32[1,2048]{1,0:T(1,128)}) custom-call(bf16[1024,1024]{1,0:T(8,128)(2,1)} %get-tuple-element.271.x_ref.refs_0_, bf16[512,2048]{1,0:T(8,128)(2,1)} %active_grad.2.g_ref, bf16[1024,2048]{1,0:T(8,128)(2,1)} %w_ref.4, bf16[1,2048]{1,0:T(2,128)(2,1)} %reshape.162.b_ref), custom_call_target="tpu_custom_call" | custom-call | flops 4294967296 | bytes 12582912 | tf_op jit(solution)/shard_map/expand/pallas_call | solution.py:392
  115.7 10.0 %reduce_grad.1 = (bf16[4,256,1024]{2,1,0:T(8,128)(2,1)}, bf16[4,256,1024]{2,1,0:T(8,128)(2,1)}) custom-call(s32[2]{0:T(128)} %pad_add_fusion.1.s_ref, bf16[512,2048]{1,0:T(8,128)(2,1)} %get-tuple-element.370.refs_0_.a_ref, bf16[512,2048]{1,0:T(8,128)(2,1)} %get-tuple-element.352.refs_1_.a_ref, ...), custom_call_target="tpu_custom_call" | custom-call | flops 4294967296 | bytes 10485760 | tf_op jit(solution)/shard_map/reduce_grad/pallas_call | solution.py:454
  125.7 2.7 collective-permute-start.8
  129.5 5.8 %back_rows.2 = (f32[512,1024]{1,0:T(8,128)}, bf16[512,1024]{1,0:T(8,128)(2,1)}, f32[8,1024]{1,0:T(8,128)}) custom-call(f32[512,1024]{1,0:T(8,128)} %get-tuple-element.261.a_ref, bf16[512,1024]{1,0:T(8,128)(2,1)} %copy-done.12, f32[512,1024]{1,0:T(8,128)} %get-tuple-element.369.source_ref.m_ref, ...), custom_call_target="tpu_custom_call" | custom-call | flops 15728640 | bytes 8388608 | tf_op jit(solution)/shard_map/back_rows/pallas_call | solution.py:656
  135.3 2.8 convolution_convert_fusion.1
  138.1 10.0 %expand_grad.1 = (bf16[4,1024,256]{2,1,0:T(8,128)(2,1)}, bf16[4,1024,256]{2,1,0:T(8,128)(2,1)}) custom-call(s32[2]{0:T(128)} %pad_add_fusion.1.s_ref, bf16[1024,1024]{1,0:T(8,128)(2,1)} %get-tuple-element.271.x_ref.refs_0_, bf16[512,2048]{1,0:T(8,128)(2,1)} %get-tuple-element.272.refs_1_, bf16[512,2048]{1,0:T(8,128)(2,1)} %get-tuple-element.273.refs_2_), custom_call_target="tpu_custom_call" | custom-call | flops 4294967296 | bytes 10485760 | tf_op jit(solution)/shard_map/expand_grad/pallas_call | solution.py:454
  149.6 2.8 convolution_convert_fusion.d0_ref
  152.4 3.7 %add_convert_fusion.2 = (bf16[2,256,1024]{2,1,0:T(8,128)(2,1)S(1)}, bf16[2,256,1024]{2,1,0:T(8,128)(2,1)}) fusion(bf16[4,256,1024]{2,1,0:T(8,128)(2,1)} %collective-permute-done.8, bf16[4,256,1024]{2,1,0:T(8,128)(2,1)S(1)} %copy-done.2), kind=kLoop, calls=%fused_computation.2 | loop fusion | flops 4194304 | bytes 6291456 | tf_op jit(solution)/shard_map/convert_element_type | solution.py:433
  157.3 1.5 add_convert_fusion
  158.8 2.7 collective-permute-done.6.d1_ref
  161.5 22.8 %attend_backward.1 = (bf16[3,1024,512]{2,1,0:T(8,128)(2,1)}, f32[4,4,512]{2,1,0:T(4,128)}) custom-call(s32[2]{0:T(128)} %pad_add_fusion.sp, bf16[3,512,512]{2,1,0:T(8,128)(2,1)} %get-tuple-element.283.a_ref, bf16[3,512,512]{2,1,0:T(8,128)(2,1)} %get-tuple-element.284.c_ref, bf16[512,512]{1,0:T(8,128)(2,1)} %convolution_convert_fusion.d0_ref, ...), custom_call_target="tpu_custom_call" | custom-call | flops 10737418240 | bytes 10485760 | tf_op jit(solution)/shard_map/attend_backward/pallas_call | solution.py:225
  185.3 2.4 add_convert_fusion.14
  188.0 1.3 collective-permute-start.13
  189.3 7.3 %heads_grad.1 = (bf16[4,2,128,512]{3,2,1,0:T(8,128)(2,1)}, bf16[4,2,128,512]{3,2,1,0:T(8,128)(2,1)}) custom-call(s32[2]{0:T(128)} %pad_add_fusion.1.s_ref, bf16[512,1024]{1,0:T(8,128)(2,1)} %get-tuple-element.302.refs_0_, bf16[512,1024]{1,0:T(8,128)(2,1)} %get-tuple-element.303.refs_1_, bf16[3,1024,512]{2,1,0:T(8,128)(2,1)} %get-tuple-element.328.refs_2_.g_ref), custom_call_target="tpu_custom_call" | custom-call | flops 2147483648 | bytes 7340032 | tf_op jit(solution)/shard_map/heads_grad/pallas_call | solution.py:454
  196.8 2.7 collective-permute-start.10
  200.6 1.2 add_convert_fusion.13
  202.0 7.5 %values_grad.1 = (bf16[4,2,128,512]{3,2,1,0:T(8,128)(2,1)}, bf16[4,2,128,512]{3,2,1,0:T(8,128)(2,1)}) custom-call(s32[2]{0:T(128)} %pad_add_fusion.1.s_ref, bf16[512,1024]{1,0:T(8,128)(2,1)} %get-tuple-element.302.refs_0_, bf16[512,1024]{1,0:T(8,128)(2,1)} %get-tuple-element.303.refs_1_, bf16[3,1024,512]{2,1,0:T(8,128)(2,1)} %get-tuple-element.328.refs_2_.g_ref, ...), custom_call_target="tpu_custom_call" | custom-call | flops 2147483648 | bytes 10485760 | tf_op jit(solution)/shard_map/values_grad/pallas_call | solution.py:454
  209.5 2.7 collective-permute-start.18
  212.4 5.6 %first_rows.2 = bf16[512,1024]{1,0:T(8,128)(2,1)} custom-call(bf16[3,1024,512]{2,1,0:T(8,128)(2,1)} %get-tuple-element.328.refs_2_.g_ref, bf16[3,1024,512]{2,1,0:T(8,128)(2,1)} %w_ref.6), custom_call_target="tpu_custom_call" | custom-call | flops 1610612736 | bytes 8388608 | tf_op jit(solution)/shard_map/first_rows/pallas_call | solution.py:611
  218.5 1.5 add_convert_fusion.11
  220.0 6.9 %collective-permute-done.12 = bf16[1,256,1024]{2,1,0:T(8,128)(2,1)S(1)} collective-permute-done((bf16[1,256,1024]{2,1,0:T(8,128)(2,1)S(1)}, bf16[1,256,1024]{2,1,0:T(8,128)(2,1)S(1)}, u32[]{:S(2)}, u32[]{:S(2)}) %collective-permute-start.12) | collective-permute-done | bytes 524320 | tf_op jit(solution)/shard_map/ppermute | solution.py:429
  228.6 1.5 add_convert_fusion.6
  230.7 8.6 %collective-permute-done.17 = bf16[1,1024,256]{2,1,0:T(8,128)(2,1)S(1)} collective-permute-done((bf16[1,1024,256]{2,1,0:T(8,128)(2,1)S(1)}, bf16[1,1024,256]{2,1,0:T(8,128)(2,1)S(1)}, u32[]{:S(2)}, u32[]{:S(2)}) %collective-permute-start.17) | collective-permute-done | bytes 524320 | tf_op jit(solution)/shard_map/ppermute | solution.py:429
  239.5 15.1 %collective-permute-done.16 = bf16[1,256,1024]{2,1,0:T(8,128)(2,1)S(1)} collective-permute-done((bf16[1,256,1024]{2,1,0:T(8,128)(2,1)S(1)}, bf16[1,256,1024]{2,1,0:T(8,128)(2,1)S(1)}, u32[]{:S(2)}, u32[]{:S(2)}) %collective-permute-start.16) | collective-permute-done | bytes 524320 | tf_op jit(solution)/shard_map/ppermute | solution.py:429
  254.7 1.3 collective-permute-start.29
  257.7 6.0 %first_rows.3.a_ref = f32[512,1024]{1,0:T(8,128)} custom-call(bf16[3,1024,512]{2,1,0:T(8,128)(2,1)} %get-tuple-element.328.refs_2_.g_ref, bf16[3,1024,512]{2,1,0:T(8,128)(2,1)} %w_ref.6), custom_call_target="tpu_custom_call" | custom-call | flops 1610612736 | bytes 8388608 | tf_op jit(solution)/shard_map/first_rows/pallas_call | solution.py:611
  263.7 5.3 %back_rows.3 = (bf16[512,1024]{1,0:T(8,128)(2,1)}, f32[8,1024]{1,0:T(8,128)}) custom-call(f32[512,1024]{1,0:T(8,128)} %first_rows.3.a_ref, bf16[512,1024]{1,0:T(8,128)(2,1)} %collective-permute-done.22.b_ref, bf16[512,1024]{1,0:T(8,128)(2,1)} %source_ref, f32[512,1024]{1,0:T(8,128)} %get-tuple-element.333.add_ref, f32[1,1024]{1,0:T(1,128)} %bitcast.37), custom_call_target="tpu_custom_call" | custom-call | flops 15728640 | bytes 8388608 | tf_op jit(solution)/shard_map/back_rows/pallas_call | solution.py:656
  269.8 1.5 collective-permute-start.23
  272.5 2.1 collective-permute-done.25
  274.7 2.1 collective-permute-start.26
  279.1 1.3 collective-permute-start.31
  281.2 1.4 collective-permute-done.23
  283.0 9.8 %collective-permute-done.19 = bf16[1,2,128,512]{3,2,1,0:T(8,128)(2,1)S(1)} collective-permute-done((bf16[1,2,128,512]{3,2,1,0:T(8,128)(2,1)S(1)}, bf16[1,2,128,512]{3,2,1,0:T(8,128)(2,1)S(1)}, u32[]{:S(2)}, u32[]{:S(2)}) %collective-permute-start.19) | collective-permute-done | bytes 262176 | tf_op jit(solution)/shard_map/ppermute | solution.py:429
  293.8 5.5 %reduced.1 = bf16[512,1024]{1,0:T(8,128)(2,1)} custom-call(bf16[512,2048]{1,0:T(8,128)(2,1)} %get-tuple-element.352.refs_1_.a_ref, bf16[2048,1024]{1,0:T(8,128)(2,1)} %w_ref.7), custom_call_target="tpu_custom_call" | custom-call | flops 2147483648 | bytes 7340032 | tf_op jit(solution)/shard_map/reduced/pallas_call | solution.py:556
  300.4 1.8 add_convert_fusion.17
  302.2 1.5 collective-permute-start.34
  303.7 8.6 %spread_reduce.1 = f32[2048,1024]{1,0:T(8,128)} custom-call(s32[2]{0:T(128)} %pad_add_fusion.1.s_ref, bf16[2,256,1024]{2,1,0:T(8,128)(2,1)} %copy-done, bf16[2,256,1024]{2,1,0:T(8,128)(2,1)} %collective-permute-done.29.refs_1_, bf16[2,256,1024]{2,1,0:T(8,128)(2,1)} %collective-permute-done.30.refs_2_, bf16[2,256,1024]{2,1,0:T(8,128)(2,1)} %collective-permute-done.31.refs_3_), custom_call_target="tpu_custom_call" | custom-call | bytes 12582912 | tf_op jit(solution)/shard_map/spread_reduce/pallas_call | solution.py:713
  312.3 1.8 collective-permute-done.28
  316.2 1.7 collective-permute-start.36
  319.0 1.3 collective-permute-start.44
  320.3 1.9 collective-permute-done.33
  322.2 2.1 collective-permute-start.39
  324.4 7.4 %output.1 = bf16[512,1024]{1,0:T(8,128)(2,1)} custom-call(f32[512,1024]{1,0:T(8,128)} %get-tuple-element.369.source_ref.m_ref, bf16[512,2048]{1,0:T(8,128)(2,1)} %get-tuple-element.370.refs_0_.a_ref, bf16[2048,1024]{1,0:T(8,128)(2,1)} %w_ref.7, bf16[512,1024]{1,0:T(8,128)(2,1)} %collective-permute-done.27.r_ref, f32[1,1024]{1,0:T(1,128)} %bitcast.41), custom_call_target="tpu_custom_call" | custom-call | flops 34359738368 | bytes 167772160 | tf_op jit(solution)/shard_map/output/pallas_call | solution.py:578
  332.4 1.8 collective-permute-start.45
  334.7 8.6 %spread_expand.1 = f32[1024,2048]{1,0:T(8,128)} custom-call(s32[2]{0:T(128)} %pad_add_fusion.1.s_ref, bf16[2,1024,256]{2,1,0:T(8,128)(2,1)} %copy-done.1, bf16[2,1024,256]{2,1,0:T(8,128)(2,1)} %copy-done.6, bf16[2,1024,256]{2,1,0:T(8,128)(2,1)} %collective-permute-done.38.refs_2_, bf16[2,1024,256]{2,1,0:T(8,128)(2,1)} %collective-permute-done.39.refs_3_), custom_call_target="tpu_custom_call" | custom-call | bytes 12582912 | tf_op jit(solution)/shard_map/spread_expand/pallas_call | solution.py:713
  345.5 3.9 %collective-permute-done.40 = f32[58,128]{1,0:T(8,128)S(1)} collective-permute-done((f32[58,128]{1,0:T(8,128)S(1)}, f32[58,128]{1,0:T(8,128)S(1)}, u32[]{:S(2)}, u32[]{:S(2)}) %collective-permute-start.40) | collective-permute-done | bytes 29728 | tf_op jit(solution)/shard_map/ppermute | solution.py:429
  353.1 8.9 %spread_heads.1 = (f32[3,1024,512]{2,1,0:T(8,128)}, f32[512,1024]{1,0:T(8,128)}) custom-call(s32[2]{0:T(128)} %pad_add_fusion.1.s_ref, bf16[2,2,128,512]{3,2,1,0:T(8,128)(2,1)} %copy-done.5, bf16[2,2,128,512]{3,2,1,0:T(8,128)(2,1)} %collective-permute-done.41.refs_1_, bf16[2,2,128,512]{3,2,1,0:T(8,128)(2,1)} %copy-done.13, ...), custom_call_target="tpu_custom_call" | custom-call | bytes 12582912 | tf_op jit(solution)/shard_map/spread_heads/pallas_call | solution.py:759
  (169 shorter events, 35.2 us)
Async XLA Ops:
  0.6 24.4 %collective-permute-start = (bf16[512,1024]{1,0:T(8,128)(2,1)}, bf16[512,1024]{1,0:T(8,128)(2,1)}, u32[]{:S(2)}, u32[]{:S(2)}) collective-permute-start(bf16[512,1024]{1,0:T(8,128)(2,1)} %source_ref), channel_id=1, source_target_pairs={{0,1},{1,0},{2,3},{3,2},{4,5},{5,4},{6,7},{7,6},{8,9},{9,8},{10,11... | collective-permute-start | bytes 3145736 | tf_op jit(solution)/shard_map/ppermute | solution.py:793
  2.6 6.4 %copy-start.10 = (bf16[512,1024]{1,0:T(8,128)(2,1)S(1)}, bf16[512,1024]{1,0:T(8,128)(2,1)}, u32[]{:S(2)}) copy-start(bf16[512,1024]{1,0:T(8,128)(2,1)} %param.29) | copy-start | bytes 3145732
  25.1 23.4 %collective-permute-start.2 = (bf16[256,1024]{1,0:T(8,128)(2,1)S(1)}, bf16[256,1024]{1,0:T(8,128)(2,1)S(1)}, u32[]{:S(2)}, u32[]{:S(2)}) collective-permute-start(bf16[256,1024]{1,0:T(8,128)(2,1)S(1)} %constant_dynamic-slice_fusion), channel_id=1, source_target_pairs={{0,1},{1,0},{2,3},{3,2},{4,5},{5,4},{6,7},{7,6},{8,9},{9,8},{10,11... | collective-permute-start | bytes 1572872 | tf_op jit(solution)/shard_map/ppermute | solution.py:793
  26.3 33.1 %collective-permute-start.4 = (bf16[512,1024]{1,0:T(8,128)(2,1)S(1)}, bf16[512,1024]{1,0:T(8,128)(2,1)S(1)}, u32[]{:S(2)}, u32[]{:S(2)}) collective-permute-start(bf16[512,1024]{1,0:T(8,128)(2,1)S(1)} %copy-done.10), channel_id=1, source_target_pairs={{0,1},{1,0},{2,3},{3,2},{4,5},{5,4},{6,7},{7,6},{8,9},{9,8},{10,11... | collective-permute-start | bytes 3145736 | tf_op jit(solution)/shard_map/ppermute | solution.py:793
  32.8 18.0 %copy-start.25 = (bf16[2048]{0:T(1024)(128)(2,1)S(1)}, bf16[2048]{0:T(1024)(128)(2,1)}, u32[]{:S(2)}) copy-start(bf16[2048]{0:T(1024)(128)(2,1)} %param.26) | copy-start | bytes 12292
  47.2 34.8 %collective-permute-start.1 = (bf16[1024,512]{1,0:T(8,128)(2,1)}, bf16[1024,512]{1,0:T(8,128)(2,1)}, u32[]{:S(2)}, u32[]{:S(2)}) collective-permute-start(bf16[1024,512]{1,0:T(8,128)(2,1)} %get-tuple-element.307.m_ref.o_ref.refs_5_), channel_id=1, source_target_pairs={{0,1},{1,0},{2,3},{3,2},{4,5},{5,4},{6,7},{7,6},{8,9},{9,8},{10,11... | collective-permute-start | bytes 3145736 | tf_op jit(solution)/shard_map/ppermute | solution.py:793
  48.4 3.9 %copy-start.17 = (bf16[256,1024]{1,0:T(8,128)(2,1)}, bf16[256,1024]{1,0:T(8,128)(2,1)S(1)}, u32[]{:S(2)}) copy-start(bf16[256,1024]{1,0:T(8,128)(2,1)S(1)} %collective-permute-done.2.a_ref) | copy-start | bytes 1572868
  48.4 3.9 %collective-permute-start.3 = (bf16[256,1024]{1,0:T(8,128)(2,1)S(1)}, bf16[256,1024]{1,0:T(8,128)(2,1)S(1)}, u32[]{:S(2)}, u32[]{:S(2)}) collective-permute-start(bf16[256,1024]{1,0:T(8,128)(2,1)S(1)} %collective-permute-done.2.a_ref), channel_id=1, source_target_pairs={{0,2},{2,0},{4,6},{6,4},{8,10},{10,8},{12,14},{14,12},{16,18},{18,... | collective-permute-start | bytes 1572872 | tf_op jit(solution)/shard_map/ppermute | solution.py:429
  101.7 26.7 %collective-permute-start.5 = (bf16[512,1024]{1,0:T(8,128)(2,1)}, bf16[512,1024]{1,0:T(8,128)(2,1)S(1)}, u32[]{:S(2)}, u32[]{:S(2)}) collective-permute-start(bf16[512,1024]{1,0:T(8,128)(2,1)} %get-tuple-element.245), channel_id=1, source_target_pairs={{0,1},{1,0},{2,3},{3,2},{4,5},{5,4},{6,7},{7,6},{8,9},{9,8},{10,11... | collective-permute-start | bytes 3145736 | tf_op jit(solution)/shard_map/ppermute | solution.py:793
  125.7 26.7 %collective-permute-start.8 = (bf16[4,256,1024]{2,1,0:T(8,128)(2,1)}, bf16[4,256,1024]{2,1,0:T(8,128)(2,1)}, u32[]{:S(2)}, u32[]{:S(2)}) collective-permute-start(bf16[4,256,1024]{2,1,0:T(8,128)(2,1)} %get-tuple-element.259), channel_id=1, source_target_pairs={{0,2},{2,0},{4,6},{6,4},{8,10},{10,8},{12,14},{14,12},{16,18},{18,... | collective-permute-start | bytes 6291464 | tf_op jit(solution)/shard_map/ppermute | solution.py:429
  129.5 5.8 %copy-start.11 = (bf16[512,1024]{1,0:T(8,128)(2,1)S(1)}, bf16[512,1024]{1,0:T(8,128)(2,1)}, u32[]{:S(2)}) copy-start(bf16[512,1024]{1,0:T(8,128)(2,1)} %order_rows.1.w1_ref) | copy-start | bytes 3145732
  138.1 11.5 %copy-start.20 = (bf16[512,1024]{1,0:T(8,128)(2,1)S(1)}, bf16[512,1024]{1,0:T(8,128)(2,1)}, u32[]{:S(2)}) copy-start(bf16[512,1024]{1,0:T(8,128)(2,1)} %w0_ref) | copy-start | bytes 3145732
  148.1 4.3 %copy-start.2 = (bf16[4,256,1024]{2,1,0:T(8,128)(2,1)S(1)}, bf16[4,256,1024]{2,1,0:T(8,128)(2,1)}, u32[]{:S(2)}) copy-start(bf16[4,256,1024]{2,1,0:T(8,128)(2,1)} %get-tuple-element.278) | copy-start | bytes 6291460
  148.1 9.2 %collective-permute-start.7 = (bf16[4,1024,256]{2,1,0:T(8,128)(2,1)}, bf16[4,1024,256]{2,1,0:T(8,128)(2,1)S(1)}, u32[]{:S(2)}, u32[]{:S(2)}) collective-permute-start(bf16[4,1024,256]{2,1,0:T(8,128)(2,1)} %get-tuple-element.274), channel_id=1, source_target_pairs={{0,2},{2,0},{4,6},{6,4},{8,10},{10,8},{12,14},{14,12},{16,18},{18,... | collective-permute-start | bytes 6291464 | tf_op jit(solution)/shard_map/ppermute | solution.py:429
  148.1 13.4 %collective-permute-start.6 = (bf16[512,512]{1,0:T(8,128)(2,1)}, bf16[512,512]{1,0:T(8,128)(2,1)}, u32[]{:S(2)}, u32[]{:S(2)}) collective-permute-start(bf16[512,512]{1,0:T(8,128)(2,1)} %convolution_convert_fusion.1), channel_id=1, source_target_pairs={{0,1},{1,0},{2,3},{3,2},{4,5},{5,4},{6,7},{7,6},{8,9},{9,8},{10,11... | collective-permute-start | bytes 1572872 | tf_op jit(solution)/shard_map/ppermute | solution.py:793
  148.5 53.5 %collective-permute-start.14 = (bf16[512,1024]{1,0:T(8,128)(2,1)}, bf16[512,1024]{1,0:T(8,128)(2,1)}, u32[]{:S(2)}, u32[]{:S(2)}) collective-permute-start(bf16[512,1024]{1,0:T(8,128)(2,1)} %get-tuple-element.305.refs_3_), channel_id=1, source_target_pairs={{0,1},{1,0},{2,3},{3,2},{4,5},{5,4},{6,7},{7,6},{8,9},{9,8},{10,11... | collective-permute-start | bytes 3145736 | tf_op jit(solution)/shard_map/ppermute | solution.py:793
  152.4 4.9 %copy-start.3 = (bf16[4,1024,256]{2,1,0:T(8,128)(2,1)S(1)}, bf16[4,1024,256]{2,1,0:T(8,128)(2,1)}, u32[]{:S(2)}) copy-start(bf16[4,1024,256]{2,1,0:T(8,128)(2,1)} %get-tuple-element.280) | copy-start | bytes 6291460
  156.1 28.3 %collective-permute-start.9 = (bf16[2,256,1024]{2,1,0:T(8,128)(2,1)}, bf16[2,256,1024]{2,1,0:T(8,128)(2,1)S(1)}, u32[]{:S(2)}, u32[]{:S(2)}) collective-permute-start(bf16[2,256,1024]{2,1,0:T(8,128)(2,1)} %get-tuple-element.400), channel_id=1, source_target_pairs={{0,4},{2,6},{4,0},{6,2},{8,12},{10,14},{12,8},{14,10},{16,20},{18,... | collective-permute-start | bytes 3145736 | tf_op jit(solution)/shard_map/ppermute | solution.py:429
  184.3 3.7 %copy-start.24 = (f32[8,1024]{1,0:T(8,128)S(1)}, f32[8,1024]{1,0:T(8,128)}, u32[]{:S(2)}) copy-start(f32[8,1024]{1,0:T(8,128)} %get-tuple-element.268) | copy-start | bytes 98308
  184.3 3.7 %copy-start.21 = (f32[4,4,512]{2,1,0:T(4,128)S(1)}, f32[4,4,512]{2,1,0:T(4,128)}, u32[]{:S(2)}) copy-start(f32[4,4,512]{2,1,0:T(4,128)} %get-tuple-element.291) | copy-start | bytes 98308
  187.7 12.1 %collective-permute-start.11 = (bf16[1,256,1024]{2,1,0:T(8,128)(2,1)}, bf16[1,256,1024]{2,1,0:T(8,128)(2,1)S(1)}, u32[]{:S(2)}, u32[]{:S(2)}) collective-permute-start(bf16[1,256,1024]{2,1,0:T(8,128)(2,1)} %get-tuple-element.408), channel_id=1, source_target_pairs={{0,8},{2,10},{4,12},{6,14},{8,0},{10,2},{12,4},{14,6},{16,24},{18,... | collective-permute-start | bytes 1572872 | tf_op jit(solution)/shard_map/ppermute | solution.py:429
  188.0 30.5 %collective-permute-start.13 = (bf16[2,1024,256]{2,1,0:T(8,128)(2,1)}, bf16[2,1024,256]{2,1,0:T(8,128)(2,1)}, u32[]{:S(2)}, u32[]{:S(2)}) collective-permute-start(bf16[2,1024,256]{2,1,0:T(8,128)(2,1)} %get-tuple-element.398), channel_id=1, source_target_pairs={{0,4},{2,6},{4,0},{6,2},{8,12},{10,14},{12,8},{14,10},{16,20},{18,... | collective-permute-start | bytes 3145736 | tf_op jit(solution)/shard_map/ppermute | solution.py:429
  196.8 30.4 %collective-permute-start.10 = (bf16[4,2,128,512]{3,2,1,0:T(8,128)(2,1)}, bf16[4,2,128,512]{3,2,1,0:T(8,128)(2,1)S(1)}, u32[]{:S(2)}, u32[]{:S(2)}) collective-permute-start(bf16[4,2,128,512]{3,2,1,0:T(8,128)(2,1)} %get-tuple-element.298), channel_id=1, source_target_pairs={{0,2},{2,0},{4,6},{6,4},{8,10},{10,8},{12,14},{14,12},{16,18},{18,... | collective-permute-start | bytes 3145736 | tf_op jit(solution)/shard_map/ppermute | solution.py:429
  201.9 25.0 %collective-permute-start.12 = (bf16[1,256,1024]{2,1,0:T(8,128)(2,1)S(1)}, bf16[1,256,1024]{2,1,0:T(8,128)(2,1)S(1)}, u32[]{:S(2)}, u32[]{:S(2)}) collective-permute-start(bf16[1,256,1024]{2,1,0:T(8,128)(2,1)S(1)} %add_convert_fusion.13), channel_id=1, source_target_pairs={{0,16},{2,18},{4,20},{6,22},{8,24},{10,26},{12,28},{14,30},{16,0},... | collective-permute-start | bytes 1572872 | tf_op jit(solution)/shard_map/ppermute | solution.py:429
  209.5 19.1 %collective-permute-start.18 = (bf16[4,2,128,512]{3,2,1,0:T(8,128)(2,1)}, bf16[4,2,128,512]{3,2,1,0:T(8,128)(2,1)}, u32[]{:S(2)}, u32[]{:S(2)}) collective-permute-start(bf16[4,2,128,512]{3,2,1,0:T(8,128)(2,1)} %get-tuple-element.308), channel_id=1, source_target_pairs={{0,2},{2,0},{4,6},{6,4},{8,10},{10,8},{12,14},{14,12},{16,18},{18,... | collective-permute-start | bytes 3145736 | tf_op jit(solution)/shard_map/ppermute | solution.py:429
  218.0 9.2 %copy-start.7 = (bf16[4,2,128,512]{3,2,1,0:T(8,128)(2,1)S(1)}, bf16[4,2,128,512]{3,2,1,0:T(8,128)(2,1)}, u32[]{:S(2)}) copy-start(bf16[4,2,128,512]{3,2,1,0:T(8,128)(2,1)} %get-tuple-element.316) | copy-start | bytes 3145732
  218.0 45.7 %collective-permute-start.22 = (bf16[512,1024]{1,0:T(8,128)(2,1)}, bf16[512,1024]{1,0:T(8,128)(2,1)}, u32[]{:S(2)}, u32[]{:S(2)}) collective-permute-start(bf16[512,1024]{1,0:T(8,128)(2,1)} %first_rows.2), channel_id=1, source_target_pairs={{0,1},{1,0},{2,3},{3,2},{4,5},{5,4},{6,7},{7,6},{8,9},{9,8},{10,11... | collective-permute-start | bytes 3145736 | tf_op jit(solution)/shard_map/ppermute | solution.py:793
  219.9 19.4 %collective-permute-start.17 = (bf16[1,1024,256]{2,1,0:T(8,128)(2,1)S(1)}, bf16[1,1024,256]{2,1,0:T(8,128)(2,1)S(1)}, u32[]{:S(2)}, u32[]{:S(2)}) collective-permute-start(bf16[1,1024,256]{2,1,0:T(8,128)(2,1)S(1)} %get-tuple-element.406), channel_id=1, source_target_pairs={{0,8},{2,10},{4,12},{6,14},{8,0},{10,2},{12,4},{14,6},{16,24},{18,... | collective-permute-start | bytes 1572872 | tf_op jit(solution)/shard_map/ppermute | solution.py:429
  227.1 27.5 %collective-permute-start.16 = (bf16[1,256,1024]{2,1,0:T(8,128)(2,1)S(1)}, bf16[1,256,1024]{2,1,0:T(8,128)(2,1)S(1)}, u32[]{:S(2)}, u32[]{:S(2)}) collective-permute-start(bf16[1,256,1024]{2,1,0:T(8,128)(2,1)S(1)} %add_convert_fusion.10), channel_id=1, source_target_pairs={{0,8},{2,10},{4,12},{6,14},{8,0},{10,2},{12,4},{14,6},{16,24},{18,... | collective-permute-start | bytes 1572872 | tf_op jit(solution)/shard_map/ppermute | solution.py:429
  227.5 28.4 %collective-permute-start.15 = (bf16[2,2,128,512]{3,2,1,0:T(8,128)(2,1)S(1)}, bf16[2,2,128,512]{3,2,1,0:T(8,128)(2,1)S(1)}, u32[]{:S(2)}, u32[]{:S(2)}) collective-permute-start(bf16[2,2,128,512]{3,2,1,0:T(8,128)(2,1)S(1)} %get-tuple-element.403), channel_id=1, source_target_pairs={{0,4},{2,6},{4,0},{6,2},{8,12},{10,14},{12,8},{14,10},{16,20},{18,... | collective-permute-start | bytes 1572872 | tf_op jit(solution)/shard_map/ppermute | solution.py:429
  230.1 26.7 %collective-permute-start.21 = (bf16[2,2,128,512]{3,2,1,0:T(8,128)(2,1)S(1)}, bf16[2,2,128,512]{3,2,1,0:T(8,128)(2,1)S(1)}, u32[]{:S(2)}, u32[]{:S(2)}) collective-permute-start(bf16[2,2,128,512]{3,2,1,0:T(8,128)(2,1)S(1)} %get-tuple-element.402), channel_id=1, source_target_pairs={{0,4},{2,6},{4,0},{6,2},{8,12},{10,14},{12,8},{14,10},{16,20},{18,... | collective-permute-start | bytes 1572872 | tf_op jit(solution)/shard_map/ppermute | solution.py:429
  239.4 30.3 %collective-permute-start.20 = (bf16[1,1024,256]{2,1,0:T(8,128)(2,1)S(1)}, bf16[1,1024,256]{2,1,0:T(8,128)(2,1)S(1)}, u32[]{:S(2)}, u32[]{:S(2)}) collective-permute-start(bf16[1,1024,256]{2,1,0:T(8,128)(2,1)S(1)} %add_convert_fusion.5), channel_id=1, source_target_pairs={{0,16},{2,18},{4,20},{6,22},{8,24},{10,26},{12,28},{14,30},{16,0},... | collective-permute-start | bytes 1572872 | tf_op jit(solution)/shard_map/ppermute | solution.py:429
  254.7 23.1 %copy-start = (bf16[2,256,1024]{2,1,0:T(8,128)(2,1)}, bf16[2,256,1024]{2,1,0:T(8,128)(2,1)S(1)}, u32[]{:S(2)}) copy-start(bf16[2,256,1024]{2,1,0:T(8,128)(2,1)S(1)} %constant_dynamic-update-slice_fusion.refs_0_) | copy-start | bytes 3145732
  254.7 24.4 %collective-permute-start.29 = (bf16[2,256,1024]{2,1,0:T(8,128)(2,1)S(1)}, bf16[2,256,1024]{2,1,0:T(8,128)(2,1)}, u32[]{:S(2)}, u32[]{:S(2)}) collective-permute-start(bf16[2,256,1024]{2,1,0:T(8,128)(2,1)S(1)} %constant_dynamic-update-slice_fusion.refs_0_), channel_id=1, source_target_pairs={{0,4},{2,6},{4,0},{6,2},{8,12},{10,14},{12,8},{14,10},{16,20},{18,... | collective-permute-start | bytes 3145736 | tf_op jit(solution)/shard_map/ppermute | solution.py:429
  257.7 20.4 %collective-permute-start.24 = (bf16[1,2,128,512]{3,2,1,0:T(8,128)(2,1)}, bf16[1,2,128,512]{3,2,1,0:T(8,128)(2,1)S(1)}, u32[]{:S(2)}, u32[]{:S(2)}) collective-permute-start(bf16[1,2,128,512]{3,2,1,0:T(8,128)(2,1)} %get-tuple-element.410), channel_id=1, source_target_pairs={{0,8},{2,10},{4,12},{6,14},{8,0},{10,2},{12,4},{14,6},{16,24},{18,... | collective-permute-start | bytes 786440 | tf_op jit(solution)/shard_map/ppermute | solution.py:429
  263.7 11.0 %copy-start.22 = (f32[1,2048]{1,0:T(1,128)S(1)}, f32[1,2048]{1,0:T(1,128)}, u32[]{:S(2)}) copy-start(f32[1,2048]{1,0:T(1,128)} %get-tuple-element.342) | copy-start | bytes 24580
  263.7 11.0 %copy-start.23 = (f32[1,2048]{1,0:T(1,128)S(1)}, f32[1,2048]{1,0:T(1,128)}, u32[]{:S(2)}) copy-start(f32[1,2048]{1,0:T(1,128)} %get-tuple-element.341) | copy-start | bytes 24580
  269.8 12.8 %collective-permute-start.23 = (bf16[1,1024,256]{2,1,0:T(8,128)(2,1)S(1)}, bf16[1,1024,256]{2,1,0:T(8,128)(2,1)S(1)}, u32[]{:S(2)}, u32[]{:S(2)}) collective-permute-start(bf16[1,1024,256]{2,1,0:T(8,128)(2,1)S(1)} %add_convert_fusion.4), channel_id=1, source_target_pairs={{0,8},{2,10},{4,12},{6,14},{8,0},{10,2},{12,4},{14,6},{16,24},{18,... | collective-permute-start | bytes 1572872 | tf_op jit(solution)/shard_map/ppermute | solution.py:429
  271.4 3.2 collective-permute-start.25
  274.7 3.0 collective-permute-start.26
  276.9 15.9 %collective-permute-start.19 = (bf16[1,2,128,512]{3,2,1,0:T(8,128)(2,1)S(1)}, bf16[1,2,128,512]{3,2,1,0:T(8,128)(2,1)S(1)}, u32[]{:S(2)}, u32[]{:S(2)}) collective-permute-start(bf16[1,2,128,512]{3,2,1,0:T(8,128)(2,1)S(1)} %get-tuple-element.411), channel_id=1, source_target_pairs={{0,8},{2,10},{4,12},{6,14},{8,0},{10,2},{12,4},{14,6},{16,24},{18,... | collective-permute-start | bytes 786440 | tf_op jit(solution)/shard_map/ppermute | solution.py:429
  277.7 24.4 %collective-permute-start.30 = (bf16[2,256,1024]{2,1,0:T(8,128)(2,1)S(1)}, bf16[2,256,1024]{2,1,0:T(8,128)(2,1)}, u32[]{:S(2)}, u32[]{:S(2)}) collective-permute-start(bf16[2,256,1024]{2,1,0:T(8,128)(2,1)S(1)} %constant_dynamic-update-slice_fusion.refs_0_), channel_id=1, source_target_pairs={{0,2},{2,0},{4,6},{6,4},{8,10},{10,8},{12,14},{14,12},{16,18},{18,... | collective-permute-start | bytes 3145736 | tf_op jit(solution)/shard_map/ppermute | solution.py:429
  279.1 23.1 %collective-permute-start.31 = (bf16[2,256,1024]{2,1,0:T(8,128)(2,1)}, bf16[2,256,1024]{2,1,0:T(8,128)(2,1)}, u32[]{:S(2)}, u32[]{:S(2)}) collective-permute-start(bf16[2,256,1024]{2,1,0:T(8,128)(2,1)} %collective-permute-done.29.refs_1_), channel_id=1, source_target_pairs={{0,2},{2,0},{4,6},{6,4},{8,10},{10,8},{12,14},{14,12},{16,18},{18,... | collective-permute-start | bytes 3145736 | tf_op jit(solution)/shard_map/ppermute | solution.py:429
  281.2 19.2 %collective-permute-start.32 = (bf16[1,2,128,512]{3,2,1,0:T(8,128)(2,1)}, bf16[1,2,128,512]{3,2,1,0:T(8,128)(2,1)}, u32[]{:S(2)}, u32[]{:S(2)}) collective-permute-start(bf16[1,2,128,512]{3,2,1,0:T(8,128)(2,1)} %add_convert_fusion.19), channel_id=1, source_target_pairs={{0,16},{2,18},{4,20},{6,22},{8,24},{10,26},{12,28},{14,30},{16,0},... | collective-permute-start | bytes 786440 | tf_op jit(solution)/shard_map/ppermute | solution.py:429
  282.7 32.5 %copy-start.1 = (bf16[2,1024,256]{2,1,0:T(8,128)(2,1)}, bf16[2,1024,256]{2,1,0:T(8,128)(2,1)S(1)}, u32[]{:S(2)}) copy-start(bf16[2,1024,256]{2,1,0:T(8,128)(2,1)S(1)} %constant_dynamic-update-slice_fusion.2.refs_0_) | copy-start | bytes 3145732
  282.7 36.3 %collective-permute-start.37 = (bf16[2,1024,256]{2,1,0:T(8,128)(2,1)S(1)}, bf16[2,1024,256]{2,1,0:T(8,128)(2,1)S(1)}, u32[]{:S(2)}, u32[]{:S(2)}) collective-permute-start(bf16[2,1024,256]{2,1,0:T(8,128)(2,1)S(1)} %constant_dynamic-update-slice_fusion.2.refs_0_), channel_id=1, source_target_pairs={{0,4},{2,6},{4,0},{6,2},{8,12},{10,14},{12,8},{14,10},{16,20},{18,... | collective-permute-start | bytes 3145736 | tf_op jit(solution)/shard_map/ppermute | solution.py:429
  299.3 25.0 %collective-permute-start.27 = (bf16[512,1024]{1,0:T(8,128)(2,1)}, bf16[512,1024]{1,0:T(8,128)(2,1)}, u32[]{:S(2)}, u32[]{:S(2)}) collective-permute-start(bf16[512,1024]{1,0:T(8,128)(2,1)} %reduced.1), channel_id=1, source_target_pairs={{0,1},{1,0},{2,3},{3,2},{4,5},{5,4},{6,7},{7,6},{8,9},{9,8},{10,11... | collective-permute-start | bytes 3145736 | tf_op jit(solution)/shard_map/ppermute | solution.py:793
  300.4 13.8 %collective-permute-start.28 = (bf16[1,2,128,512]{3,2,1,0:T(8,128)(2,1)S(1)}, bf16[1,2,128,512]{3,2,1,0:T(8,128)(2,1)}, u32[]{:S(2)}, u32[]{:S(2)}) collective-permute-start(bf16[1,2,128,512]{3,2,1,0:T(8,128)(2,1)S(1)} %add_convert_fusion.18), channel_id=1, source_target_pairs={{0,16},{2,18},{4,20},{6,22},{8,24},{10,26},{12,28},{14,30},{16,0},... | collective-permute-start | bytes 786440 | tf_op jit(solution)/shard_map/ppermute | solution.py:429
  302.2 13.1 %collective-permute-start.35 = (f32[58,128]{1,0:T(8,128)S(1)}, f32[58,128]{1,0:T(8,128)S(1)}, u32[]{:S(2)}, u32[]{:S(2)}) collective-permute-start(f32[58,128]{1,0:T(8,128)S(1)} %add.176), channel_id=1, source_target_pairs={{0,4},{2,6},{4,0},{6,2},{8,12},{10,14},{12,8},{14,10},{16,20},{18,... | collective-permute-start | bytes 89096 | tf_op jit(solution)/shard_map/ppermute | solution.py:429
  302.2 14.1 %collective-permute-start.34 = (bf16[1,2,128,512]{3,2,1,0:T(8,128)(2,1)}, bf16[1,2,128,512]{3,2,1,0:T(8,128)(2,1)S(1)}, u32[]{:S(2)}, u32[]{:S(2)}) collective-permute-start(bf16[1,2,128,512]{3,2,1,0:T(8,128)(2,1)} %add_convert_fusion.17), channel_id=1, source_target_pairs={{0,8},{2,10},{4,12},{6,14},{8,0},{10,2},{12,4},{14,6},{16,24},{18,... | collective-permute-start | bytes 786440 | tf_op jit(solution)/shard_map/ppermute | solution.py:429
  315.1 7.1 %collective-permute-start.33 = (bf16[1,2,128,512]{3,2,1,0:T(8,128)(2,1)S(1)}, bf16[1,2,128,512]{3,2,1,0:T(8,128)(2,1)S(1)}, u32[]{:S(2)}, u32[]{:S(2)}) collective-permute-start(bf16[1,2,128,512]{3,2,1,0:T(8,128)(2,1)S(1)} %add_convert_fusion.16), channel_id=1, source_target_pairs={{0,8},{2,10},{4,12},{6,14},{8,0},{10,2},{12,4},{14,6},{16,24},{18,... | collective-permute-start | bytes 786440 | tf_op jit(solution)/shard_map/ppermute | solution.py:429
  315.2 19.0 %collective-permute-start.38 = (bf16[2,1024,256]{2,1,0:T(8,128)(2,1)S(1)}, bf16[2,1024,256]{2,1,0:T(8,128)(2,1)}, u32[]{:S(2)}, u32[]{:S(2)}) collective-permute-start(bf16[2,1024,256]{2,1,0:T(8,128)(2,1)S(1)} %constant_dynamic-update-slice_fusion.2.refs_0_), channel_id=1, source_target_pairs={{0,2},{2,0},{4,6},{6,4},{8,10},{10,8},{12,14},{14,12},{16,18},{18,... | collective-permute-start | bytes 3145736 | tf_op jit(solution)/shard_map/ppermute | solution.py:429
  316.2 27.1 %collective-permute-start.36 = (f32[58,128]{1,0:T(8,128)S(1)}, f32[58,128]{1,0:T(8,128)S(1)}, u32[]{:S(2)}, u32[]{:S(2)}) collective-permute-start(f32[58,128]{1,0:T(8,128)S(1)} %add.181), channel_id=1, source_target_pairs={{0,8},{2,10},{4,12},{6,14},{8,0},{10,2},{12,4},{14,6},{16,24},{18,... | collective-permute-start | bytes 89096 | tf_op jit(solution)/shard_map/ppermute | solution.py:429
  319.0 13.4 %copy-start.4 = (bf16[2,2,128,512]{3,2,1,0:T(8,128)(2,1)}, bf16[2,2,128,512]{3,2,1,0:T(8,128)(2,1)S(1)}, u32[]{:S(2)}) copy-start(bf16[2,2,128,512]{3,2,1,0:T(8,128)(2,1)S(1)} %constant_dynamic-update-slice_fusion.4.refs_4_) | copy-start | bytes 1572868
  319.0 12.8 %copy-start.6 = (bf16[2,1024,256]{2,1,0:T(8,128)(2,1)}, bf16[2,1024,256]{2,1,0:T(8,128)(2,1)S(1)}, u32[]{:S(2)}) copy-start(bf16[2,1024,256]{2,1,0:T(8,128)(2,1)S(1)} %collective-permute-done.37.refs_1_) | copy-start | bytes 3145732
  319.0 13.4 %collective-permute-start.44 = (bf16[2,2,128,512]{3,2,1,0:T(8,128)(2,1)S(1)}, bf16[2,2,128,512]{3,2,1,0:T(8,128)(2,1)}, u32[]{:S(2)}, u32[]{:S(2)}) collective-permute-start(bf16[2,2,128,512]{3,2,1,0:T(8,128)(2,1)S(1)} %constant_dynamic-update-slice_fusion.4.refs_4_), channel_id=1, source_target_pairs={{0,4},{2,6},{4,0},{6,2},{8,12},{10,14},{12,8},{14,10},{16,20},{18,... | collective-permute-start | bytes 1572872 | tf_op jit(solution)/shard_map/ppermute | solution.py:429
  322.2 12.1 %collective-permute-start.39 = (bf16[2,1024,256]{2,1,0:T(8,128)(2,1)S(1)}, bf16[2,1024,256]{2,1,0:T(8,128)(2,1)}, u32[]{:S(2)}, u32[]{:S(2)}) collective-permute-start(bf16[2,1024,256]{2,1,0:T(8,128)(2,1)S(1)} %collective-permute-done.37.refs_1_), channel_id=1, source_target_pairs={{0,2},{2,0},{4,6},{6,4},{8,10},{10,8},{12,14},{14,12},{16,18},{18,... | collective-permute-start | bytes 3145736 | tf_op jit(solution)/shard_map/ppermute | solution.py:429
  324.3 9.9 %copy-start.5 = (bf16[2,2,128,512]{3,2,1,0:T(8,128)(2,1)}, bf16[2,2,128,512]{3,2,1,0:T(8,128)(2,1)S(1)}, u32[]{:S(2)}) copy-start(bf16[2,2,128,512]{3,2,1,0:T(8,128)(2,1)S(1)} %constant_dynamic-update-slice_fusion.6.refs_0_) | copy-start | bytes 1572868
  324.4 19.3 %collective-permute-start.41 = (bf16[2,2,128,512]{3,2,1,0:T(8,128)(2,1)S(1)}, bf16[2,2,128,512]{3,2,1,0:T(8,128)(2,1)}, u32[]{:S(2)}, u32[]{:S(2)}) collective-permute-start(bf16[2,2,128,512]{3,2,1,0:T(8,128)(2,1)S(1)} %constant_dynamic-update-slice_fusion.6.refs_0_), channel_id=1, source_target_pairs={{0,4},{2,6},{4,0},{6,2},{8,12},{10,14},{12,8},{14,10},{16,20},{18,... | collective-permute-start | bytes 1572872 | tf_op jit(solution)/shard_map/ppermute | solution.py:429
  332.4 18.9 %collective-permute-start.45 = (bf16[2,2,128,512]{3,2,1,0:T(8,128)(2,1)S(1)}, bf16[2,2,128,512]{3,2,1,0:T(8,128)(2,1)}, u32[]{:S(2)}, u32[]{:S(2)}) collective-permute-start(bf16[2,2,128,512]{3,2,1,0:T(8,128)(2,1)S(1)} %constant_dynamic-update-slice_fusion.4.refs_4_), channel_id=1, source_target_pairs={{0,2},{2,0},{4,6},{6,4},{8,10},{10,8},{12,14},{14,12},{16,18},{18,... | collective-permute-start | bytes 1572872 | tf_op jit(solution)/shard_map/ppermute | solution.py:429
  334.2 17.0 %collective-permute-start.42 = (bf16[2,2,128,512]{3,2,1,0:T(8,128)(2,1)S(1)}, bf16[2,2,128,512]{3,2,1,0:T(8,128)(2,1)S(1)}, u32[]{:S(2)}, u32[]{:S(2)}) collective-permute-start(bf16[2,2,128,512]{3,2,1,0:T(8,128)(2,1)S(1)} %constant_dynamic-update-slice_fusion.6.refs_0_), channel_id=1, source_target_pairs={{0,2},{2,0},{4,6},{6,4},{8,10},{10,8},{12,14},{14,12},{16,18},{18,... | collective-permute-start | bytes 1572872 | tf_op jit(solution)/shard_map/ppermute | solution.py:429
  334.3 17.0 %collective-permute-start.46 = (bf16[2,2,128,512]{3,2,1,0:T(8,128)(2,1)}, bf16[2,2,128,512]{3,2,1,0:T(8,128)(2,1)S(1)}, u32[]{:S(2)}, u32[]{:S(2)}) collective-permute-start(bf16[2,2,128,512]{3,2,1,0:T(8,128)(2,1)} %collective-permute-done.44.refs_5_), channel_id=1, source_target_pairs={{0,2},{2,0},{4,6},{6,4},{8,10},{10,8},{12,14},{14,12},{16,18},{18,... | collective-permute-start | bytes 1572872 | tf_op jit(solution)/shard_map/ppermute | solution.py:429
  343.6 7.7 %collective-permute-start.43 = (bf16[2,2,128,512]{3,2,1,0:T(8,128)(2,1)}, bf16[2,2,128,512]{3,2,1,0:T(8,128)(2,1)S(1)}, u32[]{:S(2)}, u32[]{:S(2)}) collective-permute-start(bf16[2,2,128,512]{3,2,1,0:T(8,128)(2,1)} %collective-permute-done.41.refs_1_), channel_id=1, source_target_pairs={{0,2},{2,0},{4,6},{6,4},{8,10},{10,8},{12,14},{14,12},{16,18},{18,... | collective-permute-start | bytes 1572872 | tf_op jit(solution)/shard_map/ppermute | solution.py:429
  344.7 4.6 %collective-permute-start.40 = (f32[58,128]{1,0:T(8,128)S(1)}, f32[58,128]{1,0:T(8,128)S(1)}, u32[]{:S(2)}, u32[]{:S(2)}) collective-permute-start(f32[58,128]{1,0:T(8,128)S(1)} %add.182), channel_id=1, source_target_pairs={{0,16},{2,18},{4,20},{6,22},{8,24},{10,26},{12,28},{14,30},{16,0},... | collective-permute-start | bytes 89096 | tf_op jit(solution)/shard_map/ppermute | solution.py:429
  (11 other events, 18.3 us)
where the time goes:
time: 367 us; the launch traced here: 362 us
  Pallas kernels  194 us (53%)
  waiting for transfers between devices  84 us (23%)
  starting transfers between devices  43.5 us (12%)
  other arithmetic  22.8 us (6%)
  local copies, waits for them, and re-layouts  10.4 us (3%)
  matrix products  5.63 us (2%)
    ppermute x37, waiting for transfers between devices, trade(): return lax.ppermute(x, 'dp', [(i, i ^ bit) for i in range(size)])  53 us
    pallas_call x4, Pallas kernels, pair_call(): pl.pallas_call(functools.partial(kernel, slot), grid_spec=pltpu.PrefetchS...  34.8 us
    ppermute x37, starting transfers between devices, trade(): return lax.ppermute(x, 'dp', [(i, i ^ bit) for i in range(size)])  34.1 us
    ppermute x10, waiting for transfers between devices, swap(): return lax.ppermute(x, 'mp', [(0, 1), (1, 0)])  30.9 us
    pallas_call x2, Pallas kernels, expand(): pl.pallas_call(expand_kernel, grid=(hidden // step,), in_specs=[pl.BlockS...  23.8 us
    pallas_call x1, Pallas kernels, attend_backward(): pl.pallas_call(kernel, grid_spec=pltpu.PrefetchScalarGridSpec(num_scalar_...  22.8 us
    convert_element_type x16, other arithmetic, add_low(): return (a.astype(F32) + b.astype(F32)).astype(BF16)  18.8 us
    pallas_call x3, Pallas kernels, columns_dot(): pl.pallas_call(functools.partial(columns_kernel, turn), grid=(columns //...  17.8 us
  transfers between devices with their start and end apart: 47, of which 18 were waited for; matrix products, arithmetic and copies ran while one was open for 9% of the time, Pallas kernels for 46%

commit v1 on v0

--- a/solution.py
+++ b/solution.py
@@ -277,27 +277,22 @@
 
 
 def project_kernel(x_ref, gain_ref, shift_ref, w_ref, low_ref, out_ref):
-    @pl.when(pl.program_id(0) == 0)
-    def _():
-        def some(i, _):
-            rows = pl.ds(pl.multiple_of(i * 128, 128), 128)
-            normed, _ = row_norm(x_ref[rows, :].astype(F32))
-            low_ref[rows, :] = (normed * gain_ref[...] + shift_ref[...]).astype(BF16)
-            return 0
-
-        lax.fori_loop(0, x_ref.shape[0] // 128, some, 0)
-
-    out_ref[0] = dot(low_ref[...], w_ref[0], 1, 0).astype(BF16)
+    normed, _ = row_norm(x_ref[...].astype(F32))
+    low = (normed * gain_ref[...] + shift_ref[...]).astype(BF16)
+    low_ref[...] = low
+    for c in range(3):
+        out_ref[c] = dot(low, w_ref[c], 1, 0).astype(BF16)
 
 
 def project(x, gain, shift, weight):
     rows, model = x.shape
     width = weight.shape[2]
+    step = min(256, rows)
     return pl.pallas_call(
         project_kernel,
-        grid=(3,),
-        in_specs=[fixed((rows, model)), fixed((1, model)), fixed((1, model)), pl.BlockSpec((1, model, width), lambda c: (c, 0, 0))],
-        out_specs=[fixed((rows, model)), pl.BlockSpec((1, rows, width), lambda c: (c, 0, 0))],
+        grid=(rows // step,),
+        in_specs=[pl.BlockSpec((step, model), lambda i: (i, 0)), fixed((1, model)), fixed((1, model)), fixed(weight.shape)],
+        out_specs=[pl.BlockSpec((step, model), lambda i: (i, 0)), pl.BlockSpec((3, step, width), lambda i: (0, i, 0))],
         out_shape=[jax.ShapeDtypeStruct((rows, model), BF16), jax.ShapeDtypeStruct((3, rows, width), BF16)],
         cost_estimate=cost(6 * rows * model * width, 2 * (2 * rows * model + weight.size + 3 * rows * width)),
         name="project",
@@ -318,7 +313,7 @@
     @pl.when(i < own_blocks)
     def _():
         middle = rows(x0_ref)
-        mid_ref[...] = middle
+        mid_ref[...] = middle.astype(BF16)
         rest(middle)
 
     @pl.when(i >= own_blocks)
@@ -345,7 +340,7 @@
             pl.BlockSpec((step, model), lambda i: (jnp.minimum(i, n - 1), 0)),
             pl.BlockSpec((step, model), lambda i: (i, 0)),
         ],
-        out_shape=[jax.ShapeDtypeStruct((own, model), F32), jax.ShapeDtypeStruct((2 * own, model), BF16)],
+        out_shape=[jax.ShapeDtypeStruct((own, model), BF16), jax.ShapeDtypeStruct((2 * own, model), BF16)],
         cost_estimate=cost(8 * own * model * width, 2 * (4 * own * model + 4 * own * width + 2 * weight.size) + 4 * own * model),
         name="mix",
     )(tokens, other, mixed, mixed_other, weight, weight_other, gain, shift)
@@ -559,14 +554,14 @@
         in_specs=[fixed(a.shape), pl.BlockSpec(*block)],
         out_specs=pl.BlockSpec((rows, step), lambda i: (0, i)),
         out_shape=jax.ShapeDtypeStruct((rows, columns), BF16),
-        cost_estimate=cost(2 * rows * depth * columns, 2 * (a.size + b.size + rows * columns)),
+        cost_estimate=cost16(2 * rows * depth * columns, 2 * (a.size + b.size + rows * columns)),
         name=name,
     )(a, b)
 
 
 def output_kernel(m_ref, a_ref, w_ref, r_ref, bias_ref, out_ref):
     out_ref[...] = (
-        m_ref[...] + dot(a_ref[...], w_ref[...], 1, 0) + r_ref[...].astype(F32) + bias_ref[...]
+        m_ref[...].astype(F32) + dot(a_ref[...], w_ref[...], 1, 0) + r_ref[...].astype(F32) + bias_ref[...]
     ).astype(BF16)
 
 
@@ -623,43 +618,39 @@
     )(grad, weight)
 
 
-def back_kernel(keep, a_ref, b_ref, source_ref, add_ref, gain_ref, *outs):
+def back_kernel(a_ref, b_ref, source_ref, add_ref, gain_ref, out_ref, sums_ref):
     @pl.when(pl.program_id(0) == 0)
     def _():
-        outs[-1][...] = jnp.zeros_like(outs[-1])
+        sums_ref[...] = jnp.zeros_like(sums_ref)
 
     def some(i, _):
         rows = pl.ds(pl.multiple_of(i * 64, 64), 64)
         normed, inverse = row_norm(source_ref[rows, :].astype(F32))
-        grad = a_ref[rows, :] + b_ref[rows, :].astype(F32)
+        grad = a_ref[rows, :].astype(F32) + b_ref[rows, :].astype(F32)
         add = add_ref[rows, :].astype(F32)
         scaled = grad * gain_ref[...]
         weighted = grad * normed
         mean = jnp.mean(scaled, axis=-1, keepdims=True)
         along = jnp.mean(scaled * normed, axis=-1, keepdims=True)
-        out = add + inverse * (scaled - mean - normed * along)
-        if keep:
-            outs[0][rows, :] = out
-        outs[-2][rows, :] = out.astype(BF16)
+        out_ref[rows, :] = (add + inverse * (scaled - mean - normed * along)).astype(BF16)
         for k, value in enumerate((weighted, grad, add)):
-            outs[-1][k:k + 1] += jnp.sum(value, axis=0, keepdims=True)
+            sums_ref[k:k + 1] += jnp.sum(value, axis=0, keepdims=True)
         return 0
 
     lax.fori_loop(0, source_ref.shape[0] // 64, some, 0)
 
 
-def back_rows(a, b, source, add, gain, keep):
+def back_rows(a, b, source, add, gain):
     rows, model = a.shape
     step = 256
     block = pl.BlockSpec((step, model), lambda i: (i, 0))
-    kinds = ([F32] if keep else []) + [BF16]
-    return pl.pallas_call(
-        functools.partial(back_kernel, keep),
+    return pl.pallas_call(
+        back_kernel,
         grid=(rows // step,),
         in_specs=[block] * 4 + [fixed((1, model))],
-        out_specs=[block] * len(kinds) + [fixed((8, model))],
-        out_shape=[jax.ShapeDtypeStruct((rows, model), kind) for kind in kinds] + [jax.ShapeDtypeStruct((8, model), F32)],
-        cost_estimate=cost(30 * rows * model, 16 * rows * model),
+        out_specs=[block, fixed((8, model))],
+        out_shape=[jax.ShapeDtypeStruct((rows, model), BF16), jax.ShapeDtypeStruct((8, model), F32)],
+        cost_estimate=cost(30 * rows * model, 10 * rows * model),
         name="back_rows",
     )(a, b, source, add, gain)
 
@@ -691,85 +682,74 @@
 
 def spread_kernel(put, s_ref, *refs):
     g = pl.program_id(0)
-    pieces, outs = refs[-4 - put.outs:-put.outs], refs[-put.outs:]
-    for a in range(4):
+    count = put.pieces
+    pieces, outs = refs[-2 * count - put.outs:-put.outs], refs[-put.outs:]
+    for a in range(2):
         @pl.when(g // 2 == a)
         def _(a=a):
-            put(pieces[a], outs)
-
-
-def spread(places, slot, pieces, put, tail, out_specs, out_shape, given=None, name=None):
+            put(pieces[a::2], outs)
+
+
+def spread(places, part, pieces, put, tail, out_specs, out_shape, given=None, name=None):
     zeros = (0,) * len(tail)
-    at = lambda g, s: g ^ s[slot]
+
+    def at(g, s):
+        return (g % 2 + 4 * (g // 2) + 2 * part) ^ s[0]
+
     in_specs = [
-        pl.BlockSpec((1, *tail), lambda g, s, a=a: (jnp.clip(g - 2 * a, 0, 1), *zeros)) for a in range(4)
+        pl.BlockSpec((1, *tail), lambda g, s, a=k % 2: (jnp.clip(g - 2 * a, 0, 1), *zeros)) for k in range(len(pieces))
     ]
     args = list(pieces)
     aliases = {}
     if given is not None:
-        in_specs.insert(0, pl.BlockSpec(memory_space=pl.ANY))
-        args.insert(0, given)
-        aliases = {1: 0}
+        in_specs = [pl.BlockSpec(memory_space=pl.ANY)] * len(given) + in_specs
+        args = [*given, *args]
+        aliases = {1 + k: k for k in range(len(given))}
     return pl.pallas_call(
         functools.partial(spread_kernel, put),
         grid_spec=pltpu.PrefetchScalarGridSpec(
-            num_scalar_prefetch=1, grid=(8,), in_specs=in_specs, out_specs=[spec(at) for spec in out_specs],
+            num_scalar_prefetch=1, grid=(4,), in_specs=in_specs, out_specs=[spec(at) for spec in out_specs],
         ),
         out_shape=out_shape,
         input_output_aliases=aliases,
-        cost_estimate=cost(0, 6 * 8 * math.prod(tail)),
+        cost_estimate=cost(0, 24 * len(pieces) // 2 * math.prod(tail)),
         name=name,
     )(places, *args)
 
 
-def put_rows(piece, outs):
-    outs[0][...] = piece[0].astype(F32)
+def by_rows(count, step):
+    def some(i, _):
+        step(pl.ds(pl.multiple_of(i * 64, 64), 64))
+        return 0
+
+    lax.fori_loop(0, count // 64, some, 0)
+
+
+def put_rows(pieces, outs):
+    def some(rows):
+        outs[0][rows, :] = pieces[0][0, rows, :].astype(F32)
+
+    by_rows(outs[0].shape[0], some)
 
 
 put_rows.outs = 1
-
-
-def spread_heads_kernel(value_slot, s_ref, *refs):
-    k = pl.program_id(0)
-    heads_ref, mixer_ref = refs[8:]
-    for slot in range(2):
-        r = k ^ s_ref[slot * value_slot]
-        for a in range(4):
-            piece = refs[4 * slot + a]
-
-            @pl.when(r // 2 == a)
-            def _(slot=slot, piece=piece):
-                if slot == 0:
-                    heads_ref[:2] = piece[0].astype(F32)
-                else:
-                    heads_ref[2] = piece[0, 0].astype(F32)
-                    mixer_ref[...] = piece[0, 1].astype(F32).T
-
-
-def spread_heads(places, value_slot, queries, values, model, width):
-    tail = (2, model // 8, width)
-
-    def spec(slot, a):
-        def at(k, s):
-            r = k ^ s[slot]
-            return (jnp.where(r // 2 == a, r % 2, 0), 0, 0, 0)
-
-        return pl.BlockSpec((1, *tail), at)
-
-    return pl.pallas_call(
-        functools.partial(spread_heads_kernel, value_slot),
-        grid_spec=pltpu.PrefetchScalarGridSpec(
-            num_scalar_prefetch=1, grid=(8,),
-            in_specs=[spec(slot * value_slot, a) for slot in range(2) for a in range(4)],
-            out_specs=[
-                pl.BlockSpec((3, model // 8, width), lambda k, s: (0, k, 0)),
-                pl.BlockSpec((width, model // 8), lambda k, s: (0, k)),
-            ],
-        ),
-        out_shape=[jax.ShapeDtypeStruct((3, model, width), F32), jax.ShapeDtypeStruct((width, model), F32)],
-        cost_estimate=cost(0, 12 * 8 * math.prod(tail)),
-        name="spread_heads",
-    )(places, *queries, *values)
+put_rows.pieces = 1
+
+
+def put_heads(pieces, outs):
+    queries, values = pieces
+
+    def some(rows):
+        for c in range(2):
+            outs[0][c, rows, :] = queries[0, c, rows, :].astype(F32)
+        outs[0][2, rows, :] = values[0, 0, rows, :].astype(F32)
+
+    by_rows(outs[0].shape[1], some)
+    outs[1][...] = values[0, 1].astype(F32).T
+
+
+put_heads.outs = 2
+put_heads.pieces = 2
 
 
 def normalize(values):
@@ -853,8 +833,11 @@
     def sixth(self):
         self.far_other = trade(tie(self.far, self.line.last), self.stages[0])
 
-    def pieces(self):
-        return self.near, self.far, self.near_other, self.far_other
+    def nears(self):
+        return self.near, self.near_other
+
+    def fars(self):
+        return self.far, self.far_other
 
 
 class Held:
@@ -935,7 +918,7 @@
 
     def expand_own():
         v.act0, v.ge0, v.gs0, v.eb0 = line(
-            lambda x, g, w, b: expand(x, 0, own, g, w, b, F32),
+            lambda x, g, w, b: expand(x, 0, own, g, w, b, BF16),
             v.second, v.active_grad0, expand_weight, row(expand_bias),
         )
 
@@ -948,8 +931,8 @@
         expand_sum.begin(*line(lambda *xs: expand_grad_part(at, 0, *xs), v.second, v.ge0, v.ge1))
 
     def middle_back():
-        v.grad_middle, v.attended0, v.second_sums = line(
-            lambda *xs: back_rows(*xs, True), v.gs0, v.gs_got, v.middle, target0, row(second_gain)
+        v.attended0, v.second_sums = line(
+            back_rows, v.gs0, v.gs_got, v.middle, target0, row(second_gain)
         )
 
     grad_mix = lambda a, w: dot(a, w, 1, 1).astype(BF16)
@@ -988,11 +971,11 @@
         v.first_got = swap(out)
 
     def first_own():
-        v.first_part = line(lambda g, w: first_rows(g, w, 0, own, F32), v.grad_projected, heads_weight)
+        v.first_part = line(lambda g, w: first_rows(g, w, 0, own, BF16), v.grad_projected, heads_weight)
 
     def first_back():
         v.tokens_grad, first_sums = line(
-            lambda *xs: back_rows(*xs, False), v.first_part, v.first_got, tokens, v.grad_middle, row(first_gain)
+            back_rows, v.first_part, v.first_got, tokens, v.attended0, row(first_gain)
         )
         v.both = join(first_sums[:2], v.second_sums[:3])
         v.both_got = swap(v.both)
@@ -1022,27 +1005,51 @@
     chunk = (hidden // 8, model)
     turned = (model, hidden // 8)
 
-    def reduce_spread():
-        (v.reduce_grad,) = line(
-            lambda *xs: spread(
-                at, 0, xs, put_rows, chunk, [lambda to: pl.BlockSpec(chunk, lambda g, s: (to(g, s), 0))],
-                [jax.ShapeDtypeStruct(reduce_weight.shape, F32)], name="spread_reduce",
-            ),
-            *reduce_sum.pieces(),
-        )
-
-    def expand_spread():
-        (v.expand_grad,) = line(
-            lambda *xs: spread(
-                at, 0, xs, put_rows, turned, [lambda to: pl.BlockSpec(turned, lambda g, s: (0, to(g, s)))],
-                [jax.ShapeDtypeStruct(expand_weight.shape, F32)], name="spread_expand",
-            ),
-            *expand_sum.pieces(),
-        )
-
-    def heads_spread():
-        v.heads_grad, v.mixer_grad = line(
-            lambda *xs: spread_heads(at, 0, xs[:4], xs[4:], model, width), *query_sum.pieces(), *value_sum.pieces()
+    piece = (2, model // 8, width)
+    reduce_shape = [jax.ShapeDtypeStruct(reduce_weight.shape, F32)]
+    expand_shape = [jax.ShapeDtypeStruct(expand_weight.shape, F32)]
+    heads_shape = [jax.ShapeDtypeStruct(heads_weight.shape, F32), jax.ShapeDtypeStruct(mixer_weight.shape, F32)]
+    reduce_spec = [lambda to: pl.BlockSpec(chunk, lambda g, s: (to(g, s), 0))]
+    expand_spec = [lambda to: pl.BlockSpec(turned, lambda g, s: (0, to(g, s)))]
+    heads_spec = [
+        lambda to: pl.BlockSpec((3, model // 8, width), lambda g, s: (0, to(g, s), 0)),
+        lambda to: pl.BlockSpec((width, model // 8), lambda g, s: (0, to(g, s))),
+    ]
+
+    def reduce_near():
+        v.reduce_grad = line(
+            lambda *xs: spread(at, 0, xs, put_rows, chunk, reduce_spec, reduce_shape, name="reduce_near"),
+            *reduce_sum.nears(),
+        )
+
+    def reduce_far():
+        v.reduce_grad = line(
+            lambda given, *xs: spread(at, 1, xs, put_rows, chunk, reduce_spec, reduce_shape, given, name="reduce_far"),
+            v.reduce_grad, *reduce_sum.fars(),
+        )
+
+    def expand_near():
+        v.expand_grad = line(
+            lambda *xs: spread(at, 0, xs, put_rows, turned, expand_spec, expand_shape, name="expand_near"),
+            *expand_sum.nears(),
+        )
+
+    def expand_far():
+        v.expand_grad = line(
+            lambda given, *xs: spread(at, 1, xs, put_rows, turned, expand_spec, expand_shape, given, name="expand_far"),
+            v.expand_grad, *expand_sum.fars(),
+        )
+
+    def heads_near():
+        v.heads_grad = line(
+            lambda *xs: spread(at, 0, xs, put_heads, piece, heads_spec, heads_shape, name="heads_near"),
+            *query_sum.nears(), *value_sum.nears(),
+        )
+
+    def heads_far():
+        v.heads_grad = line(
+            lambda given, *xs: spread(at, 1, xs, put_heads, piece, heads_spec, heads_shape, given, name="heads_far"),
+            v.heads_grad, *query_sum.fars(), *value_sum.fars(),
         )
 
     order = (
@@ -1052,9 +1059,10 @@
         query_chunks, reduce_sum.third, value_chunks, first_other, expand_sum.second, reduce_sum.fourth,
         query_sum.first, value_sum.first, expand_sum.third, reduce_sum.fifth, query_sum.second,
         value_sum.second, first_own, first_back, expand_sum.fourth, pack_first, reduce_sum.sixth, pack_next(2),
-        value_sum.third, expand_sum.fifth, query_sum.third, reduced_other, value_sum.fourth, reduce_spread,
-        query_sum.fourth, expand_sum.sixth, pack_next(4), value_sum.fifth, query_sum.fifth, output,
-        value_sum.sixth, expand_spread, pack_next(8), query_sum.sixth, pack_next(0), heads_spread,
+        value_sum.third, expand_sum.fifth, query_sum.third, reduced_other, value_sum.fourth, reduce_near,
+        reduce_far, query_sum.fourth, pack_next(4), expand_sum.sixth, value_sum.fifth, query_sum.fifth, output,
+        value_sum.sixth, expand_near, expand_far, pack_next(8), query_sum.sixth, heads_near, heads_far,
+        pack_next(0),
     )
     for step in order:
         step()
@@ -1063,8 +1071,8 @@
     expand_bias_grad = pack[5 * model : 5 * model + hidden]
     bias_part = pack[5 * model + hidden :].reshape(relative_bias.shape)
     return (
-        v.block_out, v.tokens_grad, both[0], both[1], v.heads_grad, bias_part, v.mixer_grad, both[2], both[3],
-        v.expand_grad, expand_bias_grad, v.reduce_grad, both[4],
+        v.block_out, v.tokens_grad, both[0], both[1], v.heads_grad[0], bias_part, v.heads_grad[1], both[2], both[3],
+        v.expand_grad[0], expand_bias_grad, v.reduce_grad[0], both[4],
     )
 
 

time: 367 us -> 364 us (level)
  starting transfers between devices: 43.5 us -> 38.6 us
  waiting for transfers between devices: 84 us -> 88.3 us
    pallas_call x2 -> x6, Pallas kernels: 17.2 us -> 30.9 us  [spread(): pl.pallas_call(functools.partial(spread_kernel, put), grid_spec=pltpu.Pre...]
    pallas_call x5 -> x4, Pallas kernels: 32.6 us -> 21.4 us  [the longest x2 11.1 us: project(): pl.pallas_call(project_kernel, grid=(rows // step,), in_specs=[pl.BlockSp...]
    ppermute x37, starting transfers between devices: 34.1 us -> 29.9 us  [trade(): return lax.ppermute(x, 'dp', [(i, i ^ bit) for i in range(size)])]
    convert_element_type x16, other arithmetic: 18.8 us -> 14.9 us  [add_low(): return (a.astype(F32) + b.astype(F32)).astype(BF16)]
  transfers between devices with their start and end apart: 47 -> 47, of which waited for: 18 -> 15; matrix products, arithmetic and copies ran while one was open for 9% -> 8% of each run, Pallas kernels for 46% -> 49%
where the time goes in v1:
time: 364 us; the launch traced here: 359 us
  Pallas kernels  195 us (54%)
  waiting for transfers between devices  88.3 us (24%)
  starting transfers between devices  38.6 us (11%)
  other arithmetic  20.1 us (6%)
  local copies, waits for them, and re-layouts  10.7 us (3%)
  matrix products  4.31 us (1%)
    ppermute x37, waiting for transfers between devices, trade(): return lax.ppermute(x, 'dp', [(i, i ^ bit) for i in range(size)])  54.1 us
    pallas_call x4, Pallas kernels, pair_call(): pl.pallas_call(functools.partial(kernel, slot), grid_spec=pltpu.PrefetchS...  34.8 us
    ppermute x10, waiting for transfers between devices, swap(): return lax.ppermute(x, 'mp', [(0, 1), (1, 0)])  34.2 us
    pallas_call x6, Pallas kernels, spread(): pl.pallas_call(functools.partial(spread_kernel, put), grid_spec=pltpu.Pre...  30.9 us
    ppermute x37, starting transfers between devices, trade(): return lax.ppermute(x, 'dp', [(i, i ^ bit) for i in range(size)])  29.9 us
    pallas_call x2, Pallas kernels, expand(): pl.pallas_call(expand_kernel, grid=(hidden // step,), in_specs=[pl.BlockS...  23.4 us
    pallas_call x1, Pallas kernels, attend_backward(): pl.pallas_call(kernel, grid_spec=pltpu.PrefetchScalarGridSpec(num_scalar_...  22.8 us
    pallas_call x3, Pallas kernels, columns_dot(): pl.pallas_call(functools.partial(columns_kernel, turn), grid=(columns //...  17.9 us
  transfers between devices with their start and end apart: 47, of which 15 were waited for; matrix products, arithmetic and copies ran while one was open for 8% of the time, Pallas kernels for 49%

profile of v1, /device:TPU:25, one launch (start us, length us, event | category | flops | bytes accessed | tf_op | source)
XLA Modules:
  0.0 359.1 jit_solution(11490513550792635969)
XLA Ops:
  0.6 1.3 collective-permute-start
  2.6 2.3 broadcast_select_fusion.1.a_ref.refs_2_.add_ref
  5.0 5.5 %project.2 = (bf16[512,1024]{1,0:T(8,128)(2,1)}, bf16[3,512,512]{2,1,0:T(8,128)(2,1)}) custom-call(bf16[512,1024]{1,0:T(8,128)(2,1)} %source_ref, f32[1,1024]{1,0:T(1,128)} %bitcast.35, f32[1,1024]{1,0:T(1,128)} %bitcast.38, bf16[3,1024,512]{2,1,0:T(8,128)(2,1)} %w_ref.6), custom_call_target="tpu_custom_call" | custom-call | flops 1610612736 | bytes 6815744 | tf_op jit(solution)/shard_map/project/pallas_call | solution.py:291
  10.5 6.3 %active_grad.2.g_ref = bf16[512,2048]{1,0:T(8,128)(2,1)} custom-call(bf16[512,1024]{1,0:T(8,128)(2,1)} %broadcast_select_fusion.1.a_ref.refs_2_.add_ref, bf16[2048,1024]{1,0:T(8,128)(2,1)} %w_ref.7), custom_call_target="tpu_custom_call" | custom-call | flops 34359738368 | bytes 117440512 | tf_op jit(solution)/shard_map/active_grad/pallas_call | solution.py:551
  16.7 1.5 bias_rows.1.b_ref
  18.9 6.2 %collective-permute-done.x_ref.x1_ref = bf16[512,1024]{1,0:T(8,128)(2,1)} collective-permute-done((bf16[512,1024]{1,0:T(8,128)(2,1)}, bf16[512,1024]{1,0:T(8,128)(2,1)}, u32[]{:S(2)}, u32[]{:S(2)}) %collective-permute-start) | collective-permute-done | bytes 1048608 | tf_op jit(solution)/shard_map/ppermute | solution.py:773
  26.5 5.5 %project.3 = (bf16[512,1024]{1,0:T(8,128)(2,1)}, bf16[3,512,512]{2,1,0:T(8,128)(2,1)}) custom-call(bf16[512,1024]{1,0:T(8,128)(2,1)} %collective-permute-done.x_ref.x1_ref, f32[1,1024]{1,0:T(1,128)} %bitcast.36, f32[1,1024]{1,0:T(1,128)} %bitcast.39, bf16[3,1024,512]{2,1,0:T(8,128)(2,1)} %w_ref.6), custom_call_target="tpu_custom_call" | custom-call | flops 1610612736 | bytes 6815744 | tf_op jit(solution)/shard_map/project/pallas_call | solution.py:291
  32.1 14.4 %attend_forward.1 = (bf16[1024,512]{1,0:T(8,128)(2,1)}, f32[4,1024,128]{2,1,0:T(8,128)}) custom-call(s32[2]{0:T(128)} %pad_add_fusion.sp, bf16[3,512,512]{2,1,0:T(8,128)(2,1)} %get-tuple-element.287.a_ref, bf16[3,512,512]{2,1,0:T(8,128)(2,1)} %get-tuple-element.288.c_ref, f32[4,2,2048]{2,1,0:T(2,128)} %bias_rows.1.b_ref), custom_call_target="tpu_custom_call" | custom-call | flops 4294967296 | bytes 6291456 | tf_op jit(solution)/shard_map/attend_forward/pallas_call | solution.py:124
  46.4 2.2 collective-permute-start.3
  49.2 1.3 collective-permute-start.1
  51.3 2.2 order_rows.1.w1_ref
  53.5 5.9 %collective-permute-done.4 = bf16[512,1024]{1,0:T(8,128)(2,1)S(1)} collective-permute-done((bf16[512,1024]{1,0:T(8,128)(2,1)S(1)}, bf16[512,1024]{1,0:T(8,128)(2,1)S(1)}, u32[]{:S(2)}, u32[]{:S(2)}) %collective-permute-start.4) | collective-permute-done | bytes 1048608 | tf_op jit(solution)/shard_map/ppermute | solution.py:773
  60.5 6.1 %active_grad.3.g_ref = bf16[512,2048]{1,0:T(8,128)(2,1)} custom-call(bf16[512,1024]{1,0:T(8,128)(2,1)} %broadcast_select_fusion.a_ref.refs_3_, bf16[2048,1024]{1,0:T(8,128)(2,1)} %w_ref.7), custom_call_target="tpu_custom_call" | custom-call | flops 34359738368 | bytes 117440512 | tf_op jit(solution)/shard_map/active_grad/pallas_call | solution.py:551
  66.6 15.3 %collective-permute-done.1.p_ref = bf16[1024,512]{1,0:T(8,128)(2,1)} collective-permute-done((bf16[1024,512]{1,0:T(8,128)(2,1)}, bf16[1024,512]{1,0:T(8,128)(2,1)}, u32[]{:S(2)}, u32[]{:S(2)}) %collective-permute-start.1) | collective-permute-done | bytes 1048608 | tf_op jit(solution)/shard_map/ppermute | solution.py:773
  82.0 7.8 %mix.1 = (bf16[512,1024]{1,0:T(8,128)(2,1)}, bf16[1024,1024]{1,0:T(8,128)(2,1)}) custom-call(bf16[512,1024]{1,0:T(8,128)(2,1)} %source_ref, bf16[512,1024]{1,0:T(8,128)(2,1)} %collective-permute-done.x_ref.x1_ref, bf16[1024,512]{1,0:T(8,128)(2,1)} %get-tuple-element.311.m_ref.o_ref.refs_5_, bf16[1024,512]{1,0:T(8,128)(2,1)} %collective-permute-done.1.p_ref, ...), custom_call_target="tpu_custom_call" | custom-call | flops 2147483648 | bytes 10485760 | tf_op jit(solution)/shard_map/mix/pallas_call | solution.py:329
  89.8 11.7 %expand.2 = (bf16[512,2048]{1,0:T(8,128)(2,1)}, bf16[512,2048]{1,0:T(8,128)(2,1)}, bf16[512,1024]{1,0:T(8,128)(2,1)}, f32[1,2048]{1,0:T(1,128)}) custom-call(bf16[1024,1024]{1,0:T(8,128)(2,1)} %get-tuple-element.275.x_ref.refs_0_, bf16[512,2048]{1,0:T(8,128)(2,1)} %active_grad.3.g_ref, bf16[1024,2048]{1,0:T(8,128)(2,1)} %w_ref.4, bf16[1,2048]{1,0:T(2,128)(2,1)} %reshape.162.b_ref), custom_call_target="tpu_custom_call" | custom-call | flops 4294967296 | bytes 12582912 | tf_op jit(solution)/shard_map/expand/pallas_call | solution.py:387
  101.5 1.3 collective-permute-start.5
  103.4 11.6 %expand.3 = (bf16[512,2048]{1,0:T(8,128)(2,1)}, bf16[512,2048]{1,0:T(8,128)(2,1)}, bf16[512,1024]{1,0:T(8,128)(2,1)}, f32[1,2048]{1,0:T(1,128)}) custom-call(bf16[1024,1024]{1,0:T(8,128)(2,1)} %get-tuple-element.275.x_ref.refs_0_, bf16[512,2048]{1,0:T(8,128)(2,1)} %active_grad.2.g_ref, bf16[1024,2048]{1,0:T(8,128)(2,1)} %w_ref.4, bf16[1,2048]{1,0:T(2,128)(2,1)} %reshape.162.b_ref), custom_call_target="tpu_custom_call" | custom-call | flops 4294967296 | bytes 12582912 | tf_op jit(solution)/shard_map/expand/pallas_call | solution.py:387
  115.0 9.8 %reduce_grad.1 = (bf16[4,256,1024]{2,1,0:T(8,128)(2,1)}, bf16[4,256,1024]{2,1,0:T(8,128)(2,1)}) custom-call(s32[2]{0:T(128)} %pad_add_fusion.1.s_ref, bf16[512,2048]{1,0:T(8,128)(2,1)} %get-tuple-element.375.refs_0_.a_ref, bf16[512,2048]{1,0:T(8,128)(2,1)} %get-tuple-element.356.refs_1_.a_ref, ...), custom_call_target="tpu_custom_call" | custom-call | flops 4294967296 | bytes 10485760 | tf_op jit(solution)/shard_map/reduce_grad/pallas_call | solution.py:449
  124.9 2.8 collective-permute-start.8
  128.6 5.2 %back_rows.2 = (bf16[512,1024]{1,0:T(8,128)(2,1)}, f32[8,1024]{1,0:T(8,128)}) custom-call(bf16[512,1024]{1,0:T(8,128)(2,1)} %get-tuple-element.266.a_ref, bf16[512,1024]{1,0:T(8,128)(2,1)} %copy-done.8, bf16[512,1024]{1,0:T(8,128)(2,1)} %get-tuple-element.374.source_ref.m_ref, bf16[512,1024]{1,0:T(8,128)(2,1)} %broadcast_select_fusion.1.a_ref.refs_2_.add_ref, ...), custom_call_target="tpu_custom_call" | custom-call | flops 15728640 | bytes 5242880 | tf_op jit(solution)/shard_map/back_rows/pallas_call | solution.py:647
  133.8 2.8 convolution_convert_fusion.1
  136.6 10.0 %expand_grad.1 = (bf16[4,1024,256]{2,1,0:T(8,128)(2,1)}, bf16[4,1024,256]{2,1,0:T(8,128)(2,1)}) custom-call(s32[2]{0:T(128)} %pad_add_fusion.1.s_ref, bf16[1024,1024]{1,0:T(8,128)(2,1)} %get-tuple-element.275.x_ref.refs_0_, bf16[512,2048]{1,0:T(8,128)(2,1)} %get-tuple-element.276.refs_1_, bf16[512,2048]{1,0:T(8,128)(2,1)} %get-tuple-element.277.refs_2_), custom_call_target="tpu_custom_call" | custom-call | flops 4294967296 | bytes 10485760 | tf_op jit(solution)/shard_map/expand_grad/pallas_call | solution.py:449
  148.1 1.5 convolution_convert_fusion.d0_ref
  149.7 3.7 %add_convert_fusion.2 = (bf16[2,256,1024]{2,1,0:T(8,128)(2,1)S(1)}, bf16[2,256,1024]{2,1,0:T(8,128)(2,1)}) fusion(bf16[4,256,1024]{2,1,0:T(8,128)(2,1)} %collective-permute-done.8, bf16[4,256,1024]{2,1,0:T(8,128)(2,1)S(1)} %copy-done.3), kind=kLoop, calls=%fused_computation.2 | loop fusion | flops 4194304 | bytes 6291456 | tf_op jit(solution)/shard_map/convert_element_type | solution.py:428
  154.6 1.6 add_convert_fusion
  156.1 3.9 %collective-permute-done.6.d1_ref = bf16[512,512]{1,0:T(8,128)(2,1)} collective-permute-done((bf16[512,512]{1,0:T(8,128)(2,1)}, bf16[512,512]{1,0:T(8,128)(2,1)}, u32[]{:S(2)}, u32[]{:S(2)}) %collective-permute-start.6) | collective-permute-done | bytes 524320 | tf_op jit(solution)/shard_map/ppermute | solution.py:773
  160.0 22.8 %attend_backward.1 = (bf16[3,1024,512]{2,1,0:T(8,128)(2,1)}, f32[4,4,512]{2,1,0:T(4,128)}) custom-call(s32[2]{0:T(128)} %pad_add_fusion.sp, bf16[3,512,512]{2,1,0:T(8,128)(2,1)} %get-tuple-element.287.a_ref, bf16[3,512,512]{2,1,0:T(8,128)(2,1)} %get-tuple-element.288.c_ref, bf16[512,512]{1,0:T(8,128)(2,1)} %convolution_convert_fusion.d0_ref, ...), custom_call_target="tpu_custom_call" | custom-call | flops 10737418240 | bytes 10485760 | tf_op jit(solution)/shard_map/attend_backward/pallas_call | solution.py:225
  182.8 2.7 add_convert_fusion.14
  185.8 1.3 collective-permute-start.13
  187.1 7.5 %heads_grad.1 = (bf16[4,2,128,512]{3,2,1,0:T(8,128)(2,1)}, bf16[4,2,128,512]{3,2,1,0:T(8,128)(2,1)}) custom-call(s32[2]{0:T(128)} %pad_add_fusion.1.s_ref, bf16[512,1024]{1,0:T(8,128)(2,1)} %get-tuple-element.306.refs_0_, bf16[512,1024]{1,0:T(8,128)(2,1)} %get-tuple-element.307.refs_1_, bf16[3,1024,512]{2,1,0:T(8,128)(2,1)} %get-tuple-element.332.refs_2_.g_ref), custom_call_target="tpu_custom_call" | custom-call | flops 2147483648 | bytes 7340032 | tf_op jit(solution)/shard_map/heads_grad/pallas_call | solution.py:449
  194.8 2.7 collective-permute-start.10
  200.0 7.6 %values_grad.1 = (bf16[4,2,128,512]{3,2,1,0:T(8,128)(2,1)}, bf16[4,2,128,512]{3,2,1,0:T(8,128)(2,1)}) custom-call(s32[2]{0:T(128)} %pad_add_fusion.1.s_ref, bf16[512,1024]{1,0:T(8,128)(2,1)} %get-tuple-element.306.refs_0_, bf16[512,1024]{1,0:T(8,128)(2,1)} %get-tuple-element.307.refs_1_, bf16[3,1024,512]{2,1,0:T(8,128)(2,1)} %get-tuple-element.332.refs_2_.g_ref, ...), custom_call_target="tpu_custom_call" | custom-call | flops 2147483648 | bytes 10485760 | tf_op jit(solution)/shard_map/values_grad/pallas_call | solution.py:449
  207.6 2.5 collective-permute-start.18
  210.3 5.6 %first_rows.2 = bf16[512,1024]{1,0:T(8,128)(2,1)} custom-call(bf16[3,1024,512]{2,1,0:T(8,128)(2,1)} %get-tuple-element.332.refs_2_.g_ref, bf16[3,1024,512]{2,1,0:T(8,128)(2,1)} %w_ref.6), custom_call_target="tpu_custom_call" | custom-call | flops 1610612736 | bytes 8388608 | tf_op jit(solution)/shard_map/first_rows/pallas_call | solution.py:606
  215.9 1.3 collective-permute-start.22
  217.3 1.5 add_convert_fusion.11
  219.0 6.0 %collective-permute-done.12 = bf16[1,256,1024]{2,1,0:T(8,128)(2,1)S(1)} collective-permute-done((bf16[1,256,1024]{2,1,0:T(8,128)(2,1)S(1)}, bf16[1,256,1024]{2,1,0:T(8,128)(2,1)S(1)}, u32[]{:S(2)}, u32[]{:S(2)}) %collective-permute-start.12) | collective-permute-done | bytes 524320 | tf_op jit(solution)/shard_map/ppermute | solution.py:424
  225.2 1.5 add_convert_fusion.8
  228.7 8.6 %collective-permute-done.17 = bf16[1,1024,256]{2,1,0:T(8,128)(2,1)S(1)} collective-permute-done((bf16[1,1024,256]{2,1,0:T(8,128)(2,1)S(1)}, bf16[1,1024,256]{2,1,0:T(8,128)(2,1)S(1)}, u32[]{:S(2)}, u32[]{:S(2)}) %collective-permute-start.17) | collective-permute-done | bytes 524320 | tf_op jit(solution)/shard_map/ppermute | solution.py:424
  237.5 15.8 %collective-permute-done.16 = bf16[1,256,1024]{2,1,0:T(8,128)(2,1)S(1)} collective-permute-done((bf16[1,256,1024]{2,1,0:T(8,128)(2,1)S(1)}, bf16[1,256,1024]{2,1,0:T(8,128)(2,1)S(1)}, u32[]{:S(2)}, u32[]{:S(2)}) %collective-permute-start.16) | collective-permute-done | bytes 524320 | tf_op jit(solution)/shard_map/ppermute | solution.py:424
  253.5 1.3 collective-permute-start.31
  256.4 5.6 %first_rows.3.a_ref = bf16[512,1024]{1,0:T(8,128)(2,1)} custom-call(bf16[3,1024,512]{2,1,0:T(8,128)(2,1)} %get-tuple-element.332.refs_2_.g_ref, bf16[3,1024,512]{2,1,0:T(8,128)(2,1)} %w_ref.6), custom_call_target="tpu_custom_call" | custom-call | flops 1610612736 | bytes 8388608 | tf_op jit(solution)/shard_map/first_rows/pallas_call | solution.py:606
  262.1 5.2 %back_rows.3 = (bf16[512,1024]{1,0:T(8,128)(2,1)}, f32[8,1024]{1,0:T(8,128)}) custom-call(bf16[512,1024]{1,0:T(8,128)(2,1)} %first_rows.3.a_ref, bf16[512,1024]{1,0:T(8,128)(2,1)} %collective-permute-done.22.b_ref, bf16[512,1024]{1,0:T(8,128)(2,1)} %source_ref, bf16[512,1024]{1,0:T(8,128)(2,1)} %get-tuple-element.337.refs_3_.add_ref, f32[1,1024]{1,0:T(1,128)} %bitcast.37), custom_call_target="tpu_custom_call" | custom-call | flops 15728640 | bytes 5242880 | tf_op jit(solution)/shard_map/back_rows/pallas_call | solution.py:647
  268.1 1.5 collective-permute-start.23
  270.0 2.9 collective-permute-done.25
  273.0 2.1 collective-permute-start.26
  276.5 1.4 collective-permute-done.31.refs_1_
  277.9 1.3 collective-permute-start.32
  279.2 7.4 %collective-permute-done.23 = bf16[1,1024,256]{2,1,0:T(8,128)(2,1)} collective-permute-done((bf16[1,1024,256]{2,1,0:T(8,128)(2,1)S(1)}, bf16[1,1024,256]{2,1,0:T(8,128)(2,1)}, u32[]{:S(2)}, u32[]{:S(2)}) %collective-permute-start.23) | collective-permute-done | bytes 524320 | tf_op jit(solution)/shard_map/ppermute | solution.py:424
  288.1 4.0 %collective-permute-done.19 = bf16[1,2,128,512]{3,2,1,0:T(8,128)(2,1)S(1)} collective-permute-done((bf16[1,2,128,512]{3,2,1,0:T(8,128)(2,1)}, bf16[1,2,128,512]{3,2,1,0:T(8,128)(2,1)S(1)}, u32[]{:S(2)}, u32[]{:S(2)}) %collective-permute-start.19) | collective-permute-done | bytes 262176 | tf_op jit(solution)/shard_map/ppermute | solution.py:424
  292.2 5.5 %reduced.1 = bf16[512,1024]{1,0:T(8,128)(2,1)} custom-call(bf16[512,2048]{1,0:T(8,128)(2,1)} %get-tuple-element.356.refs_1_.a_ref, bf16[2048,1024]{1,0:T(8,128)(2,1)} %w_ref.7), custom_call_target="tpu_custom_call" | custom-call | flops 34359738368 | bytes 117440512 | tf_op jit(solution)/shard_map/reduced/pallas_call | solution.py:551
  298.3 5.2 %reduce_near.1.refs_0_ = f32[2048,1024]{1,0:T(8,128)} custom-call(s32[2]{0:T(128)} %pad_add_fusion.1.s_ref, bf16[2,256,1024]{2,1,0:T(8,128)(2,1)} %copy-done.1, bf16[2,256,1024]{2,1,0:T(8,128)(2,1)} %collective-permute-done.29.refs_1_), custom_call_target="tpu_custom_call" | custom-call | bytes 6291456 | tf_op jit(solution)/shard_map/reduce_near/pallas_call | solution.py:708
  304.7 5.2 %reduce_far.1 = f32[2048,1024]{1,0:T(8,128)} custom-call(s32[2]{0:T(128)} %pad_add_fusion.1.s_ref, f32[2048,1024]{1,0:T(8,128)} %reduce_near.1.refs_0_, bf16[2,256,1024]{2,1,0:T(8,128)(2,1)} %collective-permute-done.31.refs_1_, bf16[2,256,1024]{2,1,0:T(8,128)(2,1)} %collective-permute-done.32.refs_2_), custom_call_target="tpu_custom_call", output_to_operand_aliasing={{}: (1, {})} | custom-call | bytes 6291456 | tf_op jit(solution)/shard_map/reduce_far/pallas_call | solution.py:708
  309.9 2.0 collective-permute-done.28
  312.1 2.1 collective-permute-start.37
  314.1 3.0 collective-permute-done.34
  317.9 4.9 %collective-permute-done.33 = bf16[1,2,128,512]{3,2,1,0:T(8,128)(2,1)S(1)} collective-permute-done((bf16[1,2,128,512]{3,2,1,0:T(8,128)(2,1)S(1)}, bf16[1,2,128,512]{3,2,1,0:T(8,128)(2,1)S(1)}, u32[]{:S(2)}, u32[]{:S(2)}) %collective-permute-start.33) | collective-permute-done | bytes 262176 | tf_op jit(solution)/shard_map/ppermute | solution.py:424
  323.9 6.9 %output.1 = bf16[512,1024]{1,0:T(8,128)(2,1)} custom-call(bf16[512,1024]{1,0:T(8,128)(2,1)} %get-tuple-element.374.source_ref.m_ref, bf16[512,2048]{1,0:T(8,128)(2,1)} %get-tuple-element.375.refs_0_.a_ref, bf16[2048,1024]{1,0:T(8,128)(2,1)} %w_ref.7, bf16[512,1024]{1,0:T(8,128)(2,1)} %collective-permute-done.27.r_ref, f32[1,1024]{1,0:T(1,128)} %bitcast.41), custom_call_target="tpu_custom_call" | custom-call | flops 34359738368 | bytes 167772160 | tf_op jit(solution)/shard_map/output/pallas_call | solution.py:573
  331.3 5.2 %expand_near.1.refs_0_ = f32[1024,2048]{1,0:T(8,128)} custom-call(s32[2]{0:T(128)} %pad_add_fusion.1.s_ref, bf16[2,1024,256]{2,1,0:T(8,128)(2,1)} %copy-done.2, bf16[2,1024,256]{2,1,0:T(8,128)(2,1)} %collective-permute-done.37.refs_1_), custom_call_target="tpu_custom_call" | custom-call | bytes 6291456 | tf_op jit(solution)/shard_map/expand_near/pallas_call | solution.py:708
  337.7 5.2 %expand_far.1 = f32[1024,2048]{1,0:T(8,128)} custom-call(s32[2]{0:T(128)} %pad_add_fusion.1.s_ref, f32[1024,2048]{1,0:T(8,128)} %expand_near.1.refs_0_, bf16[2,1024,256]{2,1,0:T(8,128)(2,1)} %collective-permute-done.38.refs_1_, bf16[2,1024,256]{2,1,0:T(8,128)(2,1)} %copy-done.13), custom_call_target="tpu_custom_call", output_to_operand_aliasing={{}: (1, {})} | custom-call | bytes 6291456 | tf_op jit(solution)/shard_map/expand_far/pallas_call | solution.py:708
  343.2 1.3 collective-permute-start.40
  346.1 5.1 %heads_near.1 = (f32[3,1024,512]{2,1,0:T(8,128)}, f32[512,1024]{1,0:T(8,128)}) custom-call(s32[2]{0:T(128)} %pad_add_fusion.1.s_ref, bf16[2,2,128,512]{3,2,1,0:T(8,128)(2,1)} %copy-done.7, bf16[2,2,128,512]{3,2,1,0:T(8,128)(2,1)} %copy-done.15, bf16[2,2,128,512]{3,2,1,0:T(8,128)(2,1)} %copy-done.6, bf16[2,2,128,512]{3,2,1,0:T(8,128)(2,1)} %copy-done.14), custom_call_target="tpu_custom_call" | custom-call | bytes 6291456 | tf_op jit(solution)/shard_map/heads_near/pallas_call | solution.py:708
  352.1 5.1 %heads_far.1 = (f32[3,1024,512]{2,1,0:T(8,128)}, f32[512,1024]{1,0:T(8,128)}) custom-call(s32[2]{0:T(128)} %pad_add_fusion.1.s_ref, f32[3,1024,512]{2,1,0:T(8,128)} %get-tuple-element.395.refs_0_, f32[512,1024]{1,0:T(8,128)} %get-tuple-element.396.refs_1_, ...), custom_call_target="tpu_custom_call", output_to_operand_aliasing={{0}: (1, {}), {1}: (2, {})} | custom-call | bytes 6291456 | tf_op jit(solution)/shard_map/heads_far/pallas_call | solution.py:708
  (174 shorter events, 30.9 us)
Async XLA Ops:
  0.6 24.4 %collective-permute-start = (bf16[512,1024]{1,0:T(8,128)(2,1)}, bf16[512,1024]{1,0:T(8,128)(2,1)}, u32[]{:S(2)}, u32[]{:S(2)}) collective-permute-start(bf16[512,1024]{1,0:T(8,128)(2,1)} %source_ref), channel_id=1, source_target_pairs={{0,1},{1,0},{2,3},{3,2},{4,5},{5,4},{6,7},{7,6},{8,9},{9,8},{10,11... | collective-permute-start | bytes 3145736 | tf_op jit(solution)/shard_map/ppermute | solution.py:773
  10.5 8.3 %copy-start.20 = (bf16[512,1024]{1,0:T(8,128)(2,1)S(1)}, bf16[512,1024]{1,0:T(8,128)(2,1)}, u32[]{:S(2)}) copy-start(bf16[512,1024]{1,0:T(8,128)(2,1)} %w0_ref) | copy-start | bytes 3145732
  10.5 15.8 %copy-start.11 = (bf16[512,1024]{1,0:T(8,128)(2,1)S(1)}, bf16[512,1024]{1,0:T(8,128)(2,1)}, u32[]{:S(2)}) copy-start(bf16[512,1024]{1,0:T(8,128)(2,1)} %param.29) | copy-start | bytes 3145732
  25.1 21.4 %collective-permute-start.2 = (bf16[256,1024]{1,0:T(8,128)(2,1)S(1)}, bf16[256,1024]{1,0:T(8,128)(2,1)S(1)}, u32[]{:S(2)}, u32[]{:S(2)}) collective-permute-start(bf16[256,1024]{1,0:T(8,128)(2,1)S(1)} %constant_dynamic-slice_fusion), channel_id=1, source_target_pairs={{0,1},{1,0},{2,3},{3,2},{4,5},{5,4},{6,7},{7,6},{8,9},{9,8},{10,11... | collective-permute-start | bytes 1572872 | tf_op jit(solution)/shard_map/ppermute | solution.py:773
  26.3 33.1 %collective-permute-start.4 = (bf16[512,1024]{1,0:T(8,128)(2,1)S(1)}, bf16[512,1024]{1,0:T(8,128)(2,1)S(1)}, u32[]{:S(2)}, u32[]{:S(2)}) collective-permute-start(bf16[512,1024]{1,0:T(8,128)(2,1)S(1)} %copy-done.11), channel_id=1, source_target_pairs={{0,1},{1,0},{2,3},{3,2},{4,5},{5,4},{6,7},{7,6},{8,9},{9,8},{10,11... | collective-permute-start | bytes 3145736 | tf_op jit(solution)/shard_map/ppermute | solution.py:773
  32.1 16.6 %copy-start.26 = (bf16[2048]{0:T(1024)(128)(2,1)S(1)}, bf16[2048]{0:T(1024)(128)(2,1)}, u32[]{:S(2)}) copy-start(bf16[2048]{0:T(1024)(128)(2,1)} %param.26) | copy-start | bytes 12292
  46.4 4.1 %copy-start.17 = (bf16[256,1024]{1,0:T(8,128)(2,1)}, bf16[256,1024]{1,0:T(8,128)(2,1)S(1)}, u32[]{:S(2)}) copy-start(bf16[256,1024]{1,0:T(8,128)(2,1)S(1)} %collective-permute-done.2.a_ref) | copy-start | bytes 1572868
  46.4 4.0 %collective-permute-start.3 = (bf16[256,1024]{1,0:T(8,128)(2,1)S(1)}, bf16[256,1024]{1,0:T(8,128)(2,1)S(1)}, u32[]{:S(2)}, u32[]{:S(2)}) collective-permute-start(bf16[256,1024]{1,0:T(8,128)(2,1)S(1)} %collective-permute-done.2.a_ref), channel_id=1, source_target_pairs={{0,2},{2,0},{4,6},{6,4},{8,10},{10,8},{12,14},{14,12},{16,18},{18,... | collective-permute-start | bytes 1572872 | tf_op jit(solution)/shard_map/ppermute | solution.py:424
  49.2 32.7 %collective-permute-start.1 = (bf16[1024,512]{1,0:T(8,128)(2,1)}, bf16[1024,512]{1,0:T(8,128)(2,1)}, u32[]{:S(2)}, u32[]{:S(2)}) collective-permute-start(bf16[1024,512]{1,0:T(8,128)(2,1)} %get-tuple-element.311.m_ref.o_ref.refs_5_), channel_id=1, source_target_pairs={{0,1},{1,0},{2,3},{3,2},{4,5},{5,4},{6,7},{7,6},{8,9},{9,8},{10,11... | collective-permute-start | bytes 3145736 | tf_op jit(solution)/shard_map/ppermute | solution.py:773
  101.5 26.1 %collective-permute-start.5 = (bf16[512,1024]{1,0:T(8,128)(2,1)}, bf16[512,1024]{1,0:T(8,128)(2,1)S(1)}, u32[]{:S(2)}, u32[]{:S(2)}) collective-permute-start(bf16[512,1024]{1,0:T(8,128)(2,1)} %get-tuple-element.250), channel_id=1, source_target_pairs={{0,1},{1,0},{2,3},{3,2},{4,5},{5,4},{6,7},{7,6},{8,9},{9,8},{10,11... | collective-permute-start | bytes 3145736 | tf_op jit(solution)/shard_map/ppermute | solution.py:773
  124.9 24.8 %collective-permute-start.8 = (bf16[4,256,1024]{2,1,0:T(8,128)(2,1)}, bf16[4,256,1024]{2,1,0:T(8,128)(2,1)}, u32[]{:S(2)}, u32[]{:S(2)}) collective-permute-start(bf16[4,256,1024]{2,1,0:T(8,128)(2,1)} %get-tuple-element.264), channel_id=1, source_target_pairs={{0,2},{2,0},{4,6},{6,4},{8,10},{10,8},{12,14},{14,12},{16,18},{18,... | collective-permute-start | bytes 6291464 | tf_op jit(solution)/shard_map/ppermute | solution.py:424
  128.6 5.2 %copy-start.12 = (bf16[512,1024]{1,0:T(8,128)(2,1)S(1)}, bf16[512,1024]{1,0:T(8,128)(2,1)}, u32[]{:S(2)}) copy-start(bf16[512,1024]{1,0:T(8,128)(2,1)} %order_rows.1.w1_ref) | copy-start | bytes 3145732
  136.6 10.9 %copy-start = (bf16[512,1024]{1,0:T(8,128)(2,1)S(1)}, bf16[512,1024]{1,0:T(8,128)(2,1)}, u32[]{:S(2)}) copy-start(bf16[512,1024]{1,0:T(8,128)(2,1)} %get-tuple-element.337.refs_3_.add_ref) | copy-start | bytes 3145732
  136.6 11.5 %copy-start.21 = (bf16[512,1024]{1,0:T(8,128)(2,1)S(1)}, bf16[512,1024]{1,0:T(8,128)(2,1)}, u32[]{:S(2)}) copy-start(bf16[512,1024]{1,0:T(8,128)(2,1)} %w0_ref) | copy-start | bytes 3145732
  146.6 3.1 copy-start.3
  146.6 8.0 %collective-permute-start.7 = (bf16[4,1024,256]{2,1,0:T(8,128)(2,1)}, bf16[4,1024,256]{2,1,0:T(8,128)(2,1)S(1)}, u32[]{:S(2)}, u32[]{:S(2)}) collective-permute-start(bf16[4,1024,256]{2,1,0:T(8,128)(2,1)} %get-tuple-element.278), channel_id=1, source_target_pairs={{0,2},{2,0},{4,6},{6,4},{8,10},{10,8},{12,14},{14,12},{16,18},{18,... | collective-permute-start | bytes 6291464 | tf_op jit(solution)/shard_map/ppermute | solution.py:424
  146.6 13.4 %collective-permute-start.6 = (bf16[512,512]{1,0:T(8,128)(2,1)}, bf16[512,512]{1,0:T(8,128)(2,1)}, u32[]{:S(2)}, u32[]{:S(2)}) collective-permute-start(bf16[512,512]{1,0:T(8,128)(2,1)} %convolution_convert_fusion.1), channel_id=1, source_target_pairs={{0,1},{1,0},{2,3},{3,2},{4,5},{5,4},{6,7},{7,6},{8,9},{9,8},{10,11... | collective-permute-start | bytes 1572872 | tf_op jit(solution)/shard_map/ppermute | solution.py:773
  147.6 52.5 %collective-permute-start.14 = (bf16[512,1024]{1,0:T(8,128)(2,1)S(1)}, bf16[512,1024]{1,0:T(8,128)(2,1)}, u32[]{:S(2)}, u32[]{:S(2)}) collective-permute-start(bf16[512,1024]{1,0:T(8,128)(2,1)S(1)} %copy-done), channel_id=1, source_target_pairs={{0,1},{1,0},{2,3},{3,2},{4,5},{5,4},{6,7},{7,6},{8,9},{9,8},{10,11... | collective-permute-start | bytes 3145736 | tf_op jit(solution)/shard_map/ppermute | solution.py:773
  149.7 4.9 %copy-start.4 = (bf16[4,1024,256]{2,1,0:T(8,128)(2,1)S(1)}, bf16[4,1024,256]{2,1,0:T(8,128)(2,1)}, u32[]{:S(2)}) copy-start(bf16[4,1024,256]{2,1,0:T(8,128)(2,1)} %get-tuple-element.284) | copy-start | bytes 6291460
  153.4 29.5 %collective-permute-start.9 = (bf16[2,256,1024]{2,1,0:T(8,128)(2,1)}, bf16[2,256,1024]{2,1,0:T(8,128)(2,1)}, u32[]{:S(2)}, u32[]{:S(2)}) collective-permute-start(bf16[2,256,1024]{2,1,0:T(8,128)(2,1)} %get-tuple-element.410), channel_id=1, source_target_pairs={{0,4},{2,6},{4,0},{6,2},{8,12},{10,14},{12,8},{14,10},{16,20},{18,... | collective-permute-start | bytes 3145736 | tf_op jit(solution)/shard_map/ppermute | solution.py:424
  185.5 12.3 %collective-permute-start.11 = (bf16[1,256,1024]{2,1,0:T(8,128)(2,1)}, bf16[1,256,1024]{2,1,0:T(8,128)(2,1)S(1)}, u32[]{:S(2)}, u32[]{:S(2)}) collective-permute-start(bf16[1,256,1024]{2,1,0:T(8,128)(2,1)} %get-tuple-element.418), channel_id=1, source_target_pairs={{0,8},{2,10},{4,12},{6,14},{8,0},{10,2},{12,4},{14,6},{16,24},{18,... | collective-permute-start | bytes 1572872 | tf_op jit(solution)/shard_map/ppermute | solution.py:424
  185.8 31.4 %collective-permute-start.13 = (bf16[2,1024,256]{2,1,0:T(8,128)(2,1)}, bf16[2,1024,256]{2,1,0:T(8,128)(2,1)}, u32[]{:S(2)}, u32[]{:S(2)}) collective-permute-start(bf16[2,1024,256]{2,1,0:T(8,128)(2,1)} %get-tuple-element.408), channel_id=1, source_target_pairs={{0,4},{2,6},{4,0},{6,2},{8,12},{10,14},{12,8},{14,10},{16,20},{18,... | collective-permute-start | bytes 3145736 | tf_op jit(solution)/shard_map/ppermute | solution.py:424
  187.1 11.5 %copy-start.5 = (bf16[1,256,1024]{2,1,0:T(8,128)(2,1)S(1)}, bf16[1,256,1024]{2,1,0:T(8,128)(2,1)}, u32[]{:S(2)}) copy-start(bf16[1,256,1024]{2,1,0:T(8,128)(2,1)} %get-tuple-element.303) | copy-start | bytes 1572868
  194.8 30.4 %collective-permute-start.10 = (bf16[4,2,128,512]{3,2,1,0:T(8,128)(2,1)}, bf16[4,2,128,512]{3,2,1,0:T(8,128)(2,1)}, u32[]{:S(2)}, u32[]{:S(2)}) collective-permute-start(bf16[4,2,128,512]{3,2,1,0:T(8,128)(2,1)} %get-tuple-element.302), channel_id=1, source_target_pairs={{0,2},{2,0},{4,6},{6,4},{8,10},{10,8},{12,14},{14,12},{16,18},{18,... | collective-permute-start | bytes 3145736 | tf_op jit(solution)/shard_map/ppermute | solution.py:424
  199.9 25.0 %collective-permute-start.12 = (bf16[1,256,1024]{2,1,0:T(8,128)(2,1)S(1)}, bf16[1,256,1024]{2,1,0:T(8,128)(2,1)S(1)}, u32[]{:S(2)}, u32[]{:S(2)}) collective-permute-start(bf16[1,256,1024]{2,1,0:T(8,128)(2,1)S(1)} %add_convert_fusion.13), channel_id=1, source_target_pairs={{0,16},{2,18},{4,20},{6,22},{8,24},{10,26},{12,28},{14,30},{16,0},... | collective-permute-start | bytes 1572872 | tf_op jit(solution)/shard_map/ppermute | solution.py:424
  207.6 20.0 %collective-permute-start.18 = (bf16[4,2,128,512]{3,2,1,0:T(8,128)(2,1)}, bf16[4,2,128,512]{3,2,1,0:T(8,128)(2,1)S(1)}, u32[]{:S(2)}, u32[]{:S(2)}) collective-permute-start(bf16[4,2,128,512]{3,2,1,0:T(8,128)(2,1)} %get-tuple-element.312), channel_id=1, source_target_pairs={{0,2},{2,0},{4,6},{6,4},{8,10},{10,8},{12,14},{14,12},{16,18},{18,... | collective-permute-start | bytes 3145736 | tf_op jit(solution)/shard_map/ppermute | solution.py:424
  215.9 9.3 %copy-start.9 = (bf16[4,2,128,512]{3,2,1,0:T(8,128)(2,1)S(1)}, bf16[4,2,128,512]{3,2,1,0:T(8,128)(2,1)}, u32[]{:S(2)}) copy-start(bf16[4,2,128,512]{3,2,1,0:T(8,128)(2,1)} %get-tuple-element.320) | copy-start | bytes 3145732
  215.9 46.1 %collective-permute-start.22 = (bf16[512,1024]{1,0:T(8,128)(2,1)}, bf16[512,1024]{1,0:T(8,128)(2,1)}, u32[]{:S(2)}, u32[]{:S(2)}) collective-permute-start(bf16[512,1024]{1,0:T(8,128)(2,1)} %first_rows.2), channel_id=1, source_target_pairs={{0,1},{1,0},{2,3},{3,2},{4,5},{5,4},{6,7},{7,6},{8,9},{9,8},{10,11... | collective-permute-start | bytes 3145736 | tf_op jit(solution)/shard_map/ppermute | solution.py:773
  218.7 18.6 %collective-permute-start.17 = (bf16[1,1024,256]{2,1,0:T(8,128)(2,1)S(1)}, bf16[1,1024,256]{2,1,0:T(8,128)(2,1)S(1)}, u32[]{:S(2)}, u32[]{:S(2)}) collective-permute-start(bf16[1,1024,256]{2,1,0:T(8,128)(2,1)S(1)} %get-tuple-element.416), channel_id=1, source_target_pairs={{0,8},{2,10},{4,12},{6,14},{8,0},{10,2},{12,4},{14,6},{16,24},{18,... | collective-permute-start | bytes 1572872 | tf_op jit(solution)/shard_map/ppermute | solution.py:424
  225.1 28.3 %collective-permute-start.16 = (bf16[1,256,1024]{2,1,0:T(8,128)(2,1)S(1)}, bf16[1,256,1024]{2,1,0:T(8,128)(2,1)S(1)}, u32[]{:S(2)}, u32[]{:S(2)}) collective-permute-start(bf16[1,256,1024]{2,1,0:T(8,128)(2,1)S(1)} %add_convert_fusion.10), channel_id=1, source_target_pairs={{0,8},{2,10},{4,12},{6,14},{8,0},{10,2},{12,4},{14,6},{16,24},{18,... | collective-permute-start | bytes 1572872 | tf_op jit(solution)/shard_map/ppermute | solution.py:424
  226.8 28.0 %collective-permute-start.15 = (bf16[2,2,128,512]{3,2,1,0:T(8,128)(2,1)S(1)}, bf16[2,2,128,512]{3,2,1,0:T(8,128)(2,1)S(1)}, u32[]{:S(2)}, u32[]{:S(2)}) collective-permute-start(bf16[2,2,128,512]{3,2,1,0:T(8,128)(2,1)S(1)} %get-tuple-element.413), channel_id=1, source_target_pairs={{0,4},{2,6},{4,0},{6,2},{8,12},{10,14},{12,8},{14,10},{16,20},{18,... | collective-permute-start | bytes 1572872 | tf_op jit(solution)/shard_map/ppermute | solution.py:424
  227.9 27.7 %collective-permute-start.21 = (bf16[2,2,128,512]{3,2,1,0:T(8,128)(2,1)S(1)}, bf16[2,2,128,512]{3,2,1,0:T(8,128)(2,1)S(1)}, u32[]{:S(2)}, u32[]{:S(2)}) collective-permute-start(bf16[2,2,128,512]{3,2,1,0:T(8,128)(2,1)S(1)} %get-tuple-element.412), channel_id=1, source_target_pairs={{0,4},{2,6},{4,0},{6,2},{8,12},{10,14},{12,8},{14,10},{16,20},{18,... | collective-permute-start | bytes 1572872 | tf_op jit(solution)/shard_map/ppermute | solution.py:424
  237.5 30.5 %collective-permute-start.20 = (bf16[1,1024,256]{2,1,0:T(8,128)(2,1)S(1)}, bf16[1,1024,256]{2,1,0:T(8,128)(2,1)S(1)}, u32[]{:S(2)}, u32[]{:S(2)}) collective-permute-start(bf16[1,1024,256]{2,1,0:T(8,128)(2,1)S(1)} %add_convert_fusion.5), channel_id=1, source_target_pairs={{0,16},{2,18},{4,20},{6,22},{8,24},{10,26},{12,28},{14,30},{16,0},... | collective-permute-start | bytes 1572872 | tf_op jit(solution)/shard_map/ppermute | solution.py:424
  253.5 22.6 %copy-start.1 = (bf16[2,256,1024]{2,1,0:T(8,128)(2,1)}, bf16[2,256,1024]{2,1,0:T(8,128)(2,1)S(1)}, u32[]{:S(2)}) copy-start(bf16[2,256,1024]{2,1,0:T(8,128)(2,1)S(1)} %constant_dynamic-update-slice_fusion.refs_0_) | copy-start | bytes 3145732
  253.5 24.4 %collective-permute-start.31 = (bf16[2,256,1024]{2,1,0:T(8,128)(2,1)S(1)}, bf16[2,256,1024]{2,1,0:T(8,128)(2,1)}, u32[]{:S(2)}, u32[]{:S(2)}) collective-permute-start(bf16[2,256,1024]{2,1,0:T(8,128)(2,1)S(1)} %constant_dynamic-update-slice_fusion.refs_0_), channel_id=1, source_target_pairs={{0,4},{2,6},{4,0},{6,2},{8,12},{10,14},{12,8},{14,10},{16,20},{18,... | collective-permute-start | bytes 3145736 | tf_op jit(solution)/shard_map/ppermute | solution.py:424
  256.4 19.9 %collective-permute-start.24 = (bf16[1,2,128,512]{3,2,1,0:T(8,128)(2,1)}, bf16[1,2,128,512]{3,2,1,0:T(8,128)(2,1)S(1)}, u32[]{:S(2)}, u32[]{:S(2)}) collective-permute-start(bf16[1,2,128,512]{3,2,1,0:T(8,128)(2,1)} %get-tuple-element.420), channel_id=1, source_target_pairs={{0,8},{2,10},{4,12},{6,14},{8,0},{10,2},{12,4},{14,6},{16,24},{18,... | collective-permute-start | bytes 786440 | tf_op jit(solution)/shard_map/ppermute | solution.py:424
  262.0 10.9 %copy-start.23 = (f32[1,2048]{1,0:T(1,128)S(1)}, f32[1,2048]{1,0:T(1,128)}, u32[]{:S(2)}) copy-start(f32[1,2048]{1,0:T(1,128)} %get-tuple-element.346) | copy-start | bytes 24580
  262.1 10.9 %copy-start.24 = (f32[1,2048]{1,0:T(1,128)S(1)}, f32[1,2048]{1,0:T(1,128)}, u32[]{:S(2)}) copy-start(f32[1,2048]{1,0:T(1,128)} %get-tuple-element.345) | copy-start | bytes 24580
  268.1 18.5 %collective-permute-start.23 = (bf16[1,1024,256]{2,1,0:T(8,128)(2,1)S(1)}, bf16[1,1024,256]{2,1,0:T(8,128)(2,1)}, u32[]{:S(2)}, u32[]{:S(2)}) collective-permute-start(bf16[1,1024,256]{2,1,0:T(8,128)(2,1)S(1)} %add_convert_fusion.4), channel_id=1, source_target_pairs={{0,8},{2,10},{4,12},{6,14},{8,0},{10,2},{12,4},{14,6},{16,24},{18,... | collective-permute-start | bytes 1572872 | tf_op jit(solution)/shard_map/ppermute | solution.py:424
  269.7 3.2 collective-permute-start.25
  273.0 3.0 collective-permute-start.26
  275.2 17.0 %collective-permute-start.19 = (bf16[1,2,128,512]{3,2,1,0:T(8,128)(2,1)}, bf16[1,2,128,512]{3,2,1,0:T(8,128)(2,1)S(1)}, u32[]{:S(2)}, u32[]{:S(2)}) collective-permute-start(bf16[1,2,128,512]{3,2,1,0:T(8,128)(2,1)} %get-tuple-element.421), channel_id=1, source_target_pairs={{0,8},{2,10},{4,12},{6,14},{8,0},{10,2},{12,4},{14,6},{16,24},{18,... | collective-permute-start | bytes 786440 | tf_op jit(solution)/shard_map/ppermute | solution.py:424
  276.0 22.1 %collective-permute-start.29 = (bf16[2,256,1024]{2,1,0:T(8,128)(2,1)S(1)}, bf16[2,256,1024]{2,1,0:T(8,128)(2,1)}, u32[]{:S(2)}, u32[]{:S(2)}) collective-permute-start(bf16[2,256,1024]{2,1,0:T(8,128)(2,1)S(1)} %constant_dynamic-update-slice_fusion.refs_0_), channel_id=1, source_target_pairs={{0,2},{2,0},{4,6},{6,4},{8,10},{10,8},{12,14},{14,12},{16,18},{18,... | collective-permute-start | bytes 3145736 | tf_op jit(solution)/shard_map/ppermute | solution.py:424
  276.4 21.6 %collective-permute-start.30 = (bf16[1,2,128,512]{3,2,1,0:T(8,128)(2,1)S(1)}, bf16[1,2,128,512]{3,2,1,0:T(8,128)(2,1)S(1)}, u32[]{:S(2)}, u32[]{:S(2)}) collective-permute-start(bf16[1,2,128,512]{3,2,1,0:T(8,128)(2,1)S(1)} %add_convert_fusion.19), channel_id=1, source_target_pairs={{0,16},{2,18},{4,20},{6,22},{8,24},{10,26},{12,28},{14,30},{16,0},... | collective-permute-start | bytes 786440 | tf_op jit(solution)/shard_map/ppermute | solution.py:424
  277.9 25.6 %collective-permute-start.32 = (bf16[2,256,1024]{2,1,0:T(8,128)(2,1)}, bf16[2,256,1024]{2,1,0:T(8,128)(2,1)}, u32[]{:S(2)}, u32[]{:S(2)}) collective-permute-start(bf16[2,256,1024]{2,1,0:T(8,128)(2,1)} %collective-permute-done.31.refs_1_), channel_id=1, source_target_pairs={{0,2},{2,0},{4,6},{6,4},{8,10},{10,8},{12,14},{14,12},{16,18},{18,... | collective-permute-start | bytes 3145736 | tf_op jit(solution)/shard_map/ppermute | solution.py:424
  287.7 24.3 %copy-start.2 = (bf16[2,1024,256]{2,1,0:T(8,128)(2,1)}, bf16[2,1024,256]{2,1,0:T(8,128)(2,1)S(1)}, u32[]{:S(2)}) copy-start(bf16[2,1024,256]{2,1,0:T(8,128)(2,1)S(1)} %constant_dynamic-update-slice_fusion.2.refs_0_) | copy-start | bytes 3145732
  287.8 29.4 %collective-permute-start.38 = (bf16[2,1024,256]{2,1,0:T(8,128)(2,1)S(1)}, bf16[2,1024,256]{2,1,0:T(8,128)(2,1)}, u32[]{:S(2)}, u32[]{:S(2)}) collective-permute-start(bf16[2,1024,256]{2,1,0:T(8,128)(2,1)S(1)} %constant_dynamic-update-slice_fusion.2.refs_0_), channel_id=1, source_target_pairs={{0,4},{2,6},{4,0},{6,2},{8,12},{10,14},{12,8},{14,10},{16,20},{18,... | collective-permute-start | bytes 3145736 | tf_op jit(solution)/shard_map/ppermute | solution.py:424
  297.8 26.0 %collective-permute-start.27 = (bf16[512,1024]{1,0:T(8,128)(2,1)}, bf16[512,1024]{1,0:T(8,128)(2,1)}, u32[]{:S(2)}, u32[]{:S(2)}) collective-permute-start(bf16[512,1024]{1,0:T(8,128)(2,1)} %reduced.1), channel_id=1, source_target_pairs={{0,1},{1,0},{2,3},{3,2},{4,5},{5,4},{6,7},{7,6},{8,9},{9,8},{10,11... | collective-permute-start | bytes 3145736 | tf_op jit(solution)/shard_map/ppermute | solution.py:773
  298.0 13.9 %collective-permute-start.28 = (bf16[1,2,128,512]{3,2,1,0:T(8,128)(2,1)S(1)}, bf16[1,2,128,512]{3,2,1,0:T(8,128)(2,1)S(1)}, u32[]{:S(2)}, u32[]{:S(2)}) collective-permute-start(bf16[1,2,128,512]{3,2,1,0:T(8,128)(2,1)S(1)} %add_convert_fusion.18), channel_id=1, source_target_pairs={{0,16},{2,18},{4,20},{6,22},{8,24},{10,26},{12,28},{14,30},{16,0},... | collective-permute-start | bytes 786440 | tf_op jit(solution)/shard_map/ppermute | solution.py:424
  298.1 13.9 %collective-permute-start.35 = (f32[58,128]{1,0:T(8,128)S(1)}, f32[58,128]{1,0:T(8,128)S(1)}, u32[]{:S(2)}, u32[]{:S(2)}) collective-permute-start(f32[58,128]{1,0:T(8,128)S(1)} %add.176), channel_id=1, source_target_pairs={{0,4},{2,6},{4,0},{6,2},{8,12},{10,14},{12,8},{14,10},{16,20},{18,... | collective-permute-start | bytes 89096 | tf_op jit(solution)/shard_map/ppermute | solution.py:424
  303.5 13.6 %collective-permute-start.34 = (bf16[1,2,128,512]{3,2,1,0:T(8,128)(2,1)S(1)}, bf16[1,2,128,512]{3,2,1,0:T(8,128)(2,1)S(1)}, u32[]{:S(2)}, u32[]{:S(2)}) collective-permute-start(bf16[1,2,128,512]{3,2,1,0:T(8,128)(2,1)S(1)} %add_convert_fusion.17), channel_id=1, source_target_pairs={{0,8},{2,10},{4,12},{6,14},{8,0},{10,2},{12,4},{14,6},{16,24},{18,... | collective-permute-start | bytes 786440 | tf_op jit(solution)/shard_map/ppermute | solution.py:424
  312.0 10.8 %collective-permute-start.33 = (bf16[1,2,128,512]{3,2,1,0:T(8,128)(2,1)S(1)}, bf16[1,2,128,512]{3,2,1,0:T(8,128)(2,1)S(1)}, u32[]{:S(2)}, u32[]{:S(2)}) collective-permute-start(bf16[1,2,128,512]{3,2,1,0:T(8,128)(2,1)S(1)} %add_convert_fusion.16), channel_id=1, source_target_pairs={{0,8},{2,10},{4,12},{6,14},{8,0},{10,2},{12,4},{14,6},{16,24},{18,... | collective-permute-start | bytes 786440 | tf_op jit(solution)/shard_map/ppermute | solution.py:424
  312.1 18.8 %collective-permute-start.37 = (bf16[2,1024,256]{2,1,0:T(8,128)(2,1)S(1)}, bf16[2,1024,256]{2,1,0:T(8,128)(2,1)}, u32[]{:S(2)}, u32[]{:S(2)}) collective-permute-start(bf16[2,1024,256]{2,1,0:T(8,128)(2,1)S(1)} %constant_dynamic-update-slice_fusion.2.refs_0_), channel_id=1, source_target_pairs={{0,2},{2,0},{4,6},{6,4},{8,10},{10,8},{12,14},{14,12},{16,18},{18,... | collective-permute-start | bytes 3145736 | tf_op jit(solution)/shard_map/ppermute | solution.py:424
  317.1 25.7 %collective-permute-start.36 = (f32[58,128]{1,0:T(8,128)S(1)}, f32[58,128]{1,0:T(8,128)S(1)}, u32[]{:S(2)}, u32[]{:S(2)}) collective-permute-start(f32[58,128]{1,0:T(8,128)S(1)} %add.181), channel_id=1, source_target_pairs={{0,8},{2,10},{4,12},{6,14},{8,0},{10,2},{12,4},{14,6},{16,24},{18,... | collective-permute-start | bytes 89096 | tf_op jit(solution)/shard_map/ppermute | solution.py:424
  317.2 13.7 %copy-start.6 = (bf16[2,2,128,512]{3,2,1,0:T(8,128)(2,1)}, bf16[2,2,128,512]{3,2,1,0:T(8,128)(2,1)S(1)}, u32[]{:S(2)}) copy-start(bf16[2,2,128,512]{3,2,1,0:T(8,128)(2,1)S(1)} %constant_dynamic-update-slice_fusion.4.refs_2_) | copy-start | bytes 1572868
  317.2 19.2 %collective-permute-start.45 = (bf16[2,2,128,512]{3,2,1,0:T(8,128)(2,1)S(1)}, bf16[2,2,128,512]{3,2,1,0:T(8,128)(2,1)}, u32[]{:S(2)}, u32[]{:S(2)}) collective-permute-start(bf16[2,2,128,512]{3,2,1,0:T(8,128)(2,1)S(1)} %constant_dynamic-update-slice_fusion.4.refs_2_), channel_id=1, source_target_pairs={{0,4},{2,6},{4,0},{6,2},{8,12},{10,14},{12,8},{14,10},{16,20},{18,... | collective-permute-start | bytes 1572872 | tf_op jit(solution)/shard_map/ppermute | solution.py:424
  322.7 14.0 %collective-permute-start.39 = (bf16[2,1024,256]{2,1,0:T(8,128)(2,1)}, bf16[2,1024,256]{2,1,0:T(8,128)(2,1)S(1)}, u32[]{:S(2)}, u32[]{:S(2)}) collective-permute-start(bf16[2,1024,256]{2,1,0:T(8,128)(2,1)} %collective-permute-done.38.refs_1_), channel_id=1, source_target_pairs={{0,2},{2,0},{4,6},{6,4},{8,10},{10,8},{12,14},{14,12},{16,18},{18,... | collective-permute-start | bytes 3145736 | tf_op jit(solution)/shard_map/ppermute | solution.py:424
  323.7 12.7 %copy-start.7 = (bf16[2,2,128,512]{3,2,1,0:T(8,128)(2,1)}, bf16[2,2,128,512]{3,2,1,0:T(8,128)(2,1)S(1)}, u32[]{:S(2)}) copy-start(bf16[2,2,128,512]{3,2,1,0:T(8,128)(2,1)S(1)} %constant_dynamic-update-slice_fusion.6.refs_0_) | copy-start | bytes 1572868
  323.7 19.1 %collective-permute-start.43 = (bf16[2,2,128,512]{3,2,1,0:T(8,128)(2,1)S(1)}, bf16[2,2,128,512]{3,2,1,0:T(8,128)(2,1)}, u32[]{:S(2)}, u32[]{:S(2)}) collective-permute-start(bf16[2,2,128,512]{3,2,1,0:T(8,128)(2,1)S(1)} %constant_dynamic-update-slice_fusion.6.refs_0_), channel_id=1, source_target_pairs={{0,4},{2,6},{4,0},{6,2},{8,12},{10,14},{12,8},{14,10},{16,20},{18,... | collective-permute-start | bytes 1572872 | tf_op jit(solution)/shard_map/ppermute | solution.py:424
  330.9 13.6 %collective-permute-start.42 = (bf16[2,2,128,512]{3,2,1,0:T(8,128)(2,1)S(1)}, bf16[2,2,128,512]{3,2,1,0:T(8,128)(2,1)S(1)}, u32[]{:S(2)}, u32[]{:S(2)}) collective-permute-start(bf16[2,2,128,512]{3,2,1,0:T(8,128)(2,1)S(1)} %constant_dynamic-update-slice_fusion.4.refs_2_), channel_id=1, source_target_pairs={{0,2},{2,0},{4,6},{6,4},{8,10},{10,8},{12,14},{14,12},{16,18},{18,... | collective-permute-start | bytes 1572872 | tf_op jit(solution)/shard_map/ppermute | solution.py:424
  336.4 8.1 %collective-permute-start.41 = (bf16[2,2,128,512]{3,2,1,0:T(8,128)(2,1)S(1)}, bf16[2,2,128,512]{3,2,1,0:T(8,128)(2,1)S(1)}, u32[]{:S(2)}, u32[]{:S(2)}) collective-permute-start(bf16[2,2,128,512]{3,2,1,0:T(8,128)(2,1)S(1)} %constant_dynamic-update-slice_fusion.6.refs_0_), channel_id=1, source_target_pairs={{0,2},{2,0},{4,6},{6,4},{8,10},{10,8},{12,14},{14,12},{16,18},{18,... | collective-permute-start | bytes 1572872 | tf_op jit(solution)/shard_map/ppermute | solution.py:424
  336.7 14.5 %collective-permute-start.46 = (bf16[2,2,128,512]{3,2,1,0:T(8,128)(2,1)}, bf16[2,2,128,512]{3,2,1,0:T(8,128)(2,1)}, u32[]{:S(2)}, u32[]{:S(2)}) collective-permute-start(bf16[2,2,128,512]{3,2,1,0:T(8,128)(2,1)} %collective-permute-done.45.refs_4_), channel_id=1, source_target_pairs={{0,2},{2,0},{4,6},{6,4},{8,10},{10,8},{12,14},{14,12},{16,18},{18,... | collective-permute-start | bytes 1572872 | tf_op jit(solution)/shard_map/ppermute | solution.py:424
  342.9 8.4 %collective-permute-start.44 = (bf16[2,2,128,512]{3,2,1,0:T(8,128)(2,1)}, bf16[2,2,128,512]{3,2,1,0:T(8,128)(2,1)S(1)}, u32[]{:S(2)}, u32[]{:S(2)}) collective-permute-start(bf16[2,2,128,512]{3,2,1,0:T(8,128)(2,1)} %collective-permute-done.43.refs_2_), channel_id=1, source_target_pairs={{0,2},{2,0},{4,6},{6,4},{8,10},{10,8},{12,14},{14,12},{16,18},{18,... | collective-permute-start | bytes 1572872 | tf_op jit(solution)/shard_map/ppermute | solution.py:424
  343.2 14.0 %collective-permute-start.40 = (f32[58,128]{1,0:T(8,128)S(1)}, f32[58,128]{1,0:T(8,128)S(1)}, u32[]{:S(2)}, u32[]{:S(2)}) collective-permute-start(f32[58,128]{1,0:T(8,128)S(1)} %add.182), channel_id=1, source_target_pairs={{0,16},{2,18},{4,20},{6,22},{8,24},{10,26},{12,28},{14,30},{16,0},... | collective-permute-start | bytes 89096 | tf_op jit(solution)/shard_map/ppermute | solution.py:424
  (12 other events, 20.5 us)

commit v2 on v1

--- a/solution.py
+++ b/solution.py
@@ -294,7 +294,7 @@
         in_specs=[pl.BlockSpec((step, model), lambda i: (i, 0)), fixed((1, model)), fixed((1, model)), fixed(weight.shape)],
         out_specs=[pl.BlockSpec((step, model), lambda i: (i, 0)), pl.BlockSpec((3, step, width), lambda i: (0, i, 0))],
         out_shape=[jax.ShapeDtypeStruct((rows, model), BF16), jax.ShapeDtypeStruct((3, rows, width), BF16)],
-        cost_estimate=cost(6 * rows * model * width, 2 * (2 * rows * model + weight.size + 3 * rows * width)),
+        cost_estimate=cost16(6 * rows * model * width, 2 * (2 * rows * model + weight.size + 3 * rows * width)),
         name="project",
     )(x, gain, shift, weight)
 
@@ -341,7 +341,7 @@
             pl.BlockSpec((step, model), lambda i: (i, 0)),
         ],
         out_shape=[jax.ShapeDtypeStruct((own, model), BF16), jax.ShapeDtypeStruct((2 * own, model), BF16)],
-        cost_estimate=cost(8 * own * model * width, 2 * (4 * own * model + 4 * own * width + 2 * weight.size) + 4 * own * model),
+        cost_estimate=cost4(8 * own * model * width, 2 * (4 * own * model + 4 * own * width + 2 * weight.size) + 4 * own * model),
         name="mix",
     )(tokens, other, mixed, mixed_other, weight, weight_other, gain, shift)
 
@@ -685,20 +685,19 @@
     count = put.pieces
     pieces, outs = refs[-2 * count - put.outs:-put.outs], refs[-put.outs:]
     for a in range(2):
-        @pl.when(g // 2 == a)
+        @pl.when(g == a)
         def _(a=a):
-            put(pieces[a::2], outs)
+            for j in range(2):
+                put([piece.at[j] for piece in pieces[a::2]], outs, j ^ (s_ref[0] % 2))
 
 
 def spread(places, part, pieces, put, tail, out_specs, out_shape, given=None, name=None):
     zeros = (0,) * len(tail)
 
     def at(g, s):
-        return (g % 2 + 4 * (g // 2) + 2 * part) ^ s[0]
-
-    in_specs = [
-        pl.BlockSpec((1, *tail), lambda g, s, a=k % 2: (jnp.clip(g - 2 * a, 0, 1), *zeros)) for k in range(len(pieces))
-    ]
+        return (2 * g + part) ^ (s[0] // 2)
+
+    in_specs = [pl.BlockSpec((2, *tail), lambda g, s: (0, *zeros)) for _ in pieces]
     args = list(pieces)
     aliases = {}
     if given is not None:
@@ -708,7 +707,7 @@
     return pl.pallas_call(
         functools.partial(spread_kernel, put),
         grid_spec=pltpu.PrefetchScalarGridSpec(
-            num_scalar_prefetch=1, grid=(4,), in_specs=in_specs, out_specs=[spec(at) for spec in out_specs],
+            num_scalar_prefetch=1, grid=(2,), in_specs=in_specs, out_specs=[spec(at) for spec in out_specs],
         ),
         out_shape=out_shape,
         input_output_aliases=aliases,
@@ -719,33 +718,53 @@
 
 def by_rows(count, step):
     def some(i, _):
-        step(pl.ds(pl.multiple_of(i * 64, 64), 64))
+        step(pl.multiple_of(i * 64, 64))
         return 0
 
     lax.fori_loop(0, count // 64, some, 0)
 
 
-def put_rows(pieces, outs):
-    def some(rows):
-        outs[0][rows, :] = pieces[0][0, rows, :].astype(F32)
-
-    by_rows(outs[0].shape[0], some)
+def put_rows(pieces, outs, where):
+    rows = pieces[0].shape[0]
+    base = pl.multiple_of(where * rows, rows)
+
+    def some(start):
+        outs[0][pl.ds(base + start, 64), :] = pieces[0][pl.ds(start, 64), :].astype(F32)
+
+    by_rows(rows, some)
 
 
 put_rows.outs = 1
 put_rows.pieces = 1
 
 
-def put_heads(pieces, outs):
+def put_columns(pieces, outs, where):
+    rows, columns = pieces[0].shape
+    base = pl.multiple_of(where * columns, columns)
+
+    def some(start):
+        outs[0][pl.ds(start, 64), pl.ds(base, columns)] = pieces[0][pl.ds(start, 64), :].astype(F32)
+
+    by_rows(rows, some)
+
+
+put_columns.outs = 1
+put_columns.pieces = 1
+
+
+def put_heads(pieces, outs, where):
     queries, values = pieces
-
-    def some(rows):
+    rows = queries.shape[1]
+    base = pl.multiple_of(where * rows, rows)
+
+    def some(start):
+        here, there = pl.ds(start, 64), pl.ds(base + start, 64)
         for c in range(2):
-            outs[0][c, rows, :] = queries[0, c, rows, :].astype(F32)
-        outs[0][2, rows, :] = values[0, 0, rows, :].astype(F32)
-
-    by_rows(outs[0].shape[1], some)
-    outs[1][...] = values[0, 1].astype(F32).T
+            outs[0][c, there, :] = queries[c, here, :].astype(F32)
+        outs[0][2, there, :] = values[0, here, :].astype(F32)
+
+    by_rows(rows, some)
+    outs[1][:, pl.ds(base, rows)] = values[1].astype(F32).T
 
 
 put_heads.outs = 2
@@ -1009,11 +1028,11 @@
     reduce_shape = [jax.ShapeDtypeStruct(reduce_weight.shape, F32)]
     expand_shape = [jax.ShapeDtypeStruct(expand_weight.shape, F32)]
     heads_shape = [jax.ShapeDtypeStruct(heads_weight.shape, F32), jax.ShapeDtypeStruct(mixer_weight.shape, F32)]
-    reduce_spec = [lambda to: pl.BlockSpec(chunk, lambda g, s: (to(g, s), 0))]
-    expand_spec = [lambda to: pl.BlockSpec(turned, lambda g, s: (0, to(g, s)))]
+    reduce_spec = [lambda to: pl.BlockSpec((hidden // 4, model), lambda g, s: (to(g, s), 0))]
+    expand_spec = [lambda to: pl.BlockSpec((model, hidden // 4), lambda g, s: (0, to(g, s)))]
     heads_spec = [
-        lambda to: pl.BlockSpec((3, model // 8, width), lambda g, s: (0, to(g, s), 0)),
-        lambda to: pl.BlockSpec((width, model // 8), lambda g, s: (0, to(g, s))),
+        lambda to: pl.BlockSpec((3, model // 4, width), lambda g, s: (0, to(g, s), 0)),
+        lambda to: pl.BlockSpec((width, model // 4), lambda g, s: (0, to(g, s))),
     ]
 
     def reduce_near():
@@ -1030,13 +1049,13 @@
 
     def expand_near():
         v.expand_grad = line(
-            lambda *xs: spread(at, 0, xs, put_rows, turned, expand_spec, expand_shape, name="expand_near"),
+            lambda *xs: spread(at, 0, xs, put_columns, turned, expand_spec, expand_shape, name="expand_near"),
             *expand_sum.nears(),
         )
 
     def expand_far():
         v.expand_grad = line(
-            lambda given, *xs: spread(at, 1, xs, put_rows, turned, expand_spec, expand_shape, given, name="expand_far"),
+            lambda given, *xs: spread(at, 1, xs, put_columns, turned, expand_spec, expand_shape, given, name="expand_far"),
             v.expand_grad, *expand_sum.fars(),
         )
 
@@ -1059,7 +1078,7 @@
         query_chunks, reduce_sum.third, value_chunks, first_other, expand_sum.second, reduce_sum.fourth,
         query_sum.first, value_sum.first, expand_sum.third, reduce_sum.fifth, query_sum.second,
         value_sum.second, first_own, first_back, expand_sum.fourth, pack_first, reduce_sum.sixth, pack_next(2),
-        value_sum.third, expand_sum.fifth, query_sum.third, reduced_other, value_sum.fourth, reduce_near,
+        value_sum.third, expand_sum.fifth, reduced_other, query_sum.third, reduce_near, value_sum.fourth,
         reduce_far, query_sum.fourth, pack_next(4), expand_sum.sixth, value_sum.fifth, query_sum.fifth, output,
         value_sum.sixth, expand_near, expand_far, pack_next(8), query_sum.sixth, heads_near, heads_far,
         pack_next(0),

time: 364 us -> 359 us (0.986)
  waiting for transfers between devices: 88.3 us -> 81.9 us
  starting transfers between devices: 38.6 us -> 43.1 us
  Pallas kernels: 195 us -> 191 us
    ppermute x37, waiting for transfers between devices: 54.1 us -> 47.7 us  [trade(): return lax.ppermute(x, 'dp', [(i, i ^ bit) for i in range(size)])]
    ppermute x37, starting transfers between devices: 29.9 us -> 34.3 us  [trade(): return lax.ppermute(x, 'dp', [(i, i ^ bit) for i in range(size)])]
    pallas_call x6, Pallas kernels: 30.9 us -> 26.9 us  [spread(): pl.pallas_call(functools.partial(spread_kernel, put), grid_spec=pltpu.Pre...]
  transfers between devices with their start and end apart: 47 -> 47, of which waited for: 15 -> 14; matrix products, arithmetic and copies ran while one was open for 8% -> 8% of each run, Pallas kernels for 49% -> 49%
where the time goes in v2:
time: 359 us; the launch traced here: 354 us
  Pallas kernels  191 us (53%)
  waiting for transfers between devices  81.9 us (23%)
  starting transfers between devices  43.1 us (12%)
  other arithmetic  21 us (6%)
  local copies, waits for them, and re-layouts  10.6 us (3%)
  matrix products  4.31 us (1%)
    ppermute x37, waiting for transfers between devices, trade(): return lax.ppermute(x, 'dp', [(i, i ^ bit) for i in range(size)])  47.7 us
    pallas_call x4, Pallas kernels, pair_call(): pl.pallas_call(functools.partial(kernel, slot), grid_spec=pltpu.PrefetchS...  34.8 us
    ppermute x37, starting transfers between devices, trade(): return lax.ppermute(x, 'dp', [(i, i ^ bit) for i in range(size)])  34.3 us
    ppermute x10, waiting for transfers between devices, swap(): return lax.ppermute(x, 'mp', [(0, 1), (1, 0)])  34.2 us
    pallas_call x6, Pallas kernels, spread(): pl.pallas_call(functools.partial(spread_kernel, put), grid_spec=pltpu.Pre...  26.9 us
    pallas_call x2, Pallas kernels, expand(): pl.pallas_call(expand_kernel, grid=(hidden // step,), in_specs=[pl.BlockS...  23.4 us
    pallas_call x1, Pallas kernels, attend_backward(): pl.pallas_call(kernel, grid_spec=pltpu.PrefetchScalarGridSpec(num_scalar_...  22.8 us
    pallas_call x3, Pallas kernels, columns_dot(): pl.pallas_call(functools.partial(columns_kernel, turn), grid=(columns //...  17.9 us
  transfers between devices with their start and end apart: 47, of which 14 were waited for; matrix products, arithmetic and copies ran while one was open for 8% of the time, Pallas kernels for 49%

profile of v2, /device:TPU:25, one launch (start us, length us, event | category | flops | bytes accessed | tf_op | source)
XLA Modules:
  0.0 353.9 jit_solution(1175766234871714278)
XLA Ops:
  0.6 1.3 collective-permute-start
  2.6 2.3 broadcast_select_fusion.1.a_ref.refs_2_.add_ref
  5.0 5.5 %project.2 = (bf16[512,1024]{1,0:T(8,128)(2,1)}, bf16[3,512,512]{2,1,0:T(8,128)(2,1)}) custom-call(bf16[512,1024]{1,0:T(8,128)(2,1)} %source_ref, f32[1,1024]{1,0:T(1,128)} %bitcast.35, f32[1,1024]{1,0:T(1,128)} %bitcast.38, bf16[3,1024,512]{2,1,0:T(8,128)(2,1)} %w_ref.6), custom_call_target="tpu_custom_call" | custom-call | flops 25769803776 | bytes 109051904 | tf_op jit(solution)/shard_map/project/pallas_call | solution.py:291
  10.5 6.3 %active_grad.2.g_ref = bf16[512,2048]{1,0:T(8,128)(2,1)} custom-call(bf16[512,1024]{1,0:T(8,128)(2,1)} %broadcast_select_fusion.1.a_ref.refs_2_.add_ref, bf16[2048,1024]{1,0:T(8,128)(2,1)} %w_ref.7), custom_call_target="tpu_custom_call" | custom-call | flops 34359738368 | bytes 117440512 | tf_op jit(solution)/shard_map/active_grad/pallas_call | solution.py:551
  16.7 1.5 bias_rows.1.b_ref
  18.9 6.2 %collective-permute-done.x_ref.x1_ref = bf16[512,1024]{1,0:T(8,128)(2,1)} collective-permute-done((bf16[512,1024]{1,0:T(8,128)(2,1)}, bf16[512,1024]{1,0:T(8,128)(2,1)}, u32[]{:S(2)}, u32[]{:S(2)}) %collective-permute-start) | collective-permute-done | bytes 1048608 | tf_op jit(solution)/shard_map/ppermute | solution.py:792
  26.5 5.5 %project.3 = (bf16[512,1024]{1,0:T(8,128)(2,1)}, bf16[3,512,512]{2,1,0:T(8,128)(2,1)}) custom-call(bf16[512,1024]{1,0:T(8,128)(2,1)} %collective-permute-done.x_ref.x1_ref, f32[1,1024]{1,0:T(1,128)} %bitcast.36, f32[1,1024]{1,0:T(1,128)} %bitcast.39, bf16[3,1024,512]{2,1,0:T(8,128)(2,1)} %w_ref.6), custom_call_target="tpu_custom_call" | custom-call | flops 25769803776 | bytes 109051904 | tf_op jit(solution)/shard_map/project/pallas_call | solution.py:291
  32.1 14.4 %attend_forward.1 = (bf16[1024,512]{1,0:T(8,128)(2,1)}, f32[4,1024,128]{2,1,0:T(8,128)}) custom-call(s32[2]{0:T(128)} %pad_add_fusion.sp, bf16[3,512,512]{2,1,0:T(8,128)(2,1)} %get-tuple-element.287.a_ref, bf16[3,512,512]{2,1,0:T(8,128)(2,1)} %get-tuple-element.288.c_ref, f32[4,2,2048]{2,1,0:T(2,128)} %bias_rows.1.b_ref), custom_call_target="tpu_custom_call" | custom-call | flops 4294967296 | bytes 6291456 | tf_op jit(solution)/shard_map/attend_forward/pallas_call | solution.py:124
  46.4 2.2 collective-permute-start.3
  49.2 1.3 collective-permute-start.1
  51.3 2.2 order_rows.1.w1_ref
  53.5 5.9 %collective-permute-done.4 = bf16[512,1024]{1,0:T(8,128)(2,1)S(1)} collective-permute-done((bf16[512,1024]{1,0:T(8,128)(2,1)S(1)}, bf16[512,1024]{1,0:T(8,128)(2,1)S(1)}, u32[]{:S(2)}, u32[]{:S(2)}) %collective-permute-start.4) | collective-permute-done | bytes 1048608 | tf_op jit(solution)/shard_map/ppermute | solution.py:792
  60.5 6.1 %active_grad.3.g_ref = bf16[512,2048]{1,0:T(8,128)(2,1)} custom-call(bf16[512,1024]{1,0:T(8,128)(2,1)} %broadcast_select_fusion.a_ref.refs_3_, bf16[2048,1024]{1,0:T(8,128)(2,1)} %w_ref.7), custom_call_target="tpu_custom_call" | custom-call | flops 34359738368 | bytes 117440512 | tf_op jit(solution)/shard_map/active_grad/pallas_call | solution.py:551
  66.6 15.3 %collective-permute-done.1.p_ref = bf16[1024,512]{1,0:T(8,128)(2,1)} collective-permute-done((bf16[1024,512]{1,0:T(8,128)(2,1)}, bf16[1024,512]{1,0:T(8,128)(2,1)}, u32[]{:S(2)}, u32[]{:S(2)}) %collective-permute-start.1) | collective-permute-done | bytes 1048608 | tf_op jit(solution)/shard_map/ppermute | solution.py:792
  82.0 7.8 %mix.1 = (bf16[512,1024]{1,0:T(8,128)(2,1)}, bf16[1024,1024]{1,0:T(8,128)(2,1)}) custom-call(bf16[512,1024]{1,0:T(8,128)(2,1)} %source_ref, bf16[512,1024]{1,0:T(8,128)(2,1)} %collective-permute-done.x_ref.x1_ref, bf16[1024,512]{1,0:T(8,128)(2,1)} %get-tuple-element.311.m_ref.o_ref.refs_5_, bf16[1024,512]{1,0:T(8,128)(2,1)} %collective-permute-done.1.p_ref, ...), custom_call_target="tpu_custom_call" | custom-call | flops 8589934592 | bytes 41943040 | tf_op jit(solution)/shard_map/mix/pallas_call | solution.py:329
  89.8 11.7 %expand.2 = (bf16[512,2048]{1,0:T(8,128)(2,1)}, bf16[512,2048]{1,0:T(8,128)(2,1)}, bf16[512,1024]{1,0:T(8,128)(2,1)}, f32[1,2048]{1,0:T(1,128)}) custom-call(bf16[1024,1024]{1,0:T(8,128)(2,1)} %get-tuple-element.275.x_ref.refs_0_, bf16[512,2048]{1,0:T(8,128)(2,1)} %active_grad.3.g_ref, bf16[1024,2048]{1,0:T(8,128)(2,1)} %w_ref.4, bf16[1,2048]{1,0:T(2,128)(2,1)} %reshape.162.b_ref), custom_call_target="tpu_custom_call" | custom-call | flops 4294967296 | bytes 12582912 | tf_op jit(solution)/shard_map/expand/pallas_call | solution.py:387
  101.5 1.3 collective-permute-start.5
  103.4 11.6 %expand.3 = (bf16[512,2048]{1,0:T(8,128)(2,1)}, bf16[512,2048]{1,0:T(8,128)(2,1)}, bf16[512,1024]{1,0:T(8,128)(2,1)}, f32[1,2048]{1,0:T(1,128)}) custom-call(bf16[1024,1024]{1,0:T(8,128)(2,1)} %get-tuple-element.275.x_ref.refs_0_, bf16[512,2048]{1,0:T(8,128)(2,1)} %active_grad.2.g_ref, bf16[1024,2048]{1,0:T(8,128)(2,1)} %w_ref.4, bf16[1,2048]{1,0:T(2,128)(2,1)} %reshape.162.b_ref), custom_call_target="tpu_custom_call" | custom-call | flops 4294967296 | bytes 12582912 | tf_op jit(solution)/shard_map/expand/pallas_call | solution.py:387
  115.0 9.8 %reduce_grad.1 = (bf16[4,256,1024]{2,1,0:T(8,128)(2,1)}, bf16[4,256,1024]{2,1,0:T(8,128)(2,1)}) custom-call(s32[2]{0:T(128)} %pad_add_fusion.1.s_ref, bf16[512,2048]{1,0:T(8,128)(2,1)} %get-tuple-element.375.refs_0_.a_ref, bf16[512,2048]{1,0:T(8,128)(2,1)} %get-tuple-element.354.refs_1_.a_ref, ...), custom_call_target="tpu_custom_call" | custom-call | flops 4294967296 | bytes 10485760 | tf_op jit(solution)/shard_map/reduce_grad/pallas_call | solution.py:449
  124.9 2.8 collective-permute-start.7
  128.6 5.2 %back_rows.2 = (bf16[512,1024]{1,0:T(8,128)(2,1)}, f32[8,1024]{1,0:T(8,128)}) custom-call(bf16[512,1024]{1,0:T(8,128)(2,1)} %get-tuple-element.266.a_ref, bf16[512,1024]{1,0:T(8,128)(2,1)} %copy-done.8, bf16[512,1024]{1,0:T(8,128)(2,1)} %get-tuple-element.374.source_ref.m_ref, bf16[512,1024]{1,0:T(8,128)(2,1)} %broadcast_select_fusion.1.a_ref.refs_2_.add_ref, ...), custom_call_target="tpu_custom_call" | custom-call | flops 15728640 | bytes 5242880 | tf_op jit(solution)/shard_map/back_rows/pallas_call | solution.py:647
  133.8 2.8 convolution_convert_fusion.1
  136.6 10.0 %expand_grad.1 = (bf16[4,1024,256]{2,1,0:T(8,128)(2,1)}, bf16[4,1024,256]{2,1,0:T(8,128)(2,1)}) custom-call(s32[2]{0:T(128)} %pad_add_fusion.1.s_ref, bf16[1024,1024]{1,0:T(8,128)(2,1)} %get-tuple-element.275.x_ref.refs_0_, bf16[512,2048]{1,0:T(8,128)(2,1)} %get-tuple-element.276.refs_1_, bf16[512,2048]{1,0:T(8,128)(2,1)} %get-tuple-element.277.refs_2_), custom_call_target="tpu_custom_call" | custom-call | flops 4294967296 | bytes 10485760 | tf_op jit(solution)/shard_map/expand_grad/pallas_call | solution.py:449
  148.1 1.5 convolution_convert_fusion.d0_ref
  149.7 3.7 %add_convert_fusion.2 = (bf16[2,256,1024]{2,1,0:T(8,128)(2,1)S(1)}, bf16[2,256,1024]{2,1,0:T(8,128)(2,1)}) fusion(bf16[4,256,1024]{2,1,0:T(8,128)(2,1)} %collective-permute-done.7, bf16[4,256,1024]{2,1,0:T(8,128)(2,1)S(1)} %copy-done.3), kind=kLoop, calls=%fused_computation.2 | loop fusion | flops 4194304 | bytes 6291456 | tf_op jit(solution)/shard_map/convert_element_type | solution.py:428
  154.6 1.6 add_convert_fusion
  156.1 3.9 %collective-permute-done.9.d1_ref = bf16[512,512]{1,0:T(8,128)(2,1)} collective-permute-done((bf16[512,512]{1,0:T(8,128)(2,1)}, bf16[512,512]{1,0:T(8,128)(2,1)}, u32[]{:S(2)}, u32[]{:S(2)}) %collective-permute-start.9) | collective-permute-done | bytes 524320 | tf_op jit(solution)/shard_map/ppermute | solution.py:792
  160.0 22.8 %attend_backward.1 = (bf16[3,1024,512]{2,1,0:T(8,128)(2,1)}, f32[4,4,512]{2,1,0:T(4,128)}) custom-call(s32[2]{0:T(128)} %pad_add_fusion.sp, bf16[3,512,512]{2,1,0:T(8,128)(2,1)} %get-tuple-element.287.a_ref, bf16[3,512,512]{2,1,0:T(8,128)(2,1)} %get-tuple-element.288.c_ref, bf16[512,512]{1,0:T(8,128)(2,1)} %convolution_convert_fusion.d0_ref, ...), custom_call_target="tpu_custom_call" | custom-call | flops 10737418240 | bytes 10485760 | tf_op jit(solution)/shard_map/attend_backward/pallas_call | solution.py:225
  182.8 2.7 add_convert_fusion.14
  185.8 1.3 collective-permute-start.8
  187.1 7.5 %heads_grad.1 = (bf16[4,2,128,512]{3,2,1,0:T(8,128)(2,1)}, bf16[4,2,128,512]{3,2,1,0:T(8,128)(2,1)}) custom-call(s32[2]{0:T(128)} %pad_add_fusion.1.s_ref, bf16[512,1024]{1,0:T(8,128)(2,1)} %get-tuple-element.306.refs_0_, bf16[512,1024]{1,0:T(8,128)(2,1)} %get-tuple-element.307.refs_1_, bf16[3,1024,512]{2,1,0:T(8,128)(2,1)} %get-tuple-element.332.refs_2_.g_ref), custom_call_target="tpu_custom_call" | custom-call | flops 2147483648 | bytes 7340032 | tf_op jit(solution)/shard_map/heads_grad/pallas_call | solution.py:449
  194.8 2.7 collective-permute-start.15
  200.0 7.6 %values_grad.1 = (bf16[4,2,128,512]{3,2,1,0:T(8,128)(2,1)}, bf16[4,2,128,512]{3,2,1,0:T(8,128)(2,1)}) custom-call(s32[2]{0:T(128)} %pad_add_fusion.1.s_ref, bf16[512,1024]{1,0:T(8,128)(2,1)} %get-tuple-element.306.refs_0_, bf16[512,1024]{1,0:T(8,128)(2,1)} %get-tuple-element.307.refs_1_, bf16[3,1024,512]{2,1,0:T(8,128)(2,1)} %get-tuple-element.332.refs_2_.g_ref, ...), custom_call_target="tpu_custom_call" | custom-call | flops 2147483648 | bytes 10485760 | tf_op jit(solution)/shard_map/values_grad/pallas_call | solution.py:449
  207.6 2.5 collective-permute-start.14
  210.3 5.6 %first_rows.2 = bf16[512,1024]{1,0:T(8,128)(2,1)} custom-call(bf16[3,1024,512]{2,1,0:T(8,128)(2,1)} %get-tuple-element.332.refs_2_.g_ref, bf16[3,1024,512]{2,1,0:T(8,128)(2,1)} %w_ref.6), custom_call_target="tpu_custom_call" | custom-call | flops 1610612736 | bytes 8388608 | tf_op jit(solution)/shard_map/first_rows/pallas_call | solution.py:606
  215.9 1.3 collective-permute-start.21
  217.2 1.5 add_convert_fusion.11
  219.0 6.0 %collective-permute-done.16 = bf16[1,256,1024]{2,1,0:T(8,128)(2,1)S(1)} collective-permute-done((bf16[1,256,1024]{2,1,0:T(8,128)(2,1)S(1)}, bf16[1,256,1024]{2,1,0:T(8,128)(2,1)S(1)}, u32[]{:S(2)}, u32[]{:S(2)}) %collective-permute-start.16) | collective-permute-done | bytes 524320 | tf_op jit(solution)/shard_map/ppermute | solution.py:424
  225.2 1.5 add_convert_fusion.8
  228.7 8.6 %collective-permute-done.13 = bf16[1,1024,256]{2,1,0:T(8,128)(2,1)S(1)} collective-permute-done((bf16[1,1024,256]{2,1,0:T(8,128)(2,1)S(1)}, bf16[1,1024,256]{2,1,0:T(8,128)(2,1)S(1)}, u32[]{:S(2)}, u32[]{:S(2)}) %collective-permute-start.13) | collective-permute-done | bytes 524320 | tf_op jit(solution)/shard_map/ppermute | solution.py:424
  237.5 15.8 %collective-permute-done.20 = bf16[1,256,1024]{2,1,0:T(8,128)(2,1)S(1)} collective-permute-done((bf16[1,256,1024]{2,1,0:T(8,128)(2,1)S(1)}, bf16[1,256,1024]{2,1,0:T(8,128)(2,1)S(1)}, u32[]{:S(2)}, u32[]{:S(2)}) %collective-permute-start.20) | collective-permute-done | bytes 524320 | tf_op jit(solution)/shard_map/ppermute | solution.py:424
  253.5 1.3 collective-permute-start.30
  256.4 5.6 %first_rows.3.a_ref = bf16[512,1024]{1,0:T(8,128)(2,1)} custom-call(bf16[3,1024,512]{2,1,0:T(8,128)(2,1)} %get-tuple-element.332.refs_2_.g_ref, bf16[3,1024,512]{2,1,0:T(8,128)(2,1)} %w_ref.6), custom_call_target="tpu_custom_call" | custom-call | flops 1610612736 | bytes 8388608 | tf_op jit(solution)/shard_map/first_rows/pallas_call | solution.py:606
  262.1 5.2 %back_rows.3 = (bf16[512,1024]{1,0:T(8,128)(2,1)}, f32[8,1024]{1,0:T(8,128)}) custom-call(bf16[512,1024]{1,0:T(8,128)(2,1)} %first_rows.3.a_ref, bf16[512,1024]{1,0:T(8,128)(2,1)} %collective-permute-done.21.b_ref, bf16[512,1024]{1,0:T(8,128)(2,1)} %source_ref, bf16[512,1024]{1,0:T(8,128)(2,1)} %get-tuple-element.337.refs_3_.add_ref, f32[1,1024]{1,0:T(1,128)} %bitcast.37), custom_call_target="tpu_custom_call" | custom-call | flops 15728640 | bytes 5242880 | tf_op jit(solution)/shard_map/back_rows/pallas_call | solution.py:647
  268.1 1.5 collective-permute-start.22
  270.0 2.9 collective-permute-done.24
  273.0 2.1 collective-permute-start.25
  276.5 1.4 collective-permute-done.30.refs_1_
  277.9 1.3 collective-permute-start.31
  279.2 7.4 %collective-permute-done.22 = bf16[1,1024,256]{2,1,0:T(8,128)(2,1)} collective-permute-done((bf16[1,1024,256]{2,1,0:T(8,128)(2,1)S(1)}, bf16[1,1024,256]{2,1,0:T(8,128)(2,1)}, u32[]{:S(2)}, u32[]{:S(2)}) %collective-permute-start.22) | collective-permute-done | bytes 524320 | tf_op jit(solution)/shard_map/ppermute | solution.py:424
  288.1 5.6 %reduced.1 = bf16[512,1024]{1,0:T(8,128)(2,1)} custom-call(bf16[512,2048]{1,0:T(8,128)(2,1)} %get-tuple-element.354.refs_1_.a_ref, bf16[2048,1024]{1,0:T(8,128)(2,1)} %w_ref.7), custom_call_target="tpu_custom_call" | custom-call | flops 34359738368 | bytes 117440512 | tf_op jit(solution)/shard_map/reduced/pallas_call | solution.py:551
  294.1 4.4 %reduce_near.1.refs_0_ = f32[2048,1024]{1,0:T(8,128)} custom-call(s32[2]{0:T(128)} %pad_add_fusion.1.s_ref, bf16[2,256,1024]{2,1,0:T(8,128)(2,1)} %copy-done.1, bf16[2,256,1024]{2,1,0:T(8,128)(2,1)} %collective-permute-done.29.refs_1_), custom_call_target="tpu_custom_call" | custom-call | bytes 6291456 | tf_op jit(solution)/shard_map/reduce_near/pallas_call | solution.py:707
  300.9 4.4 %reduce_far.1 = f32[2048,1024]{1,0:T(8,128)} custom-call(s32[2]{0:T(128)} %pad_add_fusion.1.s_ref, f32[2048,1024]{1,0:T(8,128)} %reduce_near.1.refs_0_, bf16[2,256,1024]{2,1,0:T(8,128)(2,1)} %collective-permute-done.30.refs_1_, bf16[2,256,1024]{2,1,0:T(8,128)(2,1)} %collective-permute-done.31.refs_2_), custom_call_target="tpu_custom_call", output_to_operand_aliasing={{}: (1, {})} | custom-call | bytes 6291456 | tf_op jit(solution)/shard_map/reduce_far/pallas_call | solution.py:707
  305.5 1.3 collective-permute-start.33
  306.8 3.6 %collective-permute-done.35 = f32[58,128]{1,0:T(8,128)S(1)} collective-permute-done((f32[58,128]{1,0:T(8,128)S(1)}, f32[58,128]{1,0:T(8,128)S(1)}, u32[]{:S(2)}, u32[]{:S(2)}) %collective-permute-start.35) | collective-permute-done | bytes 29728 | tf_op jit(solution)/shard_map/ppermute | solution.py:424
  310.4 3.7 %collective-permute-start.37 = (bf16[2,1024,256]{2,1,0:T(8,128)(2,1)S(1)}, bf16[2,1024,256]{2,1,0:T(8,128)(2,1)}, u32[]{:S(2)}, u32[]{:S(2)}) collective-permute-start(bf16[2,1024,256]{2,1,0:T(8,128)(2,1)S(1)} %constant_dynamic-update-slice_fusion.2.refs_0_), channel_id=1, source_target_pairs={{0,2},{2,0},{4,6},{6,4},{8,10},{10,8},{12,14},{14,12},{16,18},{18,... | collective-permute-start | bytes 3145736 | tf_op jit(solution)/shard_map/ppermute | solution.py:424
  314.6 2.7 collective-permute-done.33
  317.3 1.6 collective-permute-start.39
  318.9 1.3 collective-permute-start.43
  320.2 6.9 %output.1 = bf16[512,1024]{1,0:T(8,128)(2,1)} custom-call(bf16[512,1024]{1,0:T(8,128)(2,1)} %get-tuple-element.374.source_ref.m_ref, bf16[512,2048]{1,0:T(8,128)(2,1)} %get-tuple-element.375.refs_0_.a_ref, bf16[2048,1024]{1,0:T(8,128)(2,1)} %w_ref.7, bf16[512,1024]{1,0:T(8,128)(2,1)} %collective-permute-done.26.r_ref, f32[1,1024]{1,0:T(1,128)} %bitcast.41), custom_call_target="tpu_custom_call" | custom-call | flops 34359738368 | bytes 167772160 | tf_op jit(solution)/shard_map/output/pallas_call | solution.py:573
  328.0 4.5 %expand_near.1.refs_0_ = f32[1024,2048]{1,0:T(8,128)} custom-call(s32[2]{0:T(128)} %pad_add_fusion.1.s_ref, bf16[2,1024,256]{2,1,0:T(8,128)(2,1)} %copy-done.2, bf16[2,1024,256]{2,1,0:T(8,128)(2,1)} %collective-permute-done.37.refs_1_), custom_call_target="tpu_custom_call" | custom-call | bytes 6291456 | tf_op jit(solution)/shard_map/expand_near/pallas_call | solution.py:707
  333.5 4.5 %expand_far.1 = f32[1024,2048]{1,0:T(8,128)} custom-call(s32[2]{0:T(128)} %pad_add_fusion.1.s_ref, f32[1024,2048]{1,0:T(8,128)} %expand_near.1.refs_0_, bf16[2,1024,256]{2,1,0:T(8,128)(2,1)} %collective-permute-done.38.refs_1_, bf16[2,1024,256]{2,1,0:T(8,128)(2,1)} %copy-done.13), custom_call_target="tpu_custom_call", output_to_operand_aliasing={{}: (1, {})} | custom-call | bytes 6291456 | tf_op jit(solution)/shard_map/expand_far/pallas_call | solution.py:707
  342.1 4.5 %heads_near.1 = (f32[3,1024,512]{2,1,0:T(8,128)}, f32[512,1024]{1,0:T(8,128)}) custom-call(s32[2]{0:T(128)} %pad_add_fusion.1.s_ref, bf16[2,2,128,512]{3,2,1,0:T(8,128)(2,1)} %copy-done.7, bf16[2,2,128,512]{3,2,1,0:T(8,128)(2,1)} %copy-done.15, bf16[2,2,128,512]{3,2,1,0:T(8,128)(2,1)} %copy-done.6, bf16[2,2,128,512]{3,2,1,0:T(8,128)(2,1)} %copy-done.14), custom_call_target="tpu_custom_call" | custom-call | bytes 6291456 | tf_op jit(solution)/shard_map/heads_near/pallas_call | solution.py:707
  347.5 4.5 %heads_far.1 = (f32[3,1024,512]{2,1,0:T(8,128)}, f32[512,1024]{1,0:T(8,128)}) custom-call(s32[2]{0:T(128)} %pad_add_fusion.1.s_ref, f32[3,1024,512]{2,1,0:T(8,128)} %get-tuple-element.395.refs_0_, f32[512,1024]{1,0:T(8,128)} %get-tuple-element.396.refs_1_, ...), custom_call_target="tpu_custom_call", output_to_operand_aliasing={{0}: (1, {}), {1}: (2, {})} | custom-call | bytes 6291456 | tf_op jit(solution)/shard_map/heads_far/pallas_call | solution.py:707
  (174 shorter events, 32.8 us)
Async XLA Ops:
  0.6 24.4 %collective-permute-start = (bf16[512,1024]{1,0:T(8,128)(2,1)}, bf16[512,1024]{1,0:T(8,128)(2,1)}, u32[]{:S(2)}, u32[]{:S(2)}) collective-permute-start(bf16[512,1024]{1,0:T(8,128)(2,1)} %source_ref), channel_id=1, source_target_pairs={{0,1},{1,0},{2,3},{3,2},{4,5},{5,4},{6,7},{7,6},{8,9},{9,8},{10,11... | collective-permute-start | bytes 3145736 | tf_op jit(solution)/shard_map/ppermute | solution.py:792
  10.5 8.3 %copy-start.20 = (bf16[512,1024]{1,0:T(8,128)(2,1)S(1)}, bf16[512,1024]{1,0:T(8,128)(2,1)}, u32[]{:S(2)}) copy-start(bf16[512,1024]{1,0:T(8,128)(2,1)} %w0_ref) | copy-start | bytes 3145732
  10.5 15.8 %copy-start.11 = (bf16[512,1024]{1,0:T(8,128)(2,1)S(1)}, bf16[512,1024]{1,0:T(8,128)(2,1)}, u32[]{:S(2)}) copy-start(bf16[512,1024]{1,0:T(8,128)(2,1)} %param.29) | copy-start | bytes 3145732
  25.1 21.4 %collective-permute-start.2 = (bf16[256,1024]{1,0:T(8,128)(2,1)S(1)}, bf16[256,1024]{1,0:T(8,128)(2,1)S(1)}, u32[]{:S(2)}, u32[]{:S(2)}) collective-permute-start(bf16[256,1024]{1,0:T(8,128)(2,1)S(1)} %constant_dynamic-slice_fusion), channel_id=1, source_target_pairs={{0,1},{1,0},{2,3},{3,2},{4,5},{5,4},{6,7},{7,6},{8,9},{9,8},{10,11... | collective-permute-start | bytes 1572872 | tf_op jit(solution)/shard_map/ppermute | solution.py:792
  26.3 33.1 %collective-permute-start.4 = (bf16[512,1024]{1,0:T(8,128)(2,1)S(1)}, bf16[512,1024]{1,0:T(8,128)(2,1)S(1)}, u32[]{:S(2)}, u32[]{:S(2)}) collective-permute-start(bf16[512,1024]{1,0:T(8,128)(2,1)S(1)} %copy-done.11), channel_id=1, source_target_pairs={{0,1},{1,0},{2,3},{3,2},{4,5},{5,4},{6,7},{7,6},{8,9},{9,8},{10,11... | collective-permute-start | bytes 3145736 | tf_op jit(solution)/shard_map/ppermute | solution.py:792
  32.1 16.6 %copy-start.26 = (bf16[2048]{0:T(1024)(128)(2,1)S(1)}, bf16[2048]{0:T(1024)(128)(2,1)}, u32[]{:S(2)}) copy-start(bf16[2048]{0:T(1024)(128)(2,1)} %param.26) | copy-start | bytes 12292
  46.4 4.1 %copy-start.17 = (bf16[256,1024]{1,0:T(8,128)(2,1)}, bf16[256,1024]{1,0:T(8,128)(2,1)S(1)}, u32[]{:S(2)}) copy-start(bf16[256,1024]{1,0:T(8,128)(2,1)S(1)} %collective-permute-done.2.a_ref) | copy-start | bytes 1572868
  46.4 4.0 %collective-permute-start.3 = (bf16[256,1024]{1,0:T(8,128)(2,1)S(1)}, bf16[256,1024]{1,0:T(8,128)(2,1)S(1)}, u32[]{:S(2)}, u32[]{:S(2)}) collective-permute-start(bf16[256,1024]{1,0:T(8,128)(2,1)S(1)} %collective-permute-done.2.a_ref), channel_id=1, source_target_pairs={{0,2},{2,0},{4,6},{6,4},{8,10},{10,8},{12,14},{14,12},{16,18},{18,... | collective-permute-start | bytes 1572872 | tf_op jit(solution)/shard_map/ppermute | solution.py:424
  49.2 32.7 %collective-permute-start.1 = (bf16[1024,512]{1,0:T(8,128)(2,1)}, bf16[1024,512]{1,0:T(8,128)(2,1)}, u32[]{:S(2)}, u32[]{:S(2)}) collective-permute-start(bf16[1024,512]{1,0:T(8,128)(2,1)} %get-tuple-element.311.m_ref.o_ref.refs_5_), channel_id=1, source_target_pairs={{0,1},{1,0},{2,3},{3,2},{4,5},{5,4},{6,7},{7,6},{8,9},{9,8},{10,11... | collective-permute-start | bytes 3145736 | tf_op jit(solution)/shard_map/ppermute | solution.py:792
  101.5 26.1 %collective-permute-start.5 = (bf16[512,1024]{1,0:T(8,128)(2,1)}, bf16[512,1024]{1,0:T(8,128)(2,1)S(1)}, u32[]{:S(2)}, u32[]{:S(2)}) collective-permute-start(bf16[512,1024]{1,0:T(8,128)(2,1)} %get-tuple-element.250), channel_id=1, source_target_pairs={{0,1},{1,0},{2,3},{3,2},{4,5},{5,4},{6,7},{7,6},{8,9},{9,8},{10,11... | collective-permute-start | bytes 3145736 | tf_op jit(solution)/shard_map/ppermute | solution.py:792
  124.9 24.8 %collective-permute-start.7 = (bf16[4,256,1024]{2,1,0:T(8,128)(2,1)}, bf16[4,256,1024]{2,1,0:T(8,128)(2,1)}, u32[]{:S(2)}, u32[]{:S(2)}) collective-permute-start(bf16[4,256,1024]{2,1,0:T(8,128)(2,1)} %get-tuple-element.264), channel_id=1, source_target_pairs={{0,2},{2,0},{4,6},{6,4},{8,10},{10,8},{12,14},{14,12},{16,18},{18,... | collective-permute-start | bytes 6291464 | tf_op jit(solution)/shard_map/ppermute | solution.py:424
  128.6 5.2 %copy-start.12 = (bf16[512,1024]{1,0:T(8,128)(2,1)S(1)}, bf16[512,1024]{1,0:T(8,128)(2,1)}, u32[]{:S(2)}) copy-start(bf16[512,1024]{1,0:T(8,128)(2,1)} %order_rows.1.w1_ref) | copy-start | bytes 3145732
  136.6 10.9 %copy-start = (bf16[512,1024]{1,0:T(8,128)(2,1)S(1)}, bf16[512,1024]{1,0:T(8,128)(2,1)}, u32[]{:S(2)}) copy-start(bf16[512,1024]{1,0:T(8,128)(2,1)} %get-tuple-element.337.refs_3_.add_ref) | copy-start | bytes 3145732
  136.6 11.5 %copy-start.21 = (bf16[512,1024]{1,0:T(8,128)(2,1)S(1)}, bf16[512,1024]{1,0:T(8,128)(2,1)}, u32[]{:S(2)}) copy-start(bf16[512,1024]{1,0:T(8,128)(2,1)} %w0_ref) | copy-start | bytes 3145732
  146.6 3.1 copy-start.3
  146.6 8.0 %collective-permute-start.6 = (bf16[4,1024,256]{2,1,0:T(8,128)(2,1)}, bf16[4,1024,256]{2,1,0:T(8,128)(2,1)S(1)}, u32[]{:S(2)}, u32[]{:S(2)}) collective-permute-start(bf16[4,1024,256]{2,1,0:T(8,128)(2,1)} %get-tuple-element.279), channel_id=1, source_target_pairs={{0,2},{2,0},{4,6},{6,4},{8,10},{10,8},{12,14},{14,12},{16,18},{18,... | collective-permute-start | bytes 6291464 | tf_op jit(solution)/shard_map/ppermute | solution.py:424
  146.6 13.4 %collective-permute-start.9 = (bf16[512,512]{1,0:T(8,128)(2,1)}, bf16[512,512]{1,0:T(8,128)(2,1)}, u32[]{:S(2)}, u32[]{:S(2)}) collective-permute-start(bf16[512,512]{1,0:T(8,128)(2,1)} %convolution_convert_fusion.1), channel_id=1, source_target_pairs={{0,1},{1,0},{2,3},{3,2},{4,5},{5,4},{6,7},{7,6},{8,9},{9,8},{10,11... | collective-permute-start | bytes 1572872 | tf_op jit(solution)/shard_map/ppermute | solution.py:792
  147.6 52.5 %collective-permute-start.10 = (bf16[512,1024]{1,0:T(8,128)(2,1)S(1)}, bf16[512,1024]{1,0:T(8,128)(2,1)}, u32[]{:S(2)}, u32[]{:S(2)}) collective-permute-start(bf16[512,1024]{1,0:T(8,128)(2,1)S(1)} %copy-done), channel_id=1, source_target_pairs={{0,1},{1,0},{2,3},{3,2},{4,5},{5,4},{6,7},{7,6},{8,9},{9,8},{10,11... | collective-permute-start | bytes 3145736 | tf_op jit(solution)/shard_map/ppermute | solution.py:792
  149.7 4.9 %copy-start.4 = (bf16[4,1024,256]{2,1,0:T(8,128)(2,1)S(1)}, bf16[4,1024,256]{2,1,0:T(8,128)(2,1)}, u32[]{:S(2)}) copy-start(bf16[4,1024,256]{2,1,0:T(8,128)(2,1)} %get-tuple-element.284) | copy-start | bytes 6291460
  153.4 29.5 %collective-permute-start.11 = (bf16[2,256,1024]{2,1,0:T(8,128)(2,1)}, bf16[2,256,1024]{2,1,0:T(8,128)(2,1)}, u32[]{:S(2)}, u32[]{:S(2)}) collective-permute-start(bf16[2,256,1024]{2,1,0:T(8,128)(2,1)} %get-tuple-element.410), channel_id=1, source_target_pairs={{0,4},{2,6},{4,0},{6,2},{8,12},{10,14},{12,8},{14,10},{16,20},{18,... | collective-permute-start | bytes 3145736 | tf_op jit(solution)/shard_map/ppermute | solution.py:424
  185.5 12.3 %collective-permute-start.12 = (bf16[1,256,1024]{2,1,0:T(8,128)(2,1)}, bf16[1,256,1024]{2,1,0:T(8,128)(2,1)S(1)}, u32[]{:S(2)}, u32[]{:S(2)}) collective-permute-start(bf16[1,256,1024]{2,1,0:T(8,128)(2,1)} %get-tuple-element.417), channel_id=1, source_target_pairs={{0,8},{2,10},{4,12},{6,14},{8,0},{10,2},{12,4},{14,6},{16,24},{18,... | collective-permute-start | bytes 1572872 | tf_op jit(solution)/shard_map/ppermute | solution.py:424
  185.8 31.4 %collective-permute-start.8 = (bf16[2,1024,256]{2,1,0:T(8,128)(2,1)}, bf16[2,1024,256]{2,1,0:T(8,128)(2,1)}, u32[]{:S(2)}, u32[]{:S(2)}) collective-permute-start(bf16[2,1024,256]{2,1,0:T(8,128)(2,1)} %get-tuple-element.407), channel_id=1, source_target_pairs={{0,4},{2,6},{4,0},{6,2},{8,12},{10,14},{12,8},{14,10},{16,20},{18,... | collective-permute-start | bytes 3145736 | tf_op jit(solution)/shard_map/ppermute | solution.py:424
  187.1 11.5 %copy-start.5 = (bf16[1,256,1024]{2,1,0:T(8,128)(2,1)S(1)}, bf16[1,256,1024]{2,1,0:T(8,128)(2,1)}, u32[]{:S(2)}) copy-start(bf16[1,256,1024]{2,1,0:T(8,128)(2,1)} %get-tuple-element.304) | copy-start | bytes 1572868
  194.8 30.4 %collective-permute-start.15 = (bf16[4,2,128,512]{3,2,1,0:T(8,128)(2,1)}, bf16[4,2,128,512]{3,2,1,0:T(8,128)(2,1)}, u32[]{:S(2)}, u32[]{:S(2)}) collective-permute-start(bf16[4,2,128,512]{3,2,1,0:T(8,128)(2,1)} %get-tuple-element.302), channel_id=1, source_target_pairs={{0,2},{2,0},{4,6},{6,4},{8,10},{10,8},{12,14},{14,12},{16,18},{18,... | collective-permute-start | bytes 3145736 | tf_op jit(solution)/shard_map/ppermute | solution.py:424
  199.9 25.0 %collective-permute-start.16 = (bf16[1,256,1024]{2,1,0:T(8,128)(2,1)S(1)}, bf16[1,256,1024]{2,1,0:T(8,128)(2,1)S(1)}, u32[]{:S(2)}, u32[]{:S(2)}) collective-permute-start(bf16[1,256,1024]{2,1,0:T(8,128)(2,1)S(1)} %add_convert_fusion.13), channel_id=1, source_target_pairs={{0,16},{2,18},{4,20},{6,22},{8,24},{10,26},{12,28},{14,30},{16,0},... | collective-permute-start | bytes 1572872 | tf_op jit(solution)/shard_map/ppermute | solution.py:424
  207.6 20.0 %collective-permute-start.14 = (bf16[4,2,128,512]{3,2,1,0:T(8,128)(2,1)}, bf16[4,2,128,512]{3,2,1,0:T(8,128)(2,1)S(1)}, u32[]{:S(2)}, u32[]{:S(2)}) collective-permute-start(bf16[4,2,128,512]{3,2,1,0:T(8,128)(2,1)} %get-tuple-element.312), channel_id=1, source_target_pairs={{0,2},{2,0},{4,6},{6,4},{8,10},{10,8},{12,14},{14,12},{16,18},{18,... | collective-permute-start | bytes 3145736 | tf_op jit(solution)/shard_map/ppermute | solution.py:424
  215.9 9.3 %copy-start.9 = (bf16[4,2,128,512]{3,2,1,0:T(8,128)(2,1)S(1)}, bf16[4,2,128,512]{3,2,1,0:T(8,128)(2,1)}, u32[]{:S(2)}) copy-start(bf16[4,2,128,512]{3,2,1,0:T(8,128)(2,1)} %get-tuple-element.320) | copy-start | bytes 3145732
  215.9 46.1 %collective-permute-start.21 = (bf16[512,1024]{1,0:T(8,128)(2,1)}, bf16[512,1024]{1,0:T(8,128)(2,1)}, u32[]{:S(2)}, u32[]{:S(2)}) collective-permute-start(bf16[512,1024]{1,0:T(8,128)(2,1)} %first_rows.2), channel_id=1, source_target_pairs={{0,1},{1,0},{2,3},{3,2},{4,5},{5,4},{6,7},{7,6},{8,9},{9,8},{10,11... | collective-permute-start | bytes 3145736 | tf_op jit(solution)/shard_map/ppermute | solution.py:792
  218.7 18.6 %collective-permute-start.13 = (bf16[1,1024,256]{2,1,0:T(8,128)(2,1)S(1)}, bf16[1,1024,256]{2,1,0:T(8,128)(2,1)S(1)}, u32[]{:S(2)}, u32[]{:S(2)}) collective-permute-start(bf16[1,1024,256]{2,1,0:T(8,128)(2,1)S(1)} %get-tuple-element.415), channel_id=1, source_target_pairs={{0,8},{2,10},{4,12},{6,14},{8,0},{10,2},{12,4},{14,6},{16,24},{18,... | collective-permute-start | bytes 1572872 | tf_op jit(solution)/shard_map/ppermute | solution.py:424
  225.1 28.3 %collective-permute-start.20 = (bf16[1,256,1024]{2,1,0:T(8,128)(2,1)S(1)}, bf16[1,256,1024]{2,1,0:T(8,128)(2,1)S(1)}, u32[]{:S(2)}, u32[]{:S(2)}) collective-permute-start(bf16[1,256,1024]{2,1,0:T(8,128)(2,1)S(1)} %add_convert_fusion.10), channel_id=1, source_target_pairs={{0,8},{2,10},{4,12},{6,14},{8,0},{10,2},{12,4},{14,6},{16,24},{18,... | collective-permute-start | bytes 1572872 | tf_op jit(solution)/shard_map/ppermute | solution.py:424
  226.8 28.0 %collective-permute-start.19 = (bf16[2,2,128,512]{3,2,1,0:T(8,128)(2,1)S(1)}, bf16[2,2,128,512]{3,2,1,0:T(8,128)(2,1)S(1)}, u32[]{:S(2)}, u32[]{:S(2)}) collective-permute-start(bf16[2,2,128,512]{3,2,1,0:T(8,128)(2,1)S(1)} %get-tuple-element.414), channel_id=1, source_target_pairs={{0,4},{2,6},{4,0},{6,2},{8,12},{10,14},{12,8},{14,10},{16,20},{18,... | collective-permute-start | bytes 1572872 | tf_op jit(solution)/shard_map/ppermute | solution.py:424
  227.9 27.7 %collective-permute-start.18 = (bf16[2,2,128,512]{3,2,1,0:T(8,128)(2,1)S(1)}, bf16[2,2,128,512]{3,2,1,0:T(8,128)(2,1)S(1)}, u32[]{:S(2)}, u32[]{:S(2)}) collective-permute-start(bf16[2,2,128,512]{3,2,1,0:T(8,128)(2,1)S(1)} %get-tuple-element.412), channel_id=1, source_target_pairs={{0,4},{2,6},{4,0},{6,2},{8,12},{10,14},{12,8},{14,10},{16,20},{18,... | collective-permute-start | bytes 1572872 | tf_op jit(solution)/shard_map/ppermute | solution.py:424
  237.5 30.5 %collective-permute-start.17 = (bf16[1,1024,256]{2,1,0:T(8,128)(2,1)S(1)}, bf16[1,1024,256]{2,1,0:T(8,128)(2,1)S(1)}, u32[]{:S(2)}, u32[]{:S(2)}) collective-permute-start(bf16[1,1024,256]{2,1,0:T(8,128)(2,1)S(1)} %add_convert_fusion.5), channel_id=1, source_target_pairs={{0,16},{2,18},{4,20},{6,22},{8,24},{10,26},{12,28},{14,30},{16,0},... | collective-permute-start | bytes 1572872 | tf_op jit(solution)/shard_map/ppermute | solution.py:424
  253.4 22.6 %copy-start.1 = (bf16[2,256,1024]{2,1,0:T(8,128)(2,1)}, bf16[2,256,1024]{2,1,0:T(8,128)(2,1)S(1)}, u32[]{:S(2)}) copy-start(bf16[2,256,1024]{2,1,0:T(8,128)(2,1)S(1)} %constant_dynamic-update-slice_fusion.refs_0_) | copy-start | bytes 3145732
  253.5 24.4 %collective-permute-start.30 = (bf16[2,256,1024]{2,1,0:T(8,128)(2,1)S(1)}, bf16[2,256,1024]{2,1,0:T(8,128)(2,1)}, u32[]{:S(2)}, u32[]{:S(2)}) collective-permute-start(bf16[2,256,1024]{2,1,0:T(8,128)(2,1)S(1)} %constant_dynamic-update-slice_fusion.refs_0_), channel_id=1, source_target_pairs={{0,4},{2,6},{4,0},{6,2},{8,12},{10,14},{12,8},{14,10},{16,20},{18,... | collective-permute-start | bytes 3145736 | tf_op jit(solution)/shard_map/ppermute | solution.py:424
  256.4 19.9 %collective-permute-start.23 = (bf16[1,2,128,512]{3,2,1,0:T(8,128)(2,1)}, bf16[1,2,128,512]{3,2,1,0:T(8,128)(2,1)S(1)}, u32[]{:S(2)}, u32[]{:S(2)}) collective-permute-start(bf16[1,2,128,512]{3,2,1,0:T(8,128)(2,1)} %get-tuple-element.420), channel_id=1, source_target_pairs={{0,8},{2,10},{4,12},{6,14},{8,0},{10,2},{12,4},{14,6},{16,24},{18,... | collective-permute-start | bytes 786440 | tf_op jit(solution)/shard_map/ppermute | solution.py:424
  262.0 10.9 %copy-start.23 = (f32[1,2048]{1,0:T(1,128)S(1)}, f32[1,2048]{1,0:T(1,128)}, u32[]{:S(2)}) copy-start(f32[1,2048]{1,0:T(1,128)} %get-tuple-element.346) | copy-start | bytes 24580
  262.0 10.9 %copy-start.24 = (f32[1,2048]{1,0:T(1,128)S(1)}, f32[1,2048]{1,0:T(1,128)}, u32[]{:S(2)}) copy-start(f32[1,2048]{1,0:T(1,128)} %get-tuple-element.345) | copy-start | bytes 24580
  268.1 18.5 %collective-permute-start.22 = (bf16[1,1024,256]{2,1,0:T(8,128)(2,1)S(1)}, bf16[1,1024,256]{2,1,0:T(8,128)(2,1)}, u32[]{:S(2)}, u32[]{:S(2)}) collective-permute-start(bf16[1,1024,256]{2,1,0:T(8,128)(2,1)S(1)} %add_convert_fusion.4), channel_id=1, source_target_pairs={{0,8},{2,10},{4,12},{6,14},{8,0},{10,2},{12,4},{14,6},{16,24},{18,... | collective-permute-start | bytes 1572872 | tf_op jit(solution)/shard_map/ppermute | solution.py:424
  269.7 3.2 collective-permute-start.24
  273.0 3.0 collective-permute-start.25
  275.1 18.5 %collective-permute-start.27 = (bf16[1,2,128,512]{3,2,1,0:T(8,128)(2,1)}, bf16[1,2,128,512]{3,2,1,0:T(8,128)(2,1)S(1)}, u32[]{:S(2)}, u32[]{:S(2)}) collective-permute-start(bf16[1,2,128,512]{3,2,1,0:T(8,128)(2,1)} %get-tuple-element.422), channel_id=1, source_target_pairs={{0,8},{2,10},{4,12},{6,14},{8,0},{10,2},{12,4},{14,6},{16,24},{18,... | collective-permute-start | bytes 786440 | tf_op jit(solution)/shard_map/ppermute | solution.py:424
  276.0 18.0 %collective-permute-start.29 = (bf16[2,256,1024]{2,1,0:T(8,128)(2,1)S(1)}, bf16[2,256,1024]{2,1,0:T(8,128)(2,1)}, u32[]{:S(2)}, u32[]{:S(2)}) collective-permute-start(bf16[2,256,1024]{2,1,0:T(8,128)(2,1)S(1)} %constant_dynamic-update-slice_fusion.refs_0_), channel_id=1, source_target_pairs={{0,2},{2,0},{4,6},{6,4},{8,10},{10,8},{12,14},{14,12},{16,18},{18,... | collective-permute-start | bytes 3145736 | tf_op jit(solution)/shard_map/ppermute | solution.py:424
  276.4 22.0 %collective-permute-start.32 = (bf16[1,2,128,512]{3,2,1,0:T(8,128)(2,1)S(1)}, bf16[1,2,128,512]{3,2,1,0:T(8,128)(2,1)}, u32[]{:S(2)}, u32[]{:S(2)}) collective-permute-start(bf16[1,2,128,512]{3,2,1,0:T(8,128)(2,1)S(1)} %add_convert_fusion.19), channel_id=1, source_target_pairs={{0,16},{2,18},{4,20},{6,22},{8,24},{10,26},{12,28},{14,30},{16,0},... | collective-permute-start | bytes 786440 | tf_op jit(solution)/shard_map/ppermute | solution.py:424
  277.9 22.8 %collective-permute-start.31 = (bf16[2,256,1024]{2,1,0:T(8,128)(2,1)}, bf16[2,256,1024]{2,1,0:T(8,128)(2,1)}, u32[]{:S(2)}, u32[]{:S(2)}) collective-permute-start(bf16[2,256,1024]{2,1,0:T(8,128)(2,1)} %collective-permute-done.30.refs_1_), channel_id=1, source_target_pairs={{0,2},{2,0},{4,6},{6,4},{8,10},{10,8},{12,14},{14,12},{16,18},{18,... | collective-permute-start | bytes 3145736 | tf_op jit(solution)/shard_map/ppermute | solution.py:424
  287.7 22.7 %copy-start.2 = (bf16[2,1024,256]{2,1,0:T(8,128)(2,1)}, bf16[2,1024,256]{2,1,0:T(8,128)(2,1)S(1)}, u32[]{:S(2)}) copy-start(bf16[2,1024,256]{2,1,0:T(8,128)(2,1)S(1)} %constant_dynamic-update-slice_fusion.2.refs_0_) | copy-start | bytes 3145732
  287.7 26.5 %collective-permute-start.38 = (bf16[2,1024,256]{2,1,0:T(8,128)(2,1)S(1)}, bf16[2,1024,256]{2,1,0:T(8,128)(2,1)}, u32[]{:S(2)}, u32[]{:S(2)}) collective-permute-start(bf16[2,1024,256]{2,1,0:T(8,128)(2,1)S(1)} %constant_dynamic-update-slice_fusion.2.refs_0_), channel_id=1, source_target_pairs={{0,4},{2,6},{4,0},{6,2},{8,12},{10,14},{12,8},{14,10},{16,20},{18,... | collective-permute-start | bytes 3145736 | tf_op jit(solution)/shard_map/ppermute | solution.py:424
  293.6 25.3 %collective-permute-start.26 = (bf16[512,1024]{1,0:T(8,128)(2,1)}, bf16[512,1024]{1,0:T(8,128)(2,1)}, u32[]{:S(2)}, u32[]{:S(2)}) collective-permute-start(bf16[512,1024]{1,0:T(8,128)(2,1)} %reduced.1), channel_id=1, source_target_pairs={{0,1},{1,0},{2,3},{3,2},{4,5},{5,4},{6,7},{7,6},{8,9},{9,8},{10,11... | collective-permute-start | bytes 3145736 | tf_op jit(solution)/shard_map/ppermute | solution.py:792
  294.0 11.4 %collective-permute-start.28 = (bf16[1,2,128,512]{3,2,1,0:T(8,128)(2,1)S(1)}, bf16[1,2,128,512]{3,2,1,0:T(8,128)(2,1)S(1)}, u32[]{:S(2)}, u32[]{:S(2)}) collective-permute-start(bf16[1,2,128,512]{3,2,1,0:T(8,128)(2,1)S(1)} %add_convert_fusion.18), channel_id=1, source_target_pairs={{0,16},{2,18},{4,20},{6,22},{8,24},{10,26},{12,28},{14,30},{16,0},... | collective-permute-start | bytes 786440 | tf_op jit(solution)/shard_map/ppermute | solution.py:424
  298.5 11.9 %collective-permute-start.35 = (f32[58,128]{1,0:T(8,128)S(1)}, f32[58,128]{1,0:T(8,128)S(1)}, u32[]{:S(2)}, u32[]{:S(2)}) collective-permute-start(f32[58,128]{1,0:T(8,128)S(1)} %add.176), channel_id=1, source_target_pairs={{0,4},{2,6},{4,0},{6,2},{8,12},{10,14},{12,8},{14,10},{16,20},{18,... | collective-permute-start | bytes 89096 | tf_op jit(solution)/shard_map/ppermute | solution.py:424
  300.7 13.4 %collective-permute-start.34 = (bf16[1,2,128,512]{3,2,1,0:T(8,128)(2,1)S(1)}, bf16[1,2,128,512]{3,2,1,0:T(8,128)(2,1)S(1)}, u32[]{:S(2)}, u32[]{:S(2)}) collective-permute-start(bf16[1,2,128,512]{3,2,1,0:T(8,128)(2,1)S(1)} %add_convert_fusion.17), channel_id=1, source_target_pairs={{0,8},{2,10},{4,12},{6,14},{8,0},{10,2},{12,4},{14,6},{16,24},{18,... | collective-permute-start | bytes 786440 | tf_op jit(solution)/shard_map/ppermute | solution.py:424
  305.5 11.8 %collective-permute-start.33 = (bf16[1,2,128,512]{3,2,1,0:T(8,128)(2,1)S(1)}, bf16[1,2,128,512]{3,2,1,0:T(8,128)(2,1)S(1)}, u32[]{:S(2)}, u32[]{:S(2)}) collective-permute-start(bf16[1,2,128,512]{3,2,1,0:T(8,128)(2,1)S(1)} %add_convert_fusion.16), channel_id=1, source_target_pairs={{0,8},{2,10},{4,12},{6,14},{8,0},{10,2},{12,4},{14,6},{16,24},{18,... | collective-permute-start | bytes 786440 | tf_op jit(solution)/shard_map/ppermute | solution.py:424
  310.4 16.7 %collective-permute-start.37 = (bf16[2,1024,256]{2,1,0:T(8,128)(2,1)S(1)}, bf16[2,1024,256]{2,1,0:T(8,128)(2,1)}, u32[]{:S(2)}, u32[]{:S(2)}) collective-permute-start(bf16[2,1024,256]{2,1,0:T(8,128)(2,1)S(1)} %constant_dynamic-update-slice_fusion.2.refs_0_), channel_id=1, source_target_pairs={{0,2},{2,0},{4,6},{6,4},{8,10},{10,8},{12,14},{14,12},{16,18},{18,... | collective-permute-start | bytes 3145736 | tf_op jit(solution)/shard_map/ppermute | solution.py:424
  314.1 23.9 %collective-permute-start.36 = (f32[58,128]{1,0:T(8,128)S(1)}, f32[58,128]{1,0:T(8,128)S(1)}, u32[]{:S(2)}, u32[]{:S(2)}) collective-permute-start(f32[58,128]{1,0:T(8,128)S(1)} %add.181), channel_id=1, source_target_pairs={{0,8},{2,10},{4,12},{6,14},{8,0},{10,2},{12,4},{14,6},{16,24},{18,... | collective-permute-start | bytes 89096 | tf_op jit(solution)/shard_map/ppermute | solution.py:424
  314.2 12.9 %copy-start.6 = (bf16[2,2,128,512]{3,2,1,0:T(8,128)(2,1)}, bf16[2,2,128,512]{3,2,1,0:T(8,128)(2,1)S(1)}, u32[]{:S(2)}) copy-start(bf16[2,2,128,512]{3,2,1,0:T(8,128)(2,1)S(1)} %constant_dynamic-update-slice_fusion.4.refs_2_) | copy-start | bytes 1572868
  314.3 18.2 %collective-permute-start.45 = (bf16[2,2,128,512]{3,2,1,0:T(8,128)(2,1)S(1)}, bf16[2,2,128,512]{3,2,1,0:T(8,128)(2,1)}, u32[]{:S(2)}, u32[]{:S(2)}) collective-permute-start(bf16[2,2,128,512]{3,2,1,0:T(8,128)(2,1)S(1)} %constant_dynamic-update-slice_fusion.4.refs_2_), channel_id=1, source_target_pairs={{0,4},{2,6},{4,0},{6,2},{8,12},{10,14},{12,8},{14,10},{16,20},{18,... | collective-permute-start | bytes 1572872 | tf_op jit(solution)/shard_map/ppermute | solution.py:424
  317.3 15.2 %collective-permute-start.39 = (bf16[2,1024,256]{2,1,0:T(8,128)(2,1)}, bf16[2,1024,256]{2,1,0:T(8,128)(2,1)S(1)}, u32[]{:S(2)}, u32[]{:S(2)}) collective-permute-start(bf16[2,1024,256]{2,1,0:T(8,128)(2,1)} %collective-permute-done.38.refs_1_), channel_id=1, source_target_pairs={{0,2},{2,0},{4,6},{6,4},{8,10},{10,8},{12,14},{14,12},{16,18},{18,... | collective-permute-start | bytes 3145736 | tf_op jit(solution)/shard_map/ppermute | solution.py:424
  318.9 13.6 %copy-start.7 = (bf16[2,2,128,512]{3,2,1,0:T(8,128)(2,1)}, bf16[2,2,128,512]{3,2,1,0:T(8,128)(2,1)S(1)}, u32[]{:S(2)}) copy-start(bf16[2,2,128,512]{3,2,1,0:T(8,128)(2,1)S(1)} %constant_dynamic-update-slice_fusion.6.refs_0_) | copy-start | bytes 1572868
  318.9 20.3 %collective-permute-start.43 = (bf16[2,2,128,512]{3,2,1,0:T(8,128)(2,1)S(1)}, bf16[2,2,128,512]{3,2,1,0:T(8,128)(2,1)}, u32[]{:S(2)}, u32[]{:S(2)}) collective-permute-start(bf16[2,2,128,512]{3,2,1,0:T(8,128)(2,1)S(1)} %constant_dynamic-update-slice_fusion.6.refs_0_), channel_id=1, source_target_pairs={{0,4},{2,6},{4,0},{6,2},{8,12},{10,14},{12,8},{14,10},{16,20},{18,... | collective-permute-start | bytes 1572872 | tf_op jit(solution)/shard_map/ppermute | solution.py:424
  327.1 13.4 %collective-permute-start.42 = (bf16[2,2,128,512]{3,2,1,0:T(8,128)(2,1)S(1)}, bf16[2,2,128,512]{3,2,1,0:T(8,128)(2,1)S(1)}, u32[]{:S(2)}, u32[]{:S(2)}) collective-permute-start(bf16[2,2,128,512]{3,2,1,0:T(8,128)(2,1)S(1)} %constant_dynamic-update-slice_fusion.4.refs_2_), channel_id=1, source_target_pairs={{0,2},{2,0},{4,6},{6,4},{8,10},{10,8},{12,14},{14,12},{16,18},{18,... | collective-permute-start | bytes 1572872 | tf_op jit(solution)/shard_map/ppermute | solution.py:424
  332.5 8.0 %collective-permute-start.41 = (bf16[2,2,128,512]{3,2,1,0:T(8,128)(2,1)S(1)}, bf16[2,2,128,512]{3,2,1,0:T(8,128)(2,1)S(1)}, u32[]{:S(2)}, u32[]{:S(2)}) collective-permute-start(bf16[2,2,128,512]{3,2,1,0:T(8,128)(2,1)S(1)} %constant_dynamic-update-slice_fusion.6.refs_0_), channel_id=1, source_target_pairs={{0,2},{2,0},{4,6},{6,4},{8,10},{10,8},{12,14},{14,12},{16,18},{18,... | collective-permute-start | bytes 1572872 | tf_op jit(solution)/shard_map/ppermute | solution.py:424
  332.5 14.1 %collective-permute-start.46 = (bf16[2,2,128,512]{3,2,1,0:T(8,128)(2,1)}, bf16[2,2,128,512]{3,2,1,0:T(8,128)(2,1)}, u32[]{:S(2)}, u32[]{:S(2)}) collective-permute-start(bf16[2,2,128,512]{3,2,1,0:T(8,128)(2,1)} %collective-permute-done.45.refs_4_), channel_id=1, source_target_pairs={{0,2},{2,0},{4,6},{6,4},{8,10},{10,8},{12,14},{14,12},{16,18},{18,... | collective-permute-start | bytes 1572872 | tf_op jit(solution)/shard_map/ppermute | solution.py:424
  339.2 7.4 %collective-permute-start.44 = (bf16[2,2,128,512]{3,2,1,0:T(8,128)(2,1)}, bf16[2,2,128,512]{3,2,1,0:T(8,128)(2,1)S(1)}, u32[]{:S(2)}, u32[]{:S(2)}) collective-permute-start(bf16[2,2,128,512]{3,2,1,0:T(8,128)(2,1)} %collective-permute-done.43.refs_2_), channel_id=1, source_target_pairs={{0,2},{2,0},{4,6},{6,4},{8,10},{10,8},{12,14},{14,12},{16,18},{18,... | collective-permute-start | bytes 1572872 | tf_op jit(solution)/shard_map/ppermute | solution.py:424
  340.0 12.0 %collective-permute-start.40 = (f32[58,128]{1,0:T(8,128)S(1)}, f32[58,128]{1,0:T(8,128)S(1)}, u32[]{:S(2)}, u32[]{:S(2)}) collective-permute-start(f32[58,128]{1,0:T(8,128)S(1)} %add.182), channel_id=1, source_target_pairs={{0,16},{2,18},{4,20},{6,22},{8,24},{10,26},{12,28},{14,30},{16,0},... | collective-permute-start | bytes 89096 | tf_op jit(solution)/shard_map/ppermute | solution.py:424
  (12 other events, 20.4 us)

commit v3 on v2

--- a/solution.py
+++ b/solution.py
@@ -624,7 +624,7 @@
         sums_ref[...] = jnp.zeros_like(sums_ref)
 
     def some(i, _):
-        rows = pl.ds(pl.multiple_of(i * 64, 64), 64)
+        rows = pl.ds(pl.multiple_of(i * 128, 128), 128)
         normed, inverse = row_norm(source_ref[rows, :].astype(F32))
         grad = a_ref[rows, :].astype(F32) + b_ref[rows, :].astype(F32)
         add = add_ref[rows, :].astype(F32)
@@ -637,7 +637,7 @@
             sums_ref[k:k + 1] += jnp.sum(value, axis=0, keepdims=True)
         return 0
 
-    lax.fori_loop(0, source_ref.shape[0] // 64, some, 0)
+    lax.fori_loop(0, source_ref.shape[0] // 128, some, 0)
 
 
 def back_rows(a, b, source, add, gain):
@@ -687,8 +687,11 @@
     for a in range(2):
         @pl.when(g == a)
         def _(a=a):
-            for j in range(2):
+            def one(j, _):
                 put([piece.at[j] for piece in pieces[a::2]], outs, j ^ (s_ref[0] % 2))
+                return 0
+
+            lax.fori_loop(0, 2, one, 0)
 
 
 def spread(places, part, pieces, put, tail, out_specs, out_shape, given=None, name=None):

time: 359 us -> 358 us (level)
  transfers between devices with their start and end apart: 47 -> 47, of which waited for: 14 -> 15; matrix products, arithmetic and copies ran while one was open for 8% -> 8% of each run, Pallas kernels for 49% -> 48%
where the time goes in v3:
time: 358 us; the launch traced here: 354 us
  Pallas kernels  190 us (53%)
  waiting for transfers between devices  81.8 us (23%)
  starting transfers between devices  44.2 us (12%)
  other arithmetic  21 us (6%)
  local copies, waits for them, and re-layouts  10.7 us (3%)
  matrix products  4.31 us (1%)
    ppermute x37, waiting for transfers between devices, trade(): return lax.ppermute(x, 'dp', [(i, i ^ bit) for i in range(size)])  47.6 us
    pallas_call x4, Pallas kernels, pair_call(): pl.pallas_call(functools.partial(kernel, slot), grid_spec=pltpu.PrefetchS...  34.8 us
    ppermute x37, starting transfers between devices, trade(): return lax.ppermute(x, 'dp', [(i, i ^ bit) for i in range(size)])  34.6 us
    ppermute x10, waiting for transfers between devices, swap(): return lax.ppermute(x, 'mp', [(0, 1), (1, 0)])  34.2 us
    pallas_call x6, Pallas kernels, spread(): pl.pallas_call(functools.partial(spread_kernel, put), grid_spec=pltpu.Pre...  27.1 us
    pallas_call x2, Pallas kernels, expand(): pl.pallas_call(expand_kernel, grid=(hidden // step,), in_specs=[pl.BlockS...  23.4 us
    pallas_call x1, Pallas kernels, attend_backward(): pl.pallas_call(kernel, grid_spec=pltpu.PrefetchScalarGridSpec(num_scalar_...  22.8 us
    pallas_call x3, Pallas kernels, columns_dot(): pl.pallas_call(functools.partial(columns_kernel, turn), grid=(columns //...  17.9 us
  transfers between devices with their start and end apart: 47, of which 15 were waited for; matrix products, arithmetic and copies ran while one was open for 8% of the time, Pallas kernels for 48%

profile of v3, /device:TPU:25, one launch (start us, length us, event | category | flops | bytes accessed | tf_op | source)
XLA Modules:
  0.0 354.3 jit_solution(9021399632706226466)
XLA Ops:
  0.6 1.3 collective-permute-start
  2.6 2.3 broadcast_select_fusion.1.a_ref.refs_2_.add_ref
  5.0 5.5 %project.2 = (bf16[512,1024]{1,0:T(8,128)(2,1)}, bf16[3,512,512]{2,1,0:T(8,128)(2,1)}) custom-call(bf16[512,1024]{1,0:T(8,128)(2,1)} %source_ref, f32[1,1024]{1,0:T(1,128)} %bitcast.35, f32[1,1024]{1,0:T(1,128)} %bitcast.38, bf16[3,1024,512]{2,1,0:T(8,128)(2,1)} %w_ref.6), custom_call_target="tpu_custom_call" | custom-call | flops 25769803776 | bytes 109051904 | tf_op jit(solution)/shard_map/project/pallas_call | solution.py:291
  10.5 6.3 %active_grad.2.g_ref = bf16[512,2048]{1,0:T(8,128)(2,1)} custom-call(bf16[512,1024]{1,0:T(8,128)(2,1)} %broadcast_select_fusion.1.a_ref.refs_2_.add_ref, bf16[2048,1024]{1,0:T(8,128)(2,1)} %w_ref.7), custom_call_target="tpu_custom_call" | custom-call | flops 34359738368 | bytes 117440512 | tf_op jit(solution)/shard_map/active_grad/pallas_call | solution.py:551
  16.7 1.5 bias_rows.1.b_ref
  18.9 6.2 %collective-permute-done.x_ref.x1_ref = bf16[512,1024]{1,0:T(8,128)(2,1)} collective-permute-done((bf16[512,1024]{1,0:T(8,128)(2,1)}, bf16[512,1024]{1,0:T(8,128)(2,1)}, u32[]{:S(2)}, u32[]{:S(2)}) %collective-permute-start) | collective-permute-done | bytes 1048608 | tf_op jit(solution)/shard_map/ppermute | solution.py:795
  26.5 5.5 %project.3 = (bf16[512,1024]{1,0:T(8,128)(2,1)}, bf16[3,512,512]{2,1,0:T(8,128)(2,1)}) custom-call(bf16[512,1024]{1,0:T(8,128)(2,1)} %collective-permute-done.x_ref.x1_ref, f32[1,1024]{1,0:T(1,128)} %bitcast.36, f32[1,1024]{1,0:T(1,128)} %bitcast.39, bf16[3,1024,512]{2,1,0:T(8,128)(2,1)} %w_ref.6), custom_call_target="tpu_custom_call" | custom-call | flops 25769803776 | bytes 109051904 | tf_op jit(solution)/shard_map/project/pallas_call | solution.py:291
  32.1 14.4 %attend_forward.1 = (bf16[1024,512]{1,0:T(8,128)(2,1)}, f32[4,1024,128]{2,1,0:T(8,128)}) custom-call(s32[2]{0:T(128)} %pad_add_fusion.sp, bf16[3,512,512]{2,1,0:T(8,128)(2,1)} %get-tuple-element.287.a_ref, bf16[3,512,512]{2,1,0:T(8,128)(2,1)} %get-tuple-element.288.c_ref, f32[4,2,2048]{2,1,0:T(2,128)} %bias_rows.1.b_ref), custom_call_target="tpu_custom_call" | custom-call | flops 4294967296 | bytes 6291456 | tf_op jit(solution)/shard_map/attend_forward/pallas_call | solution.py:124
  46.4 2.2 collective-permute-start.3
  49.2 1.3 collective-permute-start.1
  51.3 2.2 order_rows.1.w1_ref
  53.5 5.9 %collective-permute-done.4 = bf16[512,1024]{1,0:T(8,128)(2,1)S(1)} collective-permute-done((bf16[512,1024]{1,0:T(8,128)(2,1)S(1)}, bf16[512,1024]{1,0:T(8,128)(2,1)S(1)}, u32[]{:S(2)}, u32[]{:S(2)}) %collective-permute-start.4) | collective-permute-done | bytes 1048608 | tf_op jit(solution)/shard_map/ppermute | solution.py:795
  60.5 6.1 %active_grad.3.g_ref = bf16[512,2048]{1,0:T(8,128)(2,1)} custom-call(bf16[512,1024]{1,0:T(8,128)(2,1)} %broadcast_select_fusion.a_ref.refs_3_, bf16[2048,1024]{1,0:T(8,128)(2,1)} %w_ref.7), custom_call_target="tpu_custom_call" | custom-call | flops 34359738368 | bytes 117440512 | tf_op jit(solution)/shard_map/active_grad/pallas_call | solution.py:551
  66.6 15.3 %collective-permute-done.1.p_ref = bf16[1024,512]{1,0:T(8,128)(2,1)} collective-permute-done((bf16[1024,512]{1,0:T(8,128)(2,1)}, bf16[1024,512]{1,0:T(8,128)(2,1)}, u32[]{:S(2)}, u32[]{:S(2)}) %collective-permute-start.1) | collective-permute-done | bytes 1048608 | tf_op jit(solution)/shard_map/ppermute | solution.py:795
  82.0 7.8 %mix.1 = (bf16[512,1024]{1,0:T(8,128)(2,1)}, bf16[1024,1024]{1,0:T(8,128)(2,1)}) custom-call(bf16[512,1024]{1,0:T(8,128)(2,1)} %source_ref, bf16[512,1024]{1,0:T(8,128)(2,1)} %collective-permute-done.x_ref.x1_ref, bf16[1024,512]{1,0:T(8,128)(2,1)} %get-tuple-element.311.m_ref.o_ref.refs_5_, bf16[1024,512]{1,0:T(8,128)(2,1)} %collective-permute-done.1.p_ref, ...), custom_call_target="tpu_custom_call" | custom-call | flops 8589934592 | bytes 41943040 | tf_op jit(solution)/shard_map/mix/pallas_call | solution.py:329
  89.8 11.7 %expand.2 = (bf16[512,2048]{1,0:T(8,128)(2,1)}, bf16[512,2048]{1,0:T(8,128)(2,1)}, bf16[512,1024]{1,0:T(8,128)(2,1)}, f32[1,2048]{1,0:T(1,128)}) custom-call(bf16[1024,1024]{1,0:T(8,128)(2,1)} %get-tuple-element.275.x_ref.refs_0_, bf16[512,2048]{1,0:T(8,128)(2,1)} %active_grad.3.g_ref, bf16[1024,2048]{1,0:T(8,128)(2,1)} %w_ref.4, bf16[1,2048]{1,0:T(2,128)(2,1)} %reshape.162.b_ref), custom_call_target="tpu_custom_call" | custom-call | flops 4294967296 | bytes 12582912 | tf_op jit(solution)/shard_map/expand/pallas_call | solution.py:387
  101.5 1.3 collective-permute-start.5
  103.4 11.6 %expand.3 = (bf16[512,2048]{1,0:T(8,128)(2,1)}, bf16[512,2048]{1,0:T(8,128)(2,1)}, bf16[512,1024]{1,0:T(8,128)(2,1)}, f32[1,2048]{1,0:T(1,128)}) custom-call(bf16[1024,1024]{1,0:T(8,128)(2,1)} %get-tuple-element.275.x_ref.refs_0_, bf16[512,2048]{1,0:T(8,128)(2,1)} %active_grad.2.g_ref, bf16[1024,2048]{1,0:T(8,128)(2,1)} %w_ref.4, bf16[1,2048]{1,0:T(2,128)(2,1)} %reshape.162.b_ref), custom_call_target="tpu_custom_call" | custom-call | flops 4294967296 | bytes 12582912 | tf_op jit(solution)/shard_map/expand/pallas_call | solution.py:387
  115.0 9.8 %reduce_grad.1 = (bf16[4,256,1024]{2,1,0:T(8,128)(2,1)}, bf16[4,256,1024]{2,1,0:T(8,128)(2,1)}) custom-call(s32[2]{0:T(128)} %pad_add_fusion.1.s_ref, bf16[512,2048]{1,0:T(8,128)(2,1)} %get-tuple-element.375.refs_0_.a_ref, bf16[512,2048]{1,0:T(8,128)(2,1)} %get-tuple-element.354.refs_1_.a_ref, ...), custom_call_target="tpu_custom_call" | custom-call | flops 4294967296 | bytes 10485760 | tf_op jit(solution)/shard_map/reduce_grad/pallas_call | solution.py:449
  124.9 2.8 collective-permute-start.7
  128.6 4.7 %back_rows.2 = (bf16[512,1024]{1,0:T(8,128)(2,1)}, f32[8,1024]{1,0:T(8,128)}) custom-call(bf16[512,1024]{1,0:T(8,128)(2,1)} %get-tuple-element.266.a_ref, bf16[512,1024]{1,0:T(8,128)(2,1)} %copy-done.8, bf16[512,1024]{1,0:T(8,128)(2,1)} %get-tuple-element.374.source_ref.m_ref, bf16[512,1024]{1,0:T(8,128)(2,1)} %broadcast_select_fusion.1.a_ref.refs_2_.add_ref, ...), custom_call_target="tpu_custom_call" | custom-call | flops 15728640 | bytes 5242880 | tf_op jit(solution)/shard_map/back_rows/pallas_call | solution.py:647
  133.3 2.8 convolution_convert_fusion.1
  136.1 10.0 %expand_grad.1 = (bf16[4,1024,256]{2,1,0:T(8,128)(2,1)}, bf16[4,1024,256]{2,1,0:T(8,128)(2,1)}) custom-call(s32[2]{0:T(128)} %pad_add_fusion.1.s_ref, bf16[1024,1024]{1,0:T(8,128)(2,1)} %get-tuple-element.275.x_ref.refs_0_, bf16[512,2048]{1,0:T(8,128)(2,1)} %get-tuple-element.276.refs_1_, bf16[512,2048]{1,0:T(8,128)(2,1)} %get-tuple-element.277.refs_2_), custom_call_target="tpu_custom_call" | custom-call | flops 4294967296 | bytes 10485760 | tf_op jit(solution)/shard_map/expand_grad/pallas_call | solution.py:449
  147.6 1.5 convolution_convert_fusion.d0_ref
  149.2 3.7 %add_convert_fusion.2 = (bf16[2,256,1024]{2,1,0:T(8,128)(2,1)S(1)}, bf16[2,256,1024]{2,1,0:T(8,128)(2,1)}) fusion(bf16[4,256,1024]{2,1,0:T(8,128)(2,1)} %collective-permute-done.7, bf16[4,256,1024]{2,1,0:T(8,128)(2,1)S(1)} %copy-done.3), kind=kLoop, calls=%fused_computation.2 | loop fusion | flops 4194304 | bytes 6291456 | tf_op jit(solution)/shard_map/convert_element_type | solution.py:428
  154.1 1.6 add_convert_fusion
  155.6 3.9 %collective-permute-done.9.d1_ref = bf16[512,512]{1,0:T(8,128)(2,1)} collective-permute-done((bf16[512,512]{1,0:T(8,128)(2,1)}, bf16[512,512]{1,0:T(8,128)(2,1)}, u32[]{:S(2)}, u32[]{:S(2)}) %collective-permute-start.9) | collective-permute-done | bytes 524320 | tf_op jit(solution)/shard_map/ppermute | solution.py:795
  159.5 22.8 %attend_backward.1 = (bf16[3,1024,512]{2,1,0:T(8,128)(2,1)}, f32[4,4,512]{2,1,0:T(4,128)}) custom-call(s32[2]{0:T(128)} %pad_add_fusion.sp, bf16[3,512,512]{2,1,0:T(8,128)(2,1)} %get-tuple-element.287.a_ref, bf16[3,512,512]{2,1,0:T(8,128)(2,1)} %get-tuple-element.288.c_ref, bf16[512,512]{1,0:T(8,128)(2,1)} %convolution_convert_fusion.d0_ref, ...), custom_call_target="tpu_custom_call" | custom-call | flops 10737418240 | bytes 10485760 | tf_op jit(solution)/shard_map/attend_backward/pallas_call | solution.py:225
  182.3 2.7 add_convert_fusion.14
  185.3 1.3 collective-permute-start.8
  186.6 7.5 %heads_grad.1 = (bf16[4,2,128,512]{3,2,1,0:T(8,128)(2,1)}, bf16[4,2,128,512]{3,2,1,0:T(8,128)(2,1)}) custom-call(s32[2]{0:T(128)} %pad_add_fusion.1.s_ref, bf16[512,1024]{1,0:T(8,128)(2,1)} %get-tuple-element.306.refs_0_, bf16[512,1024]{1,0:T(8,128)(2,1)} %get-tuple-element.307.refs_1_, bf16[3,1024,512]{2,1,0:T(8,128)(2,1)} %get-tuple-element.332.refs_2_.g_ref), custom_call_target="tpu_custom_call" | custom-call | flops 2147483648 | bytes 7340032 | tf_op jit(solution)/shard_map/heads_grad/pallas_call | solution.py:449
  194.3 2.7 collective-permute-start.15
  199.5 7.6 %values_grad.1 = (bf16[4,2,128,512]{3,2,1,0:T(8,128)(2,1)}, bf16[4,2,128,512]{3,2,1,0:T(8,128)(2,1)}) custom-call(s32[2]{0:T(128)} %pad_add_fusion.1.s_ref, bf16[512,1024]{1,0:T(8,128)(2,1)} %get-tuple-element.306.refs_0_, bf16[512,1024]{1,0:T(8,128)(2,1)} %get-tuple-element.307.refs_1_, bf16[3,1024,512]{2,1,0:T(8,128)(2,1)} %get-tuple-element.332.refs_2_.g_ref, ...), custom_call_target="tpu_custom_call" | custom-call | flops 2147483648 | bytes 10485760 | tf_op jit(solution)/shard_map/values_grad/pallas_call | solution.py:449
  207.1 2.5 collective-permute-start.14
  209.8 5.6 %first_rows.2 = bf16[512,1024]{1,0:T(8,128)(2,1)} custom-call(bf16[3,1024,512]{2,1,0:T(8,128)(2,1)} %get-tuple-element.332.refs_2_.g_ref, bf16[3,1024,512]{2,1,0:T(8,128)(2,1)} %w_ref.6), custom_call_target="tpu_custom_call" | custom-call | flops 1610612736 | bytes 8388608 | tf_op jit(solution)/shard_map/first_rows/pallas_call | solution.py:606
  215.4 1.3 collective-permute-start.21
  216.7 1.5 add_convert_fusion.11
  218.4 6.0 %collective-permute-done.16 = bf16[1,256,1024]{2,1,0:T(8,128)(2,1)S(1)} collective-permute-done((bf16[1,256,1024]{2,1,0:T(8,128)(2,1)S(1)}, bf16[1,256,1024]{2,1,0:T(8,128)(2,1)S(1)}, u32[]{:S(2)}, u32[]{:S(2)}) %collective-permute-start.16) | collective-permute-done | bytes 524320 | tf_op jit(solution)/shard_map/ppermute | solution.py:424
  224.7 1.5 add_convert_fusion.8
  228.2 8.6 %collective-permute-done.13 = bf16[1,1024,256]{2,1,0:T(8,128)(2,1)S(1)} collective-permute-done((bf16[1,1024,256]{2,1,0:T(8,128)(2,1)S(1)}, bf16[1,1024,256]{2,1,0:T(8,128)(2,1)S(1)}, u32[]{:S(2)}, u32[]{:S(2)}) %collective-permute-start.13) | collective-permute-done | bytes 524320 | tf_op jit(solution)/shard_map/ppermute | solution.py:424
  237.0 15.8 %collective-permute-done.20 = bf16[1,256,1024]{2,1,0:T(8,128)(2,1)S(1)} collective-permute-done((bf16[1,256,1024]{2,1,0:T(8,128)(2,1)S(1)}, bf16[1,256,1024]{2,1,0:T(8,128)(2,1)S(1)}, u32[]{:S(2)}, u32[]{:S(2)}) %collective-permute-start.20) | collective-permute-done | bytes 524320 | tf_op jit(solution)/shard_map/ppermute | solution.py:424
  253.0 1.3 collective-permute-start.30
  255.9 5.6 %first_rows.3.a_ref = bf16[512,1024]{1,0:T(8,128)(2,1)} custom-call(bf16[3,1024,512]{2,1,0:T(8,128)(2,1)} %get-tuple-element.332.refs_2_.g_ref, bf16[3,1024,512]{2,1,0:T(8,128)(2,1)} %w_ref.6), custom_call_target="tpu_custom_call" | custom-call | flops 1610612736 | bytes 8388608 | tf_op jit(solution)/shard_map/first_rows/pallas_call | solution.py:606
  261.5 4.7 %back_rows.3 = (bf16[512,1024]{1,0:T(8,128)(2,1)}, f32[8,1024]{1,0:T(8,128)}) custom-call(bf16[512,1024]{1,0:T(8,128)(2,1)} %first_rows.3.a_ref, bf16[512,1024]{1,0:T(8,128)(2,1)} %collective-permute-done.21.b_ref, bf16[512,1024]{1,0:T(8,128)(2,1)} %source_ref, bf16[512,1024]{1,0:T(8,128)(2,1)} %get-tuple-element.337.refs_3_.add_ref, f32[1,1024]{1,0:T(1,128)} %bitcast.37), custom_call_target="tpu_custom_call" | custom-call | flops 15728640 | bytes 5242880 | tf_op jit(solution)/shard_map/back_rows/pallas_call | solution.py:647
  267.1 1.5 collective-permute-start.22
  269.0 2.9 collective-permute-done.24
  272.0 2.1 collective-permute-start.25
  275.5 1.9 collective-permute-done.30.refs_1_
  277.4 1.3 collective-permute-start.31
  278.7 6.9 %collective-permute-done.22 = bf16[1,1024,256]{2,1,0:T(8,128)(2,1)} collective-permute-done((bf16[1,1024,256]{2,1,0:T(8,128)(2,1)S(1)}, bf16[1,1024,256]{2,1,0:T(8,128)(2,1)}, u32[]{:S(2)}, u32[]{:S(2)}) %collective-permute-start.22) | collective-permute-done | bytes 524320 | tf_op jit(solution)/shard_map/ppermute | solution.py:424
  287.1 5.6 %reduced.1 = bf16[512,1024]{1,0:T(8,128)(2,1)} custom-call(bf16[512,2048]{1,0:T(8,128)(2,1)} %get-tuple-element.354.refs_1_.a_ref, bf16[2048,1024]{1,0:T(8,128)(2,1)} %w_ref.7), custom_call_target="tpu_custom_call" | custom-call | flops 34359738368 | bytes 117440512 | tf_op jit(solution)/shard_map/reduced/pallas_call | solution.py:551
  293.9 4.4 %reduce_near.1.refs_0_ = f32[2048,1024]{1,0:T(8,128)} custom-call(s32[2]{0:T(128)} %pad_add_fusion.1.s_ref, bf16[2,256,1024]{2,1,0:T(8,128)(2,1)} %copy-done.1, bf16[2,256,1024]{2,1,0:T(8,128)(2,1)} %collective-permute-done.29.refs_1_), custom_call_target="tpu_custom_call" | custom-call | bytes 6291456 | tf_op jit(solution)/shard_map/reduce_near/pallas_call | solution.py:710
  300.9 4.4 %reduce_far.1 = f32[2048,1024]{1,0:T(8,128)} custom-call(s32[2]{0:T(128)} %pad_add_fusion.1.s_ref, f32[2048,1024]{1,0:T(8,128)} %reduce_near.1.refs_0_, bf16[2,256,1024]{2,1,0:T(8,128)(2,1)} %collective-permute-done.30.refs_1_, bf16[2,256,1024]{2,1,0:T(8,128)(2,1)} %collective-permute-done.31.refs_2_), custom_call_target="tpu_custom_call", output_to_operand_aliasing={{}: (1, {})} | custom-call | bytes 6291456 | tf_op jit(solution)/shard_map/reduce_far/pallas_call | solution.py:710
  306.9 2.5 collective-permute-done.35
  309.4 3.7 %collective-permute-start.37 = (bf16[2,1024,256]{2,1,0:T(8,128)(2,1)S(1)}, bf16[2,1024,256]{2,1,0:T(8,128)(2,1)}, u32[]{:S(2)}, u32[]{:S(2)}) collective-permute-start(bf16[2,1024,256]{2,1,0:T(8,128)(2,1)S(1)} %constant_dynamic-update-slice_fusion.2.refs_0_), channel_id=1, source_target_pairs={{0,2},{2,0},{4,6},{6,4},{8,10},{10,8},{12,14},{14,12},{16,18},{18,... | collective-permute-start | bytes 3145736 | tf_op jit(solution)/shard_map/ppermute | solution.py:424
  313.8 3.9 %collective-permute-done.33 = bf16[1,2,128,512]{3,2,1,0:T(8,128)(2,1)S(1)} collective-permute-done((bf16[1,2,128,512]{3,2,1,0:T(8,128)(2,1)S(1)}, bf16[1,2,128,512]{3,2,1,0:T(8,128)(2,1)S(1)}, u32[]{:S(2)}, u32[]{:S(2)}) %collective-permute-start.33) | collective-permute-done | bytes 262176 | tf_op jit(solution)/shard_map/ppermute | solution.py:424
  317.6 1.4 collective-permute-start.39
  319.9 6.9 %output.1 = bf16[512,1024]{1,0:T(8,128)(2,1)} custom-call(bf16[512,1024]{1,0:T(8,128)(2,1)} %get-tuple-element.374.source_ref.m_ref, bf16[512,2048]{1,0:T(8,128)(2,1)} %get-tuple-element.375.refs_0_.a_ref, bf16[2048,1024]{1,0:T(8,128)(2,1)} %w_ref.7, bf16[512,1024]{1,0:T(8,128)(2,1)} %collective-permute-done.26.r_ref, f32[1,1024]{1,0:T(1,128)} %bitcast.41), custom_call_target="tpu_custom_call" | custom-call | flops 34359738368 | bytes 167772160 | tf_op jit(solution)/shard_map/output/pallas_call | solution.py:573
  327.2 4.5 %expand_near.1.refs_0_ = f32[1024,2048]{1,0:T(8,128)} custom-call(s32[2]{0:T(128)} %pad_add_fusion.1.s_ref, bf16[2,1024,256]{2,1,0:T(8,128)(2,1)} %copy-done.2, bf16[2,1024,256]{2,1,0:T(8,128)(2,1)} %collective-permute-done.37.refs_1_), custom_call_target="tpu_custom_call" | custom-call | bytes 6291456 | tf_op jit(solution)/shard_map/expand_near/pallas_call | solution.py:710
  332.9 4.5 %expand_far.1 = f32[1024,2048]{1,0:T(8,128)} custom-call(s32[2]{0:T(128)} %pad_add_fusion.1.s_ref, f32[1024,2048]{1,0:T(8,128)} %expand_near.1.refs_0_, bf16[2,1024,256]{2,1,0:T(8,128)(2,1)} %collective-permute-done.38.refs_1_, bf16[2,1024,256]{2,1,0:T(8,128)(2,1)} %copy-done.13), custom_call_target="tpu_custom_call", output_to_operand_aliasing={{}: (1, {})} | custom-call | bytes 6291456 | tf_op jit(solution)/shard_map/expand_far/pallas_call | solution.py:710
  337.5 1.5 collective-permute-start.44
  339.0 1.9 collective-permute-start.40
  342.5 4.6 %heads_near.1 = (f32[3,1024,512]{2,1,0:T(8,128)}, f32[512,1024]{1,0:T(8,128)}) custom-call(s32[2]{0:T(128)} %pad_add_fusion.1.s_ref, bf16[2,2,128,512]{3,2,1,0:T(8,128)(2,1)} %copy-done.7, bf16[2,2,128,512]{3,2,1,0:T(8,128)(2,1)} %copy-done.15, bf16[2,2,128,512]{3,2,1,0:T(8,128)(2,1)} %copy-done.6, bf16[2,2,128,512]{3,2,1,0:T(8,128)(2,1)} %copy-done.14), custom_call_target="tpu_custom_call" | custom-call | bytes 6291456 | tf_op jit(solution)/shard_map/heads_near/pallas_call | solution.py:710
  347.8 4.5 %heads_far.1 = (f32[3,1024,512]{2,1,0:T(8,128)}, f32[512,1024]{1,0:T(8,128)}) custom-call(s32[2]{0:T(128)} %pad_add_fusion.1.s_ref, f32[3,1024,512]{2,1,0:T(8,128)} %get-tuple-element.395.refs_0_, f32[512,1024]{1,0:T(8,128)} %get-tuple-element.396.refs_1_, ...), custom_call_target="tpu_custom_call", output_to_operand_aliasing={{0}: (1, {}), {1}: (2, {})} | custom-call | bytes 6291456 | tf_op jit(solution)/shard_map/heads_far/pallas_call | solution.py:710
  (174 shorter events, 33.5 us)
Async XLA Ops:
  0.6 24.4 %collective-permute-start = (bf16[512,1024]{1,0:T(8,128)(2,1)}, bf16[512,1024]{1,0:T(8,128)(2,1)}, u32[]{:S(2)}, u32[]{:S(2)}) collective-permute-start(bf16[512,1024]{1,0:T(8,128)(2,1)} %source_ref), channel_id=1, source_target_pairs={{0,1},{1,0},{2,3},{3,2},{4,5},{5,4},{6,7},{7,6},{8,9},{9,8},{10,11... | collective-permute-start | bytes 3145736 | tf_op jit(solution)/shard_map/ppermute | solution.py:795
  10.5 8.3 %copy-start.20 = (bf16[512,1024]{1,0:T(8,128)(2,1)S(1)}, bf16[512,1024]{1,0:T(8,128)(2,1)}, u32[]{:S(2)}) copy-start(bf16[512,1024]{1,0:T(8,128)(2,1)} %w0_ref) | copy-start | bytes 3145732
  10.5 15.8 %copy-start.11 = (bf16[512,1024]{1,0:T(8,128)(2,1)S(1)}, bf16[512,1024]{1,0:T(8,128)(2,1)}, u32[]{:S(2)}) copy-start(bf16[512,1024]{1,0:T(8,128)(2,1)} %param.29) | copy-start | bytes 3145732
  25.1 21.4 %collective-permute-start.2 = (bf16[256,1024]{1,0:T(8,128)(2,1)S(1)}, bf16[256,1024]{1,0:T(8,128)(2,1)S(1)}, u32[]{:S(2)}, u32[]{:S(2)}) collective-permute-start(bf16[256,1024]{1,0:T(8,128)(2,1)S(1)} %constant_dynamic-slice_fusion), channel_id=1, source_target_pairs={{0,1},{1,0},{2,3},{3,2},{4,5},{5,4},{6,7},{7,6},{8,9},{9,8},{10,11... | collective-permute-start | bytes 1572872 | tf_op jit(solution)/shard_map/ppermute | solution.py:795
  26.3 33.1 %collective-permute-start.4 = (bf16[512,1024]{1,0:T(8,128)(2,1)S(1)}, bf16[512,1024]{1,0:T(8,128)(2,1)S(1)}, u32[]{:S(2)}, u32[]{:S(2)}) collective-permute-start(bf16[512,1024]{1,0:T(8,128)(2,1)S(1)} %copy-done.11), channel_id=1, source_target_pairs={{0,1},{1,0},{2,3},{3,2},{4,5},{5,4},{6,7},{7,6},{8,9},{9,8},{10,11... | collective-permute-start | bytes 3145736 | tf_op jit(solution)/shard_map/ppermute | solution.py:795
  32.1 16.6 %copy-start.26 = (bf16[2048]{0:T(1024)(128)(2,1)S(1)}, bf16[2048]{0:T(1024)(128)(2,1)}, u32[]{:S(2)}) copy-start(bf16[2048]{0:T(1024)(128)(2,1)} %param.26) | copy-start | bytes 12292
  46.4 4.1 %copy-start.17 = (bf16[256,1024]{1,0:T(8,128)(2,1)}, bf16[256,1024]{1,0:T(8,128)(2,1)S(1)}, u32[]{:S(2)}) copy-start(bf16[256,1024]{1,0:T(8,128)(2,1)S(1)} %collective-permute-done.2.a_ref) | copy-start | bytes 1572868
  46.4 4.0 %collective-permute-start.3 = (bf16[256,1024]{1,0:T(8,128)(2,1)S(1)}, bf16[256,1024]{1,0:T(8,128)(2,1)S(1)}, u32[]{:S(2)}, u32[]{:S(2)}) collective-permute-start(bf16[256,1024]{1,0:T(8,128)(2,1)S(1)} %collective-permute-done.2.a_ref), channel_id=1, source_target_pairs={{0,2},{2,0},{4,6},{6,4},{8,10},{10,8},{12,14},{14,12},{16,18},{18,... | collective-permute-start | bytes 1572872 | tf_op jit(solution)/shard_map/ppermute | solution.py:424
  49.2 32.7 %collective-permute-start.1 = (bf16[1024,512]{1,0:T(8,128)(2,1)}, bf16[1024,512]{1,0:T(8,128)(2,1)}, u32[]{:S(2)}, u32[]{:S(2)}) collective-permute-start(bf16[1024,512]{1,0:T(8,128)(2,1)} %get-tuple-element.311.m_ref.o_ref.refs_5_), channel_id=1, source_target_pairs={{0,1},{1,0},{2,3},{3,2},{4,5},{5,4},{6,7},{7,6},{8,9},{9,8},{10,11... | collective-permute-start | bytes 3145736 | tf_op jit(solution)/shard_map/ppermute | solution.py:795
  101.5 26.1 %collective-permute-start.5 = (bf16[512,1024]{1,0:T(8,128)(2,1)}, bf16[512,1024]{1,0:T(8,128)(2,1)S(1)}, u32[]{:S(2)}, u32[]{:S(2)}) collective-permute-start(bf16[512,1024]{1,0:T(8,128)(2,1)} %get-tuple-element.250), channel_id=1, source_target_pairs={{0,1},{1,0},{2,3},{3,2},{4,5},{5,4},{6,7},{7,6},{8,9},{9,8},{10,11... | collective-permute-start | bytes 3145736 | tf_op jit(solution)/shard_map/ppermute | solution.py:795
  124.9 24.3 %collective-permute-start.7 = (bf16[4,256,1024]{2,1,0:T(8,128)(2,1)}, bf16[4,256,1024]{2,1,0:T(8,128)(2,1)}, u32[]{:S(2)}, u32[]{:S(2)}) collective-permute-start(bf16[4,256,1024]{2,1,0:T(8,128)(2,1)} %get-tuple-element.264), channel_id=1, source_target_pairs={{0,2},{2,0},{4,6},{6,4},{8,10},{10,8},{12,14},{14,12},{16,18},{18,... | collective-permute-start | bytes 6291464 | tf_op jit(solution)/shard_map/ppermute | solution.py:424
  128.6 4.7 %copy-start.12 = (bf16[512,1024]{1,0:T(8,128)(2,1)S(1)}, bf16[512,1024]{1,0:T(8,128)(2,1)}, u32[]{:S(2)}) copy-start(bf16[512,1024]{1,0:T(8,128)(2,1)} %order_rows.1.w1_ref) | copy-start | bytes 3145732
  136.1 10.9 %copy-start = (bf16[512,1024]{1,0:T(8,128)(2,1)S(1)}, bf16[512,1024]{1,0:T(8,128)(2,1)}, u32[]{:S(2)}) copy-start(bf16[512,1024]{1,0:T(8,128)(2,1)} %get-tuple-element.337.refs_3_.add_ref) | copy-start | bytes 3145732
  136.1 11.5 %copy-start.21 = (bf16[512,1024]{1,0:T(8,128)(2,1)S(1)}, bf16[512,1024]{1,0:T(8,128)(2,1)}, u32[]{:S(2)}) copy-start(bf16[512,1024]{1,0:T(8,128)(2,1)} %w0_ref) | copy-start | bytes 3145732
  146.1 3.1 copy-start.3
  146.1 8.0 %collective-permute-start.6 = (bf16[4,1024,256]{2,1,0:T(8,128)(2,1)}, bf16[4,1024,256]{2,1,0:T(8,128)(2,1)S(1)}, u32[]{:S(2)}, u32[]{:S(2)}) collective-permute-start(bf16[4,1024,256]{2,1,0:T(8,128)(2,1)} %get-tuple-element.279), channel_id=1, source_target_pairs={{0,2},{2,0},{4,6},{6,4},{8,10},{10,8},{12,14},{14,12},{16,18},{18,... | collective-permute-start | bytes 6291464 | tf_op jit(solution)/shard_map/ppermute | solution.py:424
  146.1 13.4 %collective-permute-start.9 = (bf16[512,512]{1,0:T(8,128)(2,1)}, bf16[512,512]{1,0:T(8,128)(2,1)}, u32[]{:S(2)}, u32[]{:S(2)}) collective-permute-start(bf16[512,512]{1,0:T(8,128)(2,1)} %convolution_convert_fusion.1), channel_id=1, source_target_pairs={{0,1},{1,0},{2,3},{3,2},{4,5},{5,4},{6,7},{7,6},{8,9},{9,8},{10,11... | collective-permute-start | bytes 1572872 | tf_op jit(solution)/shard_map/ppermute | solution.py:795
  147.1 52.5 %collective-permute-start.10 = (bf16[512,1024]{1,0:T(8,128)(2,1)S(1)}, bf16[512,1024]{1,0:T(8,128)(2,1)}, u32[]{:S(2)}, u32[]{:S(2)}) collective-permute-start(bf16[512,1024]{1,0:T(8,128)(2,1)S(1)} %copy-done), channel_id=1, source_target_pairs={{0,1},{1,0},{2,3},{3,2},{4,5},{5,4},{6,7},{7,6},{8,9},{9,8},{10,11... | collective-permute-start | bytes 3145736 | tf_op jit(solution)/shard_map/ppermute | solution.py:795
  149.2 4.9 %copy-start.4 = (bf16[4,1024,256]{2,1,0:T(8,128)(2,1)S(1)}, bf16[4,1024,256]{2,1,0:T(8,128)(2,1)}, u32[]{:S(2)}) copy-start(bf16[4,1024,256]{2,1,0:T(8,128)(2,1)} %get-tuple-element.284) | copy-start | bytes 6291460
  152.8 29.5 %collective-permute-start.11 = (bf16[2,256,1024]{2,1,0:T(8,128)(2,1)}, bf16[2,256,1024]{2,1,0:T(8,128)(2,1)}, u32[]{:S(2)}, u32[]{:S(2)}) collective-permute-start(bf16[2,256,1024]{2,1,0:T(8,128)(2,1)} %get-tuple-element.410), channel_id=1, source_target_pairs={{0,4},{2,6},{4,0},{6,2},{8,12},{10,14},{12,8},{14,10},{16,20},{18,... | collective-permute-start | bytes 3145736 | tf_op jit(solution)/shard_map/ppermute | solution.py:424
  185.0 12.3 %collective-permute-start.12 = (bf16[1,256,1024]{2,1,0:T(8,128)(2,1)}, bf16[1,256,1024]{2,1,0:T(8,128)(2,1)S(1)}, u32[]{:S(2)}, u32[]{:S(2)}) collective-permute-start(bf16[1,256,1024]{2,1,0:T(8,128)(2,1)} %get-tuple-element.417), channel_id=1, source_target_pairs={{0,8},{2,10},{4,12},{6,14},{8,0},{10,2},{12,4},{14,6},{16,24},{18,... | collective-permute-start | bytes 1572872 | tf_op jit(solution)/shard_map/ppermute | solution.py:424
  185.3 31.4 %collective-permute-start.8 = (bf16[2,1024,256]{2,1,0:T(8,128)(2,1)}, bf16[2,1024,256]{2,1,0:T(8,128)(2,1)}, u32[]{:S(2)}, u32[]{:S(2)}) collective-permute-start(bf16[2,1024,256]{2,1,0:T(8,128)(2,1)} %get-tuple-element.407), channel_id=1, source_target_pairs={{0,4},{2,6},{4,0},{6,2},{8,12},{10,14},{12,8},{14,10},{16,20},{18,... | collective-permute-start | bytes 3145736 | tf_op jit(solution)/shard_map/ppermute | solution.py:424
  186.6 11.5 %copy-start.5 = (bf16[1,256,1024]{2,1,0:T(8,128)(2,1)S(1)}, bf16[1,256,1024]{2,1,0:T(8,128)(2,1)}, u32[]{:S(2)}) copy-start(bf16[1,256,1024]{2,1,0:T(8,128)(2,1)} %get-tuple-element.304) | copy-start | bytes 1572868
  194.3 30.4 %collective-permute-start.15 = (bf16[4,2,128,512]{3,2,1,0:T(8,128)(2,1)}, bf16[4,2,128,512]{3,2,1,0:T(8,128)(2,1)}, u32[]{:S(2)}, u32[]{:S(2)}) collective-permute-start(bf16[4,2,128,512]{3,2,1,0:T(8,128)(2,1)} %get-tuple-element.302), channel_id=1, source_target_pairs={{0,2},{2,0},{4,6},{6,4},{8,10},{10,8},{12,14},{14,12},{16,18},{18,... | collective-permute-start | bytes 3145736 | tf_op jit(solution)/shard_map/ppermute | solution.py:424
  199.4 25.0 %collective-permute-start.16 = (bf16[1,256,1024]{2,1,0:T(8,128)(2,1)S(1)}, bf16[1,256,1024]{2,1,0:T(8,128)(2,1)S(1)}, u32[]{:S(2)}, u32[]{:S(2)}) collective-permute-start(bf16[1,256,1024]{2,1,0:T(8,128)(2,1)S(1)} %add_convert_fusion.13), channel_id=1, source_target_pairs={{0,16},{2,18},{4,20},{6,22},{8,24},{10,26},{12,28},{14,30},{16,0},... | collective-permute-start | bytes 1572872 | tf_op jit(solution)/shard_map/ppermute | solution.py:424
  207.1 20.0 %collective-permute-start.14 = (bf16[4,2,128,512]{3,2,1,0:T(8,128)(2,1)}, bf16[4,2,128,512]{3,2,1,0:T(8,128)(2,1)S(1)}, u32[]{:S(2)}, u32[]{:S(2)}) collective-permute-start(bf16[4,2,128,512]{3,2,1,0:T(8,128)(2,1)} %get-tuple-element.312), channel_id=1, source_target_pairs={{0,2},{2,0},{4,6},{6,4},{8,10},{10,8},{12,14},{14,12},{16,18},{18,... | collective-permute-start | bytes 3145736 | tf_op jit(solution)/shard_map/ppermute | solution.py:424
  215.4 9.3 %copy-start.9 = (bf16[4,2,128,512]{3,2,1,0:T(8,128)(2,1)S(1)}, bf16[4,2,128,512]{3,2,1,0:T(8,128)(2,1)}, u32[]{:S(2)}) copy-start(bf16[4,2,128,512]{3,2,1,0:T(8,128)(2,1)} %get-tuple-element.320) | copy-start | bytes 3145732
  215.4 46.1 %collective-permute-start.21 = (bf16[512,1024]{1,0:T(8,128)(2,1)}, bf16[512,1024]{1,0:T(8,128)(2,1)}, u32[]{:S(2)}, u32[]{:S(2)}) collective-permute-start(bf16[512,1024]{1,0:T(8,128)(2,1)} %first_rows.2), channel_id=1, source_target_pairs={{0,1},{1,0},{2,3},{3,2},{4,5},{5,4},{6,7},{7,6},{8,9},{9,8},{10,11... | collective-permute-start | bytes 3145736 | tf_op jit(solution)/shard_map/ppermute | solution.py:795
  218.2 18.6 %collective-permute-start.13 = (bf16[1,1024,256]{2,1,0:T(8,128)(2,1)S(1)}, bf16[1,1024,256]{2,1,0:T(8,128)(2,1)S(1)}, u32[]{:S(2)}, u32[]{:S(2)}) collective-permute-start(bf16[1,1024,256]{2,1,0:T(8,128)(2,1)S(1)} %get-tuple-element.415), channel_id=1, source_target_pairs={{0,8},{2,10},{4,12},{6,14},{8,0},{10,2},{12,4},{14,6},{16,24},{18,... | collective-permute-start | bytes 1572872 | tf_op jit(solution)/shard_map/ppermute | solution.py:424
  224.6 28.3 %collective-permute-start.20 = (bf16[1,256,1024]{2,1,0:T(8,128)(2,1)S(1)}, bf16[1,256,1024]{2,1,0:T(8,128)(2,1)S(1)}, u32[]{:S(2)}, u32[]{:S(2)}) collective-permute-start(bf16[1,256,1024]{2,1,0:T(8,128)(2,1)S(1)} %add_convert_fusion.10), channel_id=1, source_target_pairs={{0,8},{2,10},{4,12},{6,14},{8,0},{10,2},{12,4},{14,6},{16,24},{18,... | collective-permute-start | bytes 1572872 | tf_op jit(solution)/shard_map/ppermute | solution.py:424
  226.3 28.0 %collective-permute-start.19 = (bf16[2,2,128,512]{3,2,1,0:T(8,128)(2,1)S(1)}, bf16[2,2,128,512]{3,2,1,0:T(8,128)(2,1)S(1)}, u32[]{:S(2)}, u32[]{:S(2)}) collective-permute-start(bf16[2,2,128,512]{3,2,1,0:T(8,128)(2,1)S(1)} %get-tuple-element.414), channel_id=1, source_target_pairs={{0,4},{2,6},{4,0},{6,2},{8,12},{10,14},{12,8},{14,10},{16,20},{18,... | collective-permute-start | bytes 1572872 | tf_op jit(solution)/shard_map/ppermute | solution.py:424
  227.4 27.7 %collective-permute-start.18 = (bf16[2,2,128,512]{3,2,1,0:T(8,128)(2,1)S(1)}, bf16[2,2,128,512]{3,2,1,0:T(8,128)(2,1)S(1)}, u32[]{:S(2)}, u32[]{:S(2)}) collective-permute-start(bf16[2,2,128,512]{3,2,1,0:T(8,128)(2,1)S(1)} %get-tuple-element.412), channel_id=1, source_target_pairs={{0,4},{2,6},{4,0},{6,2},{8,12},{10,14},{12,8},{14,10},{16,20},{18,... | collective-permute-start | bytes 1572872 | tf_op jit(solution)/shard_map/ppermute | solution.py:424
  237.0 30.0 %collective-permute-start.17 = (bf16[1,1024,256]{2,1,0:T(8,128)(2,1)S(1)}, bf16[1,1024,256]{2,1,0:T(8,128)(2,1)S(1)}, u32[]{:S(2)}, u32[]{:S(2)}) collective-permute-start(bf16[1,1024,256]{2,1,0:T(8,128)(2,1)S(1)} %add_convert_fusion.5), channel_id=1, source_target_pairs={{0,16},{2,18},{4,20},{6,22},{8,24},{10,26},{12,28},{14,30},{16,0},... | collective-permute-start | bytes 1572872 | tf_op jit(solution)/shard_map/ppermute | solution.py:424
  252.9 22.1 %copy-start.1 = (bf16[2,256,1024]{2,1,0:T(8,128)(2,1)}, bf16[2,256,1024]{2,1,0:T(8,128)(2,1)S(1)}, u32[]{:S(2)}) copy-start(bf16[2,256,1024]{2,1,0:T(8,128)(2,1)S(1)} %constant_dynamic-update-slice_fusion.refs_0_) | copy-start | bytes 3145732
  253.0 24.4 %collective-permute-start.30 = (bf16[2,256,1024]{2,1,0:T(8,128)(2,1)S(1)}, bf16[2,256,1024]{2,1,0:T(8,128)(2,1)}, u32[]{:S(2)}, u32[]{:S(2)}) collective-permute-start(bf16[2,256,1024]{2,1,0:T(8,128)(2,1)S(1)} %constant_dynamic-update-slice_fusion.refs_0_), channel_id=1, source_target_pairs={{0,4},{2,6},{4,0},{6,2},{8,12},{10,14},{12,8},{14,10},{16,20},{18,... | collective-permute-start | bytes 3145736 | tf_op jit(solution)/shard_map/ppermute | solution.py:424
  255.9 19.4 %collective-permute-start.23 = (bf16[1,2,128,512]{3,2,1,0:T(8,128)(2,1)}, bf16[1,2,128,512]{3,2,1,0:T(8,128)(2,1)S(1)}, u32[]{:S(2)}, u32[]{:S(2)}) collective-permute-start(bf16[1,2,128,512]{3,2,1,0:T(8,128)(2,1)} %get-tuple-element.420), channel_id=1, source_target_pairs={{0,8},{2,10},{4,12},{6,14},{8,0},{10,2},{12,4},{14,6},{16,24},{18,... | collective-permute-start | bytes 786440 | tf_op jit(solution)/shard_map/ppermute | solution.py:424
  261.5 10.4 %copy-start.23 = (f32[1,2048]{1,0:T(1,128)S(1)}, f32[1,2048]{1,0:T(1,128)}, u32[]{:S(2)}) copy-start(f32[1,2048]{1,0:T(1,128)} %get-tuple-element.346) | copy-start | bytes 24580
  261.5 10.4 %copy-start.24 = (f32[1,2048]{1,0:T(1,128)S(1)}, f32[1,2048]{1,0:T(1,128)}, u32[]{:S(2)}) copy-start(f32[1,2048]{1,0:T(1,128)} %get-tuple-element.345) | copy-start | bytes 24580
  267.1 18.5 %collective-permute-start.22 = (bf16[1,1024,256]{2,1,0:T(8,128)(2,1)S(1)}, bf16[1,1024,256]{2,1,0:T(8,128)(2,1)}, u32[]{:S(2)}, u32[]{:S(2)}) collective-permute-start(bf16[1,1024,256]{2,1,0:T(8,128)(2,1)S(1)} %add_convert_fusion.4), channel_id=1, source_target_pairs={{0,8},{2,10},{4,12},{6,14},{8,0},{10,2},{12,4},{14,6},{16,24},{18,... | collective-permute-start | bytes 1572872 | tf_op jit(solution)/shard_map/ppermute | solution.py:424
  268.7 3.2 collective-permute-start.24
  272.0 3.0 collective-permute-start.25
  274.1 18.5 %collective-permute-start.27 = (bf16[1,2,128,512]{3,2,1,0:T(8,128)(2,1)}, bf16[1,2,128,512]{3,2,1,0:T(8,128)(2,1)S(1)}, u32[]{:S(2)}, u32[]{:S(2)}) collective-permute-start(bf16[1,2,128,512]{3,2,1,0:T(8,128)(2,1)} %get-tuple-element.422), channel_id=1, source_target_pairs={{0,8},{2,10},{4,12},{6,14},{8,0},{10,2},{12,4},{14,6},{16,24},{18,... | collective-permute-start | bytes 786440 | tf_op jit(solution)/shard_map/ppermute | solution.py:424
  275.0 18.8 %collective-permute-start.29 = (bf16[2,256,1024]{2,1,0:T(8,128)(2,1)S(1)}, bf16[2,256,1024]{2,1,0:T(8,128)(2,1)}, u32[]{:S(2)}, u32[]{:S(2)}) collective-permute-start(bf16[2,256,1024]{2,1,0:T(8,128)(2,1)S(1)} %constant_dynamic-update-slice_fusion.refs_0_), channel_id=1, source_target_pairs={{0,2},{2,0},{4,6},{6,4},{8,10},{10,8},{12,14},{14,12},{16,18},{18,... | collective-permute-start | bytes 3145736 | tf_op jit(solution)/shard_map/ppermute | solution.py:424
  275.4 22.9 %collective-permute-start.32 = (bf16[1,2,128,512]{3,2,1,0:T(8,128)(2,1)S(1)}, bf16[1,2,128,512]{3,2,1,0:T(8,128)(2,1)}, u32[]{:S(2)}, u32[]{:S(2)}) collective-permute-start(bf16[1,2,128,512]{3,2,1,0:T(8,128)(2,1)S(1)} %add_convert_fusion.19), channel_id=1, source_target_pairs={{0,16},{2,18},{4,20},{6,22},{8,24},{10,26},{12,28},{14,30},{16,0},... | collective-permute-start | bytes 786440 | tf_op jit(solution)/shard_map/ppermute | solution.py:424
  277.4 22.4 %collective-permute-start.31 = (bf16[2,256,1024]{2,1,0:T(8,128)(2,1)}, bf16[2,256,1024]{2,1,0:T(8,128)(2,1)}, u32[]{:S(2)}, u32[]{:S(2)}) collective-permute-start(bf16[2,256,1024]{2,1,0:T(8,128)(2,1)} %collective-permute-done.30.refs_1_), channel_id=1, source_target_pairs={{0,2},{2,0},{4,6},{6,4},{8,10},{10,8},{12,14},{14,12},{16,18},{18,... | collective-permute-start | bytes 3145736 | tf_op jit(solution)/shard_map/ppermute | solution.py:424
  286.7 22.7 %copy-start.2 = (bf16[2,1024,256]{2,1,0:T(8,128)(2,1)}, bf16[2,1024,256]{2,1,0:T(8,128)(2,1)S(1)}, u32[]{:S(2)}) copy-start(bf16[2,1024,256]{2,1,0:T(8,128)(2,1)S(1)} %constant_dynamic-update-slice_fusion.2.refs_0_) | copy-start | bytes 3145732
  286.7 26.5 %collective-permute-start.38 = (bf16[2,1024,256]{2,1,0:T(8,128)(2,1)S(1)}, bf16[2,1024,256]{2,1,0:T(8,128)(2,1)}, u32[]{:S(2)}, u32[]{:S(2)}) collective-permute-start(bf16[2,1024,256]{2,1,0:T(8,128)(2,1)S(1)} %constant_dynamic-update-slice_fusion.2.refs_0_), channel_id=1, source_target_pairs={{0,4},{2,6},{4,0},{6,2},{8,12},{10,14},{12,8},{14,10},{16,20},{18,... | collective-permute-start | bytes 3145736 | tf_op jit(solution)/shard_map/ppermute | solution.py:424
  292.6 26.4 %collective-permute-start.26 = (bf16[512,1024]{1,0:T(8,128)(2,1)}, bf16[512,1024]{1,0:T(8,128)(2,1)}, u32[]{:S(2)}, u32[]{:S(2)}) collective-permute-start(bf16[512,1024]{1,0:T(8,128)(2,1)} %reduced.1), channel_id=1, source_target_pairs={{0,1},{1,0},{2,3},{3,2},{4,5},{5,4},{6,7},{7,6},{8,9},{9,8},{10,11... | collective-permute-start | bytes 3145736 | tf_op jit(solution)/shard_map/ppermute | solution.py:795
  293.8 12.6 %collective-permute-start.28 = (bf16[1,2,128,512]{3,2,1,0:T(8,128)(2,1)S(1)}, bf16[1,2,128,512]{3,2,1,0:T(8,128)(2,1)S(1)}, u32[]{:S(2)}, u32[]{:S(2)}) collective-permute-start(bf16[1,2,128,512]{3,2,1,0:T(8,128)(2,1)S(1)} %add_convert_fusion.18), channel_id=1, source_target_pairs={{0,16},{2,18},{4,20},{6,22},{8,24},{10,26},{12,28},{14,30},{16,0},... | collective-permute-start | bytes 786440 | tf_op jit(solution)/shard_map/ppermute | solution.py:424
  298.3 11.1 %collective-permute-start.35 = (f32[58,128]{1,0:T(8,128)S(1)}, f32[58,128]{1,0:T(8,128)S(1)}, u32[]{:S(2)}, u32[]{:S(2)}) collective-permute-start(f32[58,128]{1,0:T(8,128)S(1)} %add.176), channel_id=1, source_target_pairs={{0,4},{2,6},{4,0},{6,2},{8,12},{10,14},{12,8},{14,10},{16,20},{18,... | collective-permute-start | bytes 89096 | tf_op jit(solution)/shard_map/ppermute | solution.py:424
  299.8 13.3 %collective-permute-start.34 = (bf16[1,2,128,512]{3,2,1,0:T(8,128)(2,1)S(1)}, bf16[1,2,128,512]{3,2,1,0:T(8,128)(2,1)S(1)}, u32[]{:S(2)}, u32[]{:S(2)}) collective-permute-start(bf16[1,2,128,512]{3,2,1,0:T(8,128)(2,1)S(1)} %add_convert_fusion.17), channel_id=1, source_target_pairs={{0,8},{2,10},{4,12},{6,14},{8,0},{10,2},{12,4},{14,6},{16,24},{18,... | collective-permute-start | bytes 786440 | tf_op jit(solution)/shard_map/ppermute | solution.py:424
  306.5 11.1 %collective-permute-start.33 = (bf16[1,2,128,512]{3,2,1,0:T(8,128)(2,1)S(1)}, bf16[1,2,128,512]{3,2,1,0:T(8,128)(2,1)S(1)}, u32[]{:S(2)}, u32[]{:S(2)}) collective-permute-start(bf16[1,2,128,512]{3,2,1,0:T(8,128)(2,1)S(1)} %add_convert_fusion.16), channel_id=1, source_target_pairs={{0,8},{2,10},{4,12},{6,14},{8,0},{10,2},{12,4},{14,6},{16,24},{18,... | collective-permute-start | bytes 786440 | tf_op jit(solution)/shard_map/ppermute | solution.py:424
  309.4 17.4 %collective-permute-start.37 = (bf16[2,1024,256]{2,1,0:T(8,128)(2,1)S(1)}, bf16[2,1024,256]{2,1,0:T(8,128)(2,1)}, u32[]{:S(2)}, u32[]{:S(2)}) collective-permute-start(bf16[2,1024,256]{2,1,0:T(8,128)(2,1)S(1)} %constant_dynamic-update-slice_fusion.2.refs_0_), channel_id=1, source_target_pairs={{0,2},{2,0},{4,6},{6,4},{8,10},{10,8},{12,14},{14,12},{16,18},{18,... | collective-permute-start | bytes 3145736 | tf_op jit(solution)/shard_map/ppermute | solution.py:424
  313.1 24.4 %collective-permute-start.36 = (f32[58,128]{1,0:T(8,128)S(1)}, f32[58,128]{1,0:T(8,128)S(1)}, u32[]{:S(2)}, u32[]{:S(2)}) collective-permute-start(f32[58,128]{1,0:T(8,128)S(1)} %add.181), channel_id=1, source_target_pairs={{0,8},{2,10},{4,12},{6,14},{8,0},{10,2},{12,4},{14,6},{16,24},{18,... | collective-permute-start | bytes 89096 | tf_op jit(solution)/shard_map/ppermute | solution.py:424
  313.2 13.6 %copy-start.6 = (bf16[2,2,128,512]{3,2,1,0:T(8,128)(2,1)}, bf16[2,2,128,512]{3,2,1,0:T(8,128)(2,1)S(1)}, u32[]{:S(2)}) copy-start(bf16[2,2,128,512]{3,2,1,0:T(8,128)(2,1)S(1)} %constant_dynamic-update-slice_fusion.4.refs_2_) | copy-start | bytes 1572868
  313.3 18.5 %collective-permute-start.45 = (bf16[2,2,128,512]{3,2,1,0:T(8,128)(2,1)S(1)}, bf16[2,2,128,512]{3,2,1,0:T(8,128)(2,1)}, u32[]{:S(2)}, u32[]{:S(2)}) collective-permute-start(bf16[2,2,128,512]{3,2,1,0:T(8,128)(2,1)S(1)} %constant_dynamic-update-slice_fusion.4.refs_2_), channel_id=1, source_target_pairs={{0,4},{2,6},{4,0},{6,2},{8,12},{10,14},{12,8},{14,10},{16,20},{18,... | collective-permute-start | bytes 1572872 | tf_op jit(solution)/shard_map/ppermute | solution.py:424
  317.6 14.3 %collective-permute-start.39 = (bf16[2,1024,256]{2,1,0:T(8,128)(2,1)}, bf16[2,1024,256]{2,1,0:T(8,128)(2,1)S(1)}, u32[]{:S(2)}, u32[]{:S(2)}) collective-permute-start(bf16[2,1024,256]{2,1,0:T(8,128)(2,1)} %collective-permute-done.38.refs_1_), channel_id=1, source_target_pairs={{0,2},{2,0},{4,6},{6,4},{8,10},{10,8},{12,14},{14,12},{16,18},{18,... | collective-permute-start | bytes 3145736 | tf_op jit(solution)/shard_map/ppermute | solution.py:424
  319.1 12.7 %copy-start.7 = (bf16[2,2,128,512]{3,2,1,0:T(8,128)(2,1)}, bf16[2,2,128,512]{3,2,1,0:T(8,128)(2,1)S(1)}, u32[]{:S(2)}) copy-start(bf16[2,2,128,512]{3,2,1,0:T(8,128)(2,1)S(1)} %constant_dynamic-update-slice_fusion.6.refs_0_) | copy-start | bytes 1572868
  319.1 18.5 %collective-permute-start.43 = (bf16[2,2,128,512]{3,2,1,0:T(8,128)(2,1)S(1)}, bf16[2,2,128,512]{3,2,1,0:T(8,128)(2,1)}, u32[]{:S(2)}, u32[]{:S(2)}) collective-permute-start(bf16[2,2,128,512]{3,2,1,0:T(8,128)(2,1)S(1)} %constant_dynamic-update-slice_fusion.6.refs_0_), channel_id=1, source_target_pairs={{0,4},{2,6},{4,0},{6,2},{8,12},{10,14},{12,8},{14,10},{16,20},{18,... | collective-permute-start | bytes 1572872 | tf_op jit(solution)/shard_map/ppermute | solution.py:424
  326.8 14.0 %collective-permute-start.42 = (bf16[2,2,128,512]{3,2,1,0:T(8,128)(2,1)S(1)}, bf16[2,2,128,512]{3,2,1,0:T(8,128)(2,1)S(1)}, u32[]{:S(2)}, u32[]{:S(2)}) collective-permute-start(bf16[2,2,128,512]{3,2,1,0:T(8,128)(2,1)S(1)} %constant_dynamic-update-slice_fusion.4.refs_2_), channel_id=1, source_target_pairs={{0,2},{2,0},{4,6},{6,4},{8,10},{10,8},{12,14},{14,12},{16,18},{18,... | collective-permute-start | bytes 1572872 | tf_op jit(solution)/shard_map/ppermute | solution.py:424
  331.7 9.1 %collective-permute-start.41 = (bf16[2,2,128,512]{3,2,1,0:T(8,128)(2,1)S(1)}, bf16[2,2,128,512]{3,2,1,0:T(8,128)(2,1)S(1)}, u32[]{:S(2)}, u32[]{:S(2)}) collective-permute-start(bf16[2,2,128,512]{3,2,1,0:T(8,128)(2,1)S(1)} %constant_dynamic-update-slice_fusion.6.refs_0_), channel_id=1, source_target_pairs={{0,2},{2,0},{4,6},{6,4},{8,10},{10,8},{12,14},{14,12},{16,18},{18,... | collective-permute-start | bytes 1572872 | tf_op jit(solution)/shard_map/ppermute | solution.py:424
  331.9 15.1 %collective-permute-start.46 = (bf16[2,2,128,512]{3,2,1,0:T(8,128)(2,1)}, bf16[2,2,128,512]{3,2,1,0:T(8,128)(2,1)}, u32[]{:S(2)}, u32[]{:S(2)}) collective-permute-start(bf16[2,2,128,512]{3,2,1,0:T(8,128)(2,1)} %collective-permute-done.45.refs_4_), channel_id=1, source_target_pairs={{0,2},{2,0},{4,6},{6,4},{8,10},{10,8},{12,14},{14,12},{16,18},{18,... | collective-permute-start | bytes 1572872 | tf_op jit(solution)/shard_map/ppermute | solution.py:424
  337.5 9.5 %collective-permute-start.44 = (bf16[2,2,128,512]{3,2,1,0:T(8,128)(2,1)}, bf16[2,2,128,512]{3,2,1,0:T(8,128)(2,1)S(1)}, u32[]{:S(2)}, u32[]{:S(2)}) collective-permute-start(bf16[2,2,128,512]{3,2,1,0:T(8,128)(2,1)} %collective-permute-done.43.refs_2_), channel_id=1, source_target_pairs={{0,2},{2,0},{4,6},{6,4},{8,10},{10,8},{12,14},{14,12},{16,18},{18,... | collective-permute-start | bytes 1572872 | tf_op jit(solution)/shard_map/ppermute | solution.py:424
  339.0 13.4 %collective-permute-start.40 = (f32[58,128]{1,0:T(8,128)S(1)}, f32[58,128]{1,0:T(8,128)S(1)}, u32[]{:S(2)}, u32[]{:S(2)}) collective-permute-start(f32[58,128]{1,0:T(8,128)S(1)} %add.182), channel_id=1, source_target_pairs={{0,16},{2,18},{4,20},{6,22},{8,24},{10,26},{12,28},{14,30},{16,0},... | collective-permute-start | bytes 89096 | tf_op jit(solution)/shard_map/ppermute | solution.py:424
  (12 other events, 20.4 us)
